TPU v7x, 32 devices: a whole 2x2x4 slice. The times are simulated.
32 devices in a mesh: expert: 8 (over z, y), tensor: 4 (over x, core).
Axes of the slice: x: 2, y: 2, z: 4, core: 2. Of those that a mesh axis runs over, the one named last changes fastest.
Arguments:
- tokens: bfloat16 [3152, 1024], P('expert'), may hold values from -6 to 6
- gain_attn: float32 [1024], replicated, may hold values from 0.5 to 1.5
- shift_attn: float32 [1024], replicated, may hold values from -1.75 to 1.75
- w_qkv: bfloat16 [3, 1024, 1024], P(None, None, 'tensor'), may hold values from -0.1875 to 0.1875
- b_qv: float32 [2, 1024], P(None, 'tensor'), may hold values from -1.75 to 1.75
- w_out: bfloat16 [1024, 1024], P('tensor'), may hold values from -2 to 2
- b_out: float32 [1024], replicated, may hold values from -1.75 to 1.75
- gain_moe: float32 [1024], replicated, may hold values from 0.5 to 1.5
- shift_moe: float32 [1024], replicated, may hold values from -1.75 to 1.75
- w_router: bfloat16 [1024, 8], replicated, may hold values from -0.125 to 0.125
- w_in: bfloat16 [8, 1024, 4096], P('expert', None, 'tensor'), may hold values from -0.1875 to 0.1875
- b_in: float32 [8, 4096], P('expert', 'tensor'), may hold values from -1.75 to 1.75
- w_back: bfloat16 [8, 4096, 1024], P('expert', 'tensor'), may hold values from -0.625 to 0.625
- b_back: float32 [8, 1024], P('expert'), may hold values from -5 to 5
- routes: int32 [3152, 2], P('expert'), may hold values from 0 to 7, all different within a row; in each aligned block of 394 rows (0 to 393, 394 to 787, ...) at most 160 rows name the same one
- d_out: bfloat16 [3152, 1024], P('expert'), may hold values from -8 to 8
Outputs:
- activations: bfloat16 [3152, 1024], P('expert')
- d_tokens: float32 [3152, 1024], P('expert')
- d_gain_attn: float32 [1024], replicated
- d_shift_attn: float32 [1024], replicated
- d_w_qkv: float32 [3, 1024, 1024], P(None, None, 'tensor')
- d_b_qv: float32 [2, 1024], P(None, 'tensor')
- d_w_out: float32 [1024, 1024], P('tensor')
- d_b_out: float32 [1024], replicated
- d_gain_moe: float32 [1024], replicated
- d_shift_moe: float32 [1024], replicated
- d_w_router: float32 [1024, 8], replicated
- d_w_in: float32 [8, 1024, 4096], P('expert', None, 'tensor')
- d_b_in: float32 [8, 4096], P('expert', 'tensor')
- d_w_back: float32 [8, 4096, 1024], P('expert', 'tensor')
- d_b_back: float32 [8, 1024], P('expert')
Inputs may be any that keep to these rules, and one draw needn't show every extreme that they name: `routes`: in the rows of one device no expert is named more than 160 times, and a token's 2 choices differ.
All inputs are finite; a program needn't handle non-finite values.
Results may differ from a plain program's by a relative error of at most 0.019.
Values may be sent and summed in bfloat16 or wider, within the bound.
No kernel may reach another device: no remote copies, remote signals or barrier semaphores. Data moves between devices by JAX's collectives and lax.ppermute only.
A program may use at most 128 MiB of HBM per device.

v0:
```python
import functools

import jax
import jax.numpy as jnp
from jax import lax
from jax.experimental import pallas as pl
from jax.experimental.pallas import tpu as pltpu
from jax.sharding import PartitionSpec as P

HD = 64
SEQ = 197
LANES = 128
VMEM_LIMIT = 52 * 1024 * 1024
EXTRA = 16

epsilon = 1e-06
f32 = jnp.float32
bf16 = jnp.bfloat16


def dot(left, right, left_dim, right_dim, precision=None):
    return lax.dot_general(
        left,
        right,
        (((left_dim,), (right_dim,)), ((), ())),
        precision=precision,
        preferred_element_type=f32,
    )


def call(body, outs, ins, flops, grid=None, in_specs=None, out_specs=None, scalars=0, scratch=()):
    specs = {"scratch_shapes": list(scratch)}
    if grid is not None:
        specs["grid"] = grid
        specs["in_specs"] = in_specs
        specs["out_specs"] = out_specs
    else:
        specs["in_specs"] = [
            pl.BlockSpec(memory_space=pltpu.SMEM if i < scalars else pltpu.VMEM)
            for i in range(len(ins))
        ]
        specs["out_specs"] = [pl.BlockSpec(memory_space=pltpu.VMEM) for _ in outs]
    moved = sum(a.size * a.dtype.itemsize for a in list(ins) + list(outs))
    return pl.pallas_call(
        body,
        out_shape=outs,
        compiler_params=pltpu.CompilerParams(vmem_limit_bytes=VMEM_LIMIT),
        cost_estimate=pl.CostEstimate(flops=flops, bytes_accessed=moved, transcendentals=0),
        **specs,
    )(*ins)


def sds(shape, dtype):
    return jax.ShapeDtypeStruct(shape, dtype)


def swap(values, axis, bit):
    count = lax.axis_size(axis)
    return lax.ppermute(values, axis, [(i, i ^ bit) for i in range(count)])


def bits_of(count):
    return [1 << i for i in range(count.bit_length() - 1)]


def gather_tensor(values, diagonal=False):
    count = lax.axis_size("tensor")
    held = {0: values}
    for bit in reversed(bits_of(count)):
        step = bit ^ 1 if diagonal and bit > 1 else bit
        for key in list(held):
            held[key ^ step] = swap(held[key], "tensor", step)
    return [held[key] for key in range(count)]


def add(left, right):
    return (left.astype(f32) + right.astype(f32)).astype(left.dtype)


def scatter_step(held, bit):
    kept = {}
    for key in sorted(held):
        if not key & bit:
            kept[key] = add(held[key], swap(held[key | bit], "tensor", bit))
    return kept


def butterfly(values, axis):
    for bit in bits_of(lax.axis_size(axis)):
        came = swap(values, axis, bit)
        values = add(values, came)
    return values


def sum_experts(values, order):
    index = lax.axis_index("expert")
    for bit in order:
        half = values.shape[0] // 2
        side = (index & bit) // bit
        keep = lax.dynamic_slice_in_dim(values, side * half, half, 0)
        send = lax.dynamic_slice_in_dim(values, (1 - side) * half, half, 0)
        came = swap(send, "expert", bit)
        values = (keep.astype(f32) + came.astype(f32)).astype(bf16)
    for bit in reversed(order):
        side = (index & bit) // bit
        came = swap(values, "expert", bit)
        values = jnp.where(
            side == 0,
            jnp.concatenate([values, came], 0),
            jnp.concatenate([came, values], 0),
        )
    return values


def norm_parts(values):
    center = values - jnp.mean(values, axis=-1, keepdims=True)
    variance = jnp.mean(center * center, axis=-1, keepdims=True)
    rstd = lax.rsqrt(variance + epsilon)
    return center * rstd, rstd


def norm_back(grad, normal, rstd, gain):
    scaled = grad * gain
    mean_g = jnp.mean(scaled, axis=-1, keepdims=True)
    mean_gn = jnp.mean(scaled * normal, axis=-1, keepdims=True)
    return rstd * (scaled - mean_g - normal * mean_gn)


def same_image(rows):
    left = lax.broadcasted_iota(jnp.int32, (rows, rows), 0)
    right = lax.broadcasted_iota(jnp.int32, (rows, rows), 1)
    left_id = jnp.zeros((rows, rows), jnp.int32)
    right_id = jnp.zeros((rows, rows), jnp.int32)
    for edge in range(SEQ, rows, SEQ):
        left_id = left_id + (left >= edge).astype(jnp.int32)
        right_id = right_id + (right >= edge).astype(jnp.int32)
    return left_id == right_id


def head_probs(queries, keys, inside):
    scores = dot(queries, keys, 1, 1) * (HD ** (-0.5))
    scores = jnp.where(inside, scores, -1e30)
    top = jnp.max(scores, axis=-1, keepdims=True)
    powers = jnp.exp(scores - top)
    return powers * (1.0 / jnp.sum(powers, axis=-1, keepdims=True))


def lane_heads(rows):
    lane = lax.broadcasted_iota(jnp.int32, (rows, LANES), 1)
    return [(lane // HD) == head for head in range(LANES // HD)]


def attend_kernel(tok_ref, gain_ref, shift_ref, w_ref, b_ref, norm_ref, q_ref, k_ref, v_ref, mix_ref):
    rows = tok_ref.shape[0]
    normal, _ = norm_parts(tok_ref[...].astype(f32))
    normed = (normal * gain_ref[...] + shift_ref[...]).astype(bf16)
    norm_ref[...] = normed
    q_ref[...] = (dot(normed, w_ref[0], 1, 0) + b_ref[0:1, :]).astype(bf16)
    k_ref[...] = dot(normed, w_ref[1], 1, 0).astype(bf16)
    v_ref[...] = (dot(normed, w_ref[2], 1, 0) + b_ref[1:2, :]).astype(bf16)
    inside = same_image(rows)
    heads = lane_heads(rows)
    for start in range(0, q_ref.shape[1], LANES):
        cols = slice(start, start + LANES)
        queries, keys, value_rows = q_ref[:, cols], k_ref[:, cols], v_ref[:, cols]
        mixed = jnp.zeros((rows, LANES), f32)
        for mask in heads:
            probs = head_probs(jnp.where(mask, queries, 0).astype(bf16), keys, inside)
            mixed = jnp.where(mask, dot(probs.astype(bf16), value_rows, 1, 0), mixed)
        mix_ref[:, cols] = mixed.astype(bf16)


def slot_numbers(named, earlier, ids, axis, stride):
    numbers = []
    for mask in named:
        slot = jnp.sum(jnp.where(mask, earlier, 0.0), axis=axis, keepdims=True).astype(jnp.int32)
        owner = jnp.sum(jnp.where(mask, ids, 0), axis=axis, keepdims=True)
        numbers.append(owner * stride + slot)
    return numbers


def one_hot(targets, shape, axis):
    ids = lax.broadcasted_iota(jnp.int32, shape, axis)
    table = jnp.zeros(shape, f32)
    for target in targets:
        table = jnp.where(ids == target, 1.0, table)
    return table.astype(bf16)


def route_kernel(
    idx_ref,
    routes_ref,
    flipped_ref,
    dout_ref,
    plain_ref,
    padded_ref,
    dispatch_ref,
    send_ref,
    *,
    experts,
    capacity,
):
    rows = plain_ref.shape[0]
    width = send_ref.shape[1]
    top = routes_ref.shape[1]
    first = lax.broadcasted_iota(jnp.int32, (rows, rows), 0)
    second = lax.broadcasted_iota(jnp.int32, (rows, rows), 1)

    ids = lax.broadcasted_iota(jnp.int32, (experts, rows), 0)
    named = [flipped_ref[k : k + 1, :] == ids for k in range(top)]
    tally = sum(m.astype(f32) for m in named).astype(bf16)
    earlier = dot(tally, (first < second).astype(f32).astype(bf16), 1, 0)
    numbers = slot_numbers(named, earlier, ids, 0, capacity)
    dispatch_ref[...] = one_hot(numbers, dispatch_ref.shape, 0)
    start = pl.multiple_of(idx_ref[0] * width, LANES)
    send_ref[...] = dot(dispatch_ref[...], dout_ref[:, pl.ds(start, width)], 1, 0).astype(bf16)

    ids = lax.broadcasted_iota(jnp.int32, (rows, experts), 1)
    named = [routes_ref[:, k : k + 1] == ids for k in range(top)]
    tally = sum(m.astype(f32) for m in named).astype(bf16)
    earlier = dot((second < first).astype(f32).astype(bf16), tally, 1, 0)
    for ref, stride in ((plain_ref, capacity), (padded_ref, capacity + EXTRA)):
        ref[...] = one_hot(slot_numbers(named, earlier, ids, 1, stride), ref.shape, 1)


def middle_kernel(*refs, blocks):
    idx_ref, refs = refs[0], refs[1:]
    mix_refs, w_refs, refs = refs[:blocks], refs[blocks : 2 * blocks], refs[2 * blocks :]
    tok_ref, bias_ref, gain_ref, shift_ref, router_ref, dispatch_ref = refs[:6]
    resid_ref, second_ref, probs_ref, send_ref, terms_ref = refs[6:]
    width = send_ref.shape[1]
    for key in range(blocks):
        terms_ref[key] = dot(mix_refs[key][...], w_refs[key][...], 1, 0)
    terms = [terms_ref[key] for key in range(blocks)]
    while len(terms) > 1:
        terms = [terms[i] + terms[i + 1] for i in range(0, len(terms), 2)]
    residual = tok_ref[...].astype(f32) + terms[0] + bias_ref[...]
    resid_ref[...] = residual
    normal, _ = norm_parts(residual)
    second_ref[...] = (normal * gain_ref[...] + shift_ref[...]).astype(bf16)
    start = pl.multiple_of((idx_ref[0] & 1) * width, LANES)
    send_ref[...] = dot(dispatch_ref[...], second_ref[:, pl.ds(start, width)], 1, 0).astype(bf16)
    logits = dot(second_ref[...], router_ref[...], 1, 0)
    powers = jnp.exp(logits - jnp.max(logits, axis=-1, keepdims=True))
    probs_ref[...] = powers / jnp.sum(powers, axis=-1, keepdims=True)


def early_kernel(*refs, blocks):
    idx_ref, piece_refs, w_ref = refs[0], refs[1 : 1 + blocks], refs[1 + blocks]
    rows_ref, unscaled_ref = refs[2 + blocks :]
    piece = piece_refs[0].shape[-1]
    for key, piece_ref in enumerate(piece_refs):
        cols = pl.ds(pl.multiple_of((idx_ref[0] ^ key) * piece, LANES), piece)
        rows_ref[:, cols] = piece_ref[...]
    unscaled_ref[...] = dot(rows_ref[...], w_ref[...], 1, 1)


def expert_kernel(
    idx_ref,
    own_ref,
    other_ref,
    grad_ref,
    unscaled_ref,
    w_in_ref,
    b_in_ref,
    b_back_ref,
    router_ref,
    *outs,
    blocks,
):
    piece_refs = outs[:blocks]
    act_ref, pre_ref, grady_ref, gate_ref, dbin_ref, dbback_ref = outs[blocks:]
    count, capacity = piece_refs[0].shape[0], piece_refs[0].shape[1] - EXTRA
    tensor_id, expert_id = idx_ref[0], idx_ref[1]
    side = tensor_id & 1
    width = w_in_ref.shape[0] // 2
    piece = w_in_ref.shape[0] // blocks
    own, other = own_ref[...], other_ref[...]
    low_half = jnp.where(side == 0, own, other)
    high_half = jnp.where(side == 0, other, own)
    logits = dot(low_half, router_ref[0:width, :], 1, 0) + dot(
        high_half, router_ref[width:, :], 1, 0
    )
    powers = jnp.exp(logits - jnp.max(logits, axis=-1, keepdims=True))
    ids = lax.broadcasted_iota(jnp.int32, logits.shape, 1)
    gate = jnp.sum(jnp.where(ids == expert_id, powers, 0.0), axis=-1, keepdims=True) / jnp.sum(
        powers, axis=-1, keepdims=True
    )
    gate_ref[...] = gate
    pre_act = (
        dot(low_half, w_in_ref[0:width, :], 1, 0)
        + dot(high_half, w_in_ref[width:, :], 1, 0)
        + b_in_ref[...]
    )
    cdf = 0.5 * (1.0 + lax.erf(pre_act * (2.0**-0.5)))
    density = jnp.exp(-0.5 * pre_act * pre_act) * 0.3989422804014327
    act = (pre_act * cdf).astype(bf16)
    act_ref[...] = act
    unscaled = unscaled_ref[...]
    grad_pre = (gate * unscaled * (cdf + pre_act * density)).astype(bf16)
    pre_ref[...] = grad_pre
    grad_rows = grad_ref[...].astype(f32)
    gate_grads = jnp.sum(act.astype(f32) * unscaled, axis=1, keepdims=True) + jnp.sum(
        grad_rows * b_back_ref[...], axis=1, keepdims=True
    ) * (1.0 / blocks)
    gate_grads = jnp.broadcast_to(gate_grads, (gate_grads.shape[0], LANES)).T
    grad_y = (gate * grad_rows).astype(bf16)
    grady_ref[...] = grad_y

    @pl.when(pl.program_id(0) == 0)
    def _():
        dbin_ref[...] = jnp.zeros_like(dbin_ref)
        dbback_ref[...] = jnp.zeros_like(dbback_ref)

    dbin_ref[...] += jnp.sum(grad_pre.astype(f32), axis=0, keepdims=True)
    dbback_ref[...] += jnp.sum(grad_y.astype(f32), axis=0, keepdims=True)
    for key, piece_ref in enumerate(piece_refs):
        start = pl.multiple_of((tensor_id ^ key) * piece, LANES)
        rows = dot(grad_pre, w_in_ref[pl.ds(start, piece), :], 1, 1)
        for source in range(count):
            part = slice(source * capacity, (source + 1) * capacity)
            piece_ref[source, 0:capacity, :] = rows[part, :].astype(bf16)
            piece_ref[source, capacity : capacity + EXTRA, :] = jnp.zeros((EXTRA, piece), bf16)
            for first in range(0, capacity, piece):
                lanes = min(piece, capacity - first)
                place = capacity + first // piece
                here = source * capacity + first
                piece_ref[source, place : place + 1, 0:lanes] = gate_grads[
                    0:1, here : here + lanes
                ].astype(bf16)


def back_kernel(idx_ref, act_ref, gate_ref, w_ref, bias_ref, *piece_refs):
    blocks = len(piece_refs)
    piece = piece_refs[0].shape[-1]
    for key, piece_ref in enumerate(piece_refs):
        cols = pl.ds(pl.multiple_of((idx_ref[0] ^ key) * piece, LANES), piece)
        rows = dot(act_ref[...], w_ref[:, cols], 1, 0) + bias_ref[:, cols] * (1.0 / blocks)
        piece_ref[...] = (gate_ref[...] * rows).astype(bf16)


def combine_kernel(place_ref, home_ref, out_ref):
    out_ref[...] = dot(place_ref[...], home_ref[...], 1, 0).astype(bf16)


def finish_kernel(idx_ref, resid_ref, *refs):
    piece_refs, out_ref = refs[:-1], refs[-1]
    piece = piece_refs[0].shape[1]
    for key, piece_ref in enumerate(piece_refs):
        cols = pl.ds(pl.multiple_of((idx_ref[0] ^ key) * piece, LANES), piece)
        out_ref[:, cols] = (resid_ref[:, cols] + piece_ref[...].astype(f32)).astype(bf16)


def residual_kernel(*refs, blocks, capacity):
    idx_ref, piece_refs, refs = refs[0], refs[1 : 1 + blocks], refs[1 + blocks :]
    residual_body(idx_ref, piece_refs, *refs, capacity=capacity)


def residual_body(
    idx_ref,
    piece_refs,
    gg_ref,
    place_ref,
    probs_ref,
    second_ref,
    router_ref,
    resid_ref,
    gain_ref,
    dout_ref,
    w_ref,
    mix_ref,
    grad_ref,
    dw_ref,
    gmix_ref,
    small_ref,
    disp_ref,
    *,
    capacity,
):
    probs = probs_ref[...]
    experts = probs.shape[1]
    slots = place_ref.shape[1]
    piece = piece_refs[0].shape[1]
    stride = capacity + EXTRA
    lane = lax.broadcasted_iota(jnp.int32, (experts, slots), 1)
    first = lax.broadcasted_iota(jnp.int32, (experts, slots), 0) * stride
    segment = (lane >= first) & (lane < first + capacity)
    gate_rows = jnp.where(segment, jnp.broadcast_to(gg_ref[...], (experts, slots)), 0.0)
    grad_probs = dot(place_ref[...], gate_rows.astype(bf16), 1, 1)
    for key, piece_ref in enumerate(piece_refs):
        cols = pl.ds(pl.multiple_of((idx_ref[0] ^ key) * piece, LANES), piece)
        disp_ref[:, cols] = piece_ref[...]
    grad_logits = (
        probs * (grad_probs - jnp.sum(probs * grad_probs, axis=1, keepdims=True))
    ).astype(bf16)
    second_grad = disp_ref[...].astype(f32) + dot(grad_logits, router_ref[...], 1, 1)
    normal, rstd = norm_parts(resid_ref[...])
    grad_resid = dout_ref[...].astype(f32) + norm_back(second_grad, normal, rstd, gain_ref[...])
    grad_ref[...] = grad_resid
    branch = grad_resid.astype(bf16)
    gmix_ref[...] = dot(branch, w_ref[...], 1, 1).astype(bf16)
    dw_ref[...] = dot(mix_ref[...], branch, 0, 0).astype(bf16)
    small_ref[0:experts, :] = dot(grad_logits, second_ref[...], 0, 0)
    small_ref[experts : experts + 1, :] = jnp.sum(second_grad * normal, axis=0, keepdims=True)
    small_ref[experts + 1 : experts + 2, :] = jnp.sum(second_grad, axis=0, keepdims=True)
    small_ref[experts + 2 : experts + 3, :] = jnp.sum(grad_resid, axis=0, keepdims=True)


def attend_back_kernel(
    q_ref, k_ref, v_ref, gmix_ref, norm_ref, w_ref, dw_ref, db_ref, part_ref, gq_ref, gk_ref, gv_ref
):
    rows = q_ref.shape[0]
    inside = same_image(rows)
    heads = lane_heads(rows)
    scale = HD ** (-0.5)
    for start in range(0, q_ref.shape[1], LANES):
        cols = slice(start, start + LANES)
        queries, keys, value_rows = q_ref[:, cols], k_ref[:, cols], v_ref[:, cols]
        grad_mixed = gmix_ref[:, cols]
        grad_q = jnp.zeros((rows, LANES), f32)
        grad_k = jnp.zeros((rows, LANES), f32)
        grad_v = jnp.zeros((rows, LANES), f32)
        for mask in heads:
            one_q = jnp.where(mask, queries, 0).astype(bf16)
            one_g = jnp.where(mask, grad_mixed, 0).astype(bf16)
            probs = head_probs(one_q, keys, inside)
            grad_v = grad_v + dot(probs.astype(bf16), one_g, 0, 0)
            grad_attn = dot(one_g, value_rows, 1, 1)
            delta = jnp.sum(probs * grad_attn, axis=-1, keepdims=True)
            grad_scores = (probs * (grad_attn - delta)).astype(bf16)
            grad_q = jnp.where(mask, dot(grad_scores, keys, 1, 0), grad_q)
            grad_k = grad_k + dot(grad_scores, one_q, 0, 0)
        gq_ref[:, cols] = (grad_q * scale).astype(bf16)
        gk_ref[:, cols] = (grad_k * scale).astype(bf16)
        gv_ref[:, cols] = grad_v.astype(bf16)
    normed = norm_ref[...]
    total = None
    for part, ref in enumerate((gq_ref, gk_ref, gv_ref)):
        grads = ref[...]
        dw_ref[part] = dot(normed, grads, 0, 0).astype(bf16)
        term = dot(grads, w_ref[part], 1, 1)
        total = term if total is None else total + term
    part_ref[...] = total.astype(bf16)
    db_ref[0:1, :] = jnp.sum(gq_ref[...].astype(f32), axis=0, keepdims=True)
    db_ref[1:2, :] = jnp.sum(gv_ref[...].astype(f32), axis=0, keepdims=True)


def first_kernel(tok_ref, gain_ref, grad_ref, resid_ref, out_ref, small_ref):
    normal, rstd = norm_parts(tok_ref[...].astype(f32))
    grad = grad_ref[...].astype(f32)
    out_ref[...] = resid_ref[...] + norm_back(grad, normal, rstd, gain_ref[...])
    small_ref[0:1, :] = jnp.sum(grad * normal, axis=0, keepdims=True)
    small_ref[1:2, :] = jnp.sum(grad, axis=0, keepdims=True)


def on_device(
    tokens,
    gain_attn,
    shift_attn,
    w_qkv,
    b_qv,
    w_out,
    b_out,
    gain_moe,
    shift_moe,
    w_router,
    w_in,
    b_in,
    w_back,
    b_back,
    routes,
    d_out,
):
    groups = lax.axis_size("expert")
    blocks = lax.axis_size("tensor")
    rows, width = tokens.shape
    top = routes.shape[1]
    experts = w_router.shape[1]
    capacity = (top * rows * 16 // (10 * experts) + 7) // 8 * 8
    slots = experts * capacity
    local = w_qkv.shape[2]
    piece = width // blocks
    half = width // 2
    hidden = w_in.shape[2]
    row = lambda vec: vec.reshape(1, -1)
    tensor_id = lax.axis_index("tensor").astype(jnp.int32)
    expert_id = lax.axis_index("expert").astype(jnp.int32)
    ids = jnp.stack([tensor_id, expert_id])
    stride = capacity + EXTRA
    row_bits = bits_of(blocks)

    plain, padded, dispatch_place, grad_send = call(
        functools.partial(route_kernel, experts=experts, capacity=capacity),
        [
            sds((rows, slots), bf16),
            sds((rows, experts * stride), bf16),
            sds((slots, rows), bf16),
            sds((slots, piece), bf16),
        ],
        [ids, routes, routes.T, d_out],
        2 * rows * slots * piece,
        scalars=1,
    )
    w_out_all = gather_tensor(w_out, diagonal=True)
    tokens_in, grad_send = lax.optimization_barrier((tokens, grad_send))
    grad_came = lax.all_to_all(
        grad_send.reshape(experts, capacity, piece), "expert", 0, 0, tiled=True
    ).reshape(slots, piece)

    normed, queries, keys, value_rows, mixed = call(
        attend_kernel,
        [sds((rows, width), bf16)] + [sds((rows, local), bf16)] * 4,
        [tokens_in, row(gain_attn), row(shift_attn), w_qkv, b_qv],
        6 * rows * width * local,
    )
    mixed_all = gather_tensor(mixed)
    residual, second_low, router_probs, send = call(
        functools.partial(middle_kernel, blocks=blocks),
        [
            sds((rows, width), f32),
            sds((rows, width), bf16),
            sds((rows, experts), f32),
            sds((slots, half), bf16),
        ],
        [
            ids,
            *mixed_all,
            *w_out_all,
            tokens,
            row(b_out),
            row(gain_moe),
            row(shift_moe),
            w_router,
            dispatch_place,
        ],
        2 * rows * width * width + 2 * rows * slots * half,
        scalars=1,
        scratch=[pltpu.VMEM((blocks, rows, width), f32)],
    )

    own = lax.all_to_all(
        send.reshape(experts, capacity, half), "expert", 0, 0, tiled=True
    ).reshape(slots, half)
    smem = pl.BlockSpec(memory_space=pltpu.SMEM)
    count = max(1, min(experts, 320 // capacity))
    tile = count * capacity
    steps = slots // tile

    def whole(shape):
        return pl.BlockSpec(shape, lambda i: (0,) * len(shape))

    def by_row(cols):
        return pl.BlockSpec((tile, cols), lambda i: (i, 0))

    grad_rows, unscaled = call(
        functools.partial(early_kernel, blocks=blocks),
        [sds((slots, width), bf16), sds((slots, hidden), f32)],
        [ids, *gather_tensor(grad_came, diagonal=True), w_back[0]],
        2 * slots * width * hidden,
        grid=(steps,),
        in_specs=[smem] + [by_row(piece)] * blocks + [whole((hidden, width))],
        out_specs=[by_row(width), by_row(hidden)],
    )
    own, grad_rows, unscaled = lax.optimization_barrier((own, grad_rows, unscaled))
    other = swap(own, "tensor", 1)

    outs = call(
        functools.partial(expert_kernel, blocks=blocks),
        [sds((experts, stride, piece), bf16)] * blocks
        + [
            sds((slots, hidden), bf16),
            sds((slots, hidden), bf16),
            sds((slots, width), bf16),
            sds((slots, 1), f32),
            sds((1, hidden), f32),
            sds((1, width), f32),
        ],
        [ids, own, other, grad_rows, unscaled, w_in[0], b_in, b_back, w_router],
        4 * slots * width * hidden,
        grid=(steps,),
        in_specs=[
            smem,
            by_row(half),
            by_row(half),
            by_row(width),
            by_row(hidden),
            whole((width, hidden)),
            whole((1, hidden)),
            whole((1, width)),
            whole((width, experts)),
        ],
        out_specs=[pl.BlockSpec((count, stride, piece), lambda i: (i, 0, 0))] * blocks
        + [
            by_row(hidden),
            by_row(hidden),
            by_row(width),
            by_row(1),
            whole((1, hidden)),
            whole((1, width)),
        ],
    )
    held = scatter_step(dict(enumerate(outs[:blocks])), row_bits[0])
    activated, grad_pre, grad_y, gate, d_b_in, d_b_back = outs[blocks:]
    held, activated, grad_pre, grad_y = lax.optimization_barrier(
        (held, activated, grad_pre, grad_y)
    )

    out_pieces = call(
        back_kernel,
        [sds((slots, piece), bf16)] * blocks,
        [ids, activated, gate, w_back[0], b_back],
        2 * slots * width * hidden,
        grid=(steps,),
        in_specs=[smem, by_row(hidden), by_row(1), whole((hidden, width)), whole((1, width))],
        out_specs=[by_row(piece)] * blocks,
    )
    out_held = scatter_step(dict(enumerate(out_pieces)), row_bits[0])

    for bit in row_bits[1:]:
        held = scatter_step(held, bit)
    home = lax.all_to_all(held[0], "expert", 0, 0, tiled=True)
    for bit in row_bits[1:]:
        out_held = scatter_step(out_held, bit)

    d_w_back = dot(activated, grad_y, 0, 0)[None]
    side = tensor_id & 1
    rows_in = jnp.where(
        side == 0,
        jnp.concatenate([own, other], axis=1),
        jnp.concatenate([other, own], axis=1),
    )
    d_w_in = dot(rows_in, grad_pre, 0, 0)[None]
    home, d_w_back, d_w_in = lax.optimization_barrier((home, d_w_back, d_w_in))
    out_sent = out_held[0]
    dispatch = call(
        combine_kernel,
        [sds((rows, piece), bf16)],
        [padded, home.reshape(experts * stride, piece)],
        2 * rows * slots * piece,
    )[0]
    dispatch_all = gather_tensor(dispatch)
    gate_lines = -(-capacity // piece)
    gate_grads = home[:, capacity : capacity + gate_lines, :].reshape(experts, gate_lines * piece)
    gate_grads = jnp.pad(gate_grads[:, :capacity].astype(f32), ((0, 0), (0, EXTRA)))
    gate_grads = gate_grads.reshape(1, experts * stride)

    out_home = lax.all_to_all(
        out_sent.reshape(experts, capacity, piece), "expert", 0, 0, tiled=True
    ).reshape(slots, piece)
    mixture = call(
        combine_kernel, [sds((rows, piece), bf16)], [plain, out_home], 2 * rows * slots * piece
    )[0]
    activations = call(
        finish_kernel,
        [sds((rows, width), bf16)],
        [ids, residual, *gather_tensor(mixture)],
        rows * width,
        scalars=1,
    )[0]

    grad_resid, d_w_out, grad_mixed, small = call(
        functools.partial(residual_kernel, blocks=blocks, capacity=capacity),
        [
            sds((rows, width), f32),
            sds((local, width), bf16),
            sds((rows, local), bf16),
            sds((experts + 3, width), f32),
        ],
        [
            ids,
            *dispatch_all,
            gate_grads,
            padded,
            router_probs,
            second_low,
            w_router,
            residual,
            row(gain_moe),
            d_out,
            w_out,
            mixed,
        ],
        4 * rows * width * local,
        scalars=1,
        scratch=[pltpu.VMEM((rows, width), bf16)],
    )
    d_w_qkv, d_b_qv, partial_grad, _, _, _ = call(
        attend_back_kernel,
        [
            sds((3, width, local), bf16),
            sds((2, local), f32),
            sds((rows, width), bf16),
            sds((rows, local), bf16),
            sds((rows, local), bf16),
            sds((rows, local), bf16),
        ],
        [queries, keys, value_rows, grad_mixed, normed, w_qkv],
        12 * rows * width * local,
    )
    order = bits_of(groups)
    d_w_out = sum_experts(d_w_out, order)
    cut = 3 * width // 2
    d_w_qkv = d_w_qkv.reshape(3 * width, local)
    d_w_qkv = jnp.concatenate(
        [
            sum_experts(d_w_qkv[:cut], order),
            sum_experts(d_w_qkv[cut:], order[1:2] + order[:1] + order[2:]),
        ],
        axis=0,
    ).reshape(3, width, local)

    grad_normed = butterfly(partial_grad, "tensor")
    d_tokens, first_small = call(
        first_kernel,
        [sds((rows, width), f32), sds((2, width), f32)],
        [tokens, row(gain_attn), grad_normed, grad_resid],
        rows * width,
    )
    bias_row = jnp.pad(d_b_qv, ((0, 0), (0, width - local)))
    packed = jnp.concatenate([small, first_small, bias_row], axis=0).astype(bf16)
    packed = butterfly(packed, "expert").astype(f32)
    return (
        activations,
        d_tokens,
        packed[experts + 3],
        packed[experts + 4],
        d_w_qkv.astype(f32),
        packed[experts + 5 : experts + 7, :local],
        d_w_out.astype(f32),
        packed[experts + 2],
        packed[experts],
        packed[experts + 1],
        packed[:experts].T,
        d_w_in,
        d_b_in,
        d_w_back,
        d_b_back,
    )


def solution(mesh):
    in_specs = (
        P("expert", None),
        P(),
        P(),
        P(None, None, "tensor"),
        P(None, "tensor"),
        P("tensor", None),
        P(),
        P(),
        P(),
        P(),
        P("expert", None, "tensor"),
        P("expert", "tensor"),
        P("expert", "tensor", None),
        P("expert", None),
        P("expert", None),
        P("expert", None),
    )
    out_specs = (
        P("expert", None),
        P("expert", None),
        P(),
        P(),
        P(None, None, "tensor"),
        P(None, "tensor"),
        P("tensor", None),
        P(),
        P(),
        P(),
        P(),
        P("expert", None, "tensor"),
        P("expert", "tensor"),
        P("expert", "tensor", None),
        P("expert", None),
    )
    return jax.shard_map(
        on_device, mesh=mesh, in_specs=in_specs, out_specs=out_specs, check_vma=False
    )
```

profile of v0, /device:TPU:0, one launch (start us, length us, event | category | flops | bytes accessed | tf_op | source)
XLA Modules:
  0.0 255.7 jit_solution(13029953103270233565)
XLA Ops:
  5.9 4.4 %shard_map.271 = (bf16[394,1280]{1,0:T(8,128)(2,1)}, bf16[394,1408]{1,0:T(8,128)(2,1)}, bf16[1280,394]{1,0:T(8,128)(2,1)}, bf16[1280,256]{1,0:T(8,128)(2,1)}) custom-call(s32[2]{0:T(128)S(1)} %pad_add_fusion.idx_ref.refs_0_, s32[394,2]{1,0:T(8,128)S(1)} %copy.35.routes_ref, s32[2,394]{1,0:T(2,128)S(1)} %bitcast.46, bf16[394,1024]{1,0:T(8,128)(2,1)S(1)} %copy-done.1), custom_call_target="tpu_custom_call" | custom-call | flops 258211840 | bytes 4595368 | tf_op jit(solution)/shard_map/pallas_call | solution.py:44
  10.3 6.0 %all-to-all-start.1 = ((bf16[8,160,256]{2,1,0:T(8,128)(2,1)}), bf16[8,160,256]{2,1,0:T(8,128)(2,1)S(1)}, u32[]{:S(2)}, u32[]{:S(2)}) async-start(bf16[8,160,256]{2,1,0:T(8,128)(2,1)} %bitcast.10), calls=%async_computation.1 | async-start | bytes 1310720 | tf_op jit(solution)/shard_map/all_to_all | solution.py:506
  16.9 4.7 %shard_map.272 = (bf16[394,1024]{1,0:T(8,128)(2,1)S(1)}, bf16[394,256]{1,0:T(8,128)(2,1)S(1)}, bf16[394,256]{1,0:T(8,128)(2,1)S(1)}, bf16[394,256]{1,0:T(8,128)(2,1)S(1)}, bf16[394,256]{1,0:T(8,128)(2,1)S(1)}) custom-call(bf16[394,1024]{1,0:T(8,128)(2,1)} %tok_ref.2, f32[1,1024]{1,0:T(1,128)S(1)} %bitcast.44, f32[1,1024]{1,0:T(1,128)S(1)} %bitcast.47, ...), custom_call_target="tpu_custom_call" | custom-call | flops 619708416 | bytes 4003840 | tf_op jit(solution)/shard_map/pallas_call | solution.py:44
  24.6 5.9 %collective-permute-done.1.refs_3_ = bf16[394,256]{1,0:T(8,128)(2,1)S(1)} collective-permute-done((bf16[394,256]{1,0:T(8,128)(2,1)S(1)}, bf16[394,256]{1,0:T(8,128)(2,1)S(1)}, u32[]{:S(2)}, u32[]{:S(2)}) %collective-permute-start.1) | collective-permute-done | bytes 201760 | tf_op jit(solution)/shard_map/ppermute | solution.py:59
  32.0 5.6 %shard_map.273 = (f32[394,1024]{1,0:T(8,128)}, bf16[394,1024]{1,0:T(8,128)(2,1)}, f32[394,8]{1,0:T(8,128)S(1)}, bf16[1280,512]{1,0:T(8,128)(2,1)}) custom-call(s32[2]{0:T(128)S(1)} %pad_add_fusion.idx_ref.refs_0_, bf16[394,256]{1,0:T(8,128)(2,1)S(1)} %get-tuple-element.68.refs_1_.refs_14_, bf16[394,256]{1,0:T(8,128)(2,1)S(1)} %collective-permute-done.refs_2_, ...), custom_call_target="tpu_custom_call" | custom-call | flops 1342701568 | bytes 8492360 | tf_op jit(solution)/shard_map/pallas_call | solution.py:44
  37.6 5.8 %all-to-all-start = ((bf16[8,160,512]{2,1,0:T(8,128)(2,1)}), bf16[8,160,512]{2,1,0:T(8,128)(2,1)S(1)}, u32[]{:S(2)}, u32[]{:S(2)}) async-start(bf16[8,160,512]{2,1,0:T(8,128)(2,1)} %bitcast.55), calls=%async_computation | async-start | bytes 2621440 | tf_op jit(solution)/shard_map/all_to_all | solution.py:541
  44.9 15.4 %collective-permute-done.7.refs_4_ = bf16[1280,256]{1,0:T(8,128)(2,1)S(1)} collective-permute-done((bf16[1280,256]{1,0:T(8,128)(2,1)S(1)}, bf16[1280,256]{1,0:T(8,128)(2,1)S(1)}, u32[]{:S(2)}, u32[]{:S(2)}) %collective-permute-start.7) | collective-permute-done | bytes 655392 | tf_op jit(solution)/shard_map/ppermute | solution.py:59
  62.4 6.9 %shard_map.274 = (bf16[1280,1024]{1,0:T(8,128)(2,1)}, f32[1280,1024]{1,0:T(8,128)}) custom-call(s32[2]{0:T(128)S(1)} %pad_add_fusion.idx_ref.refs_0_, bf16[1280,256]{1,0:T(8,128)(2,1)S(1)} %bitcast.41, bf16[1280,256]{1,0:T(8,128)(2,1)S(1)} %collective-permute-done.6.refs_2_, bf16[1280,256]{1,0:T(8,128)(2,1)S(1)} %collective-permute-done.8.refs_3_, ...), custom_call_target="tpu_custom_call" | custom-call | flops 2684354560 | bytes 12582920 | tf_op jit(solution)/shard_map/pallas_call | solution.py:44
  69.3 5.7 %all-to-all-done = bf16[8,160,512]{2,1,0:T(8,128)(2,1)S(1)} async-done(((bf16[8,160,512]{2,1,0:T(8,128)(2,1)}), bf16[8,160,512]{2,1,0:T(8,128)(2,1)S(1)}, u32[]{:S(2)}, u32[]{:S(2)}) %all-to-all-start) | async-done | bytes 1310752 | tf_op jit(solution)/shard_map/all_to_all | solution.py:541
  75.1 3.2 %collective-permute-done.9.other_ref = bf16[1280,512]{1,0:T(8,128)(2,1)} collective-permute-done((bf16[1280,512]{1,0:T(8,128)(2,1)S(1)}, bf16[1280,512]{1,0:T(8,128)(2,1)}, u32[]{:S(2)}, u32[]{:S(2)}) %collective-permute-start.9) | collective-permute-done | bytes 1310752 | tf_op jit(solution)/shard_map/ppermute | solution.py:59
  78.2 17.2 %shard_map.275 = (bf16[8,176,256]{2,1,0:T(8,128)(2,1)S(1)}, bf16[8,176,256]{2,1,0:T(8,128)(2,1)}, bf16[8,176,256]{2,1,0:T(8,128)(2,1)}, bf16[8,176,256]{2,1,0:T(...) custom-call(s32[2]{0:T(128)S(1)} %pad_add_fusion.idx_ref.refs_0_, ...), custom_call_target="tpu_custom_call" | custom-call | flops 5368709120 | bytes 23368712 | tf_op jit(solution)/shard_map/pallas_call | solution.py:44
  101.8 6.5 %shard_map.276 = (bf16[1280,256]{1,0:T(8,128)(2,1)S(1)}, bf16[1280,256]{1,0:T(8,128)(2,1)}, bf16[1280,256]{1,0:T(8,128)(2,1)S(1)}, bf16[1280,256]{1,0:T(8,128)(2,1)}) custom-call(s32[2]{0:T(128)S(1)} %pad_add_fusion.idx_ref.refs_0_, bf16[1280,1024]{1,0:T(8,128)(2,1)} %get-tuple-element.86.act_ref, f32[1280,1]{1,0:T(8,128)} %copy-done.18, ...), custom_call_target="tpu_custom_call" | custom-call | flops 2684354560 | bytes 7349256 | tf_op jit(solution)/shard_map/pallas_call | solution.py:44
  108.8 10.1 %collective-permute-done.18 = bf16[8,176,256]{2,1,0:T(8,128)(2,1)} collective-permute-done((bf16[8,176,256]{2,1,0:T(8,128)(2,1)}, bf16[8,176,256]{2,1,0:T(8,128)(2,1)}, u32[]{:S(2)}, u32[]{:S(2)}) %collective-permute-start.18) | collective-permute-done | bytes 720928 | tf_op jit(solution)/shard_map/ppermute | solution.py:59
  121.0 3.6 %all-to-all-start.3 = ((bf16[8,176,256]{2,1,0:T(8,128)(2,1)}), bf16[8,176,256]{2,1,0:T(8,128)(2,1)S(1)}, u32[]{:S(2)}, u32[]{:S(2)}) async-start(bf16[8,176,256]{2,1,0:T(8,128)(2,1)} %add_convert_fusion.2), calls=%async_computation.3 | async-start | bytes 1441792 | tf_op jit(solution)/shard_map/all_to_all | solution.py:621
  124.7 8.5 %fusion.7 = f32[1,1024,1024]{2,1,0:T(8,128)} fusion(bf16[1280,1024]{1,0:T(8,128)(2,1)} %get-tuple-element.99, bf16[1280,512]{1,0:T(8,128)(2,1)} %collective-permute-done.9.other_ref, bf16[1280,512]{1,0:T(8,128)(2,1)} %bitcast.54, pred[]{:T(512)S(6)} %eq.8), kind=kOutput, calls=%fused_computation.8 | convolution fusion | flops 2696151040 | bytes 9437185 | tf_op jit(solution)/shard_map/dot_general | solution.py:22
  136.8 4.4 %convolution_bitcast_fusion = f32[1,1024,1024]{2,1,0:T(8,128)} fusion(bf16[1280,1024]{1,0:T(8,128)(2,1)S(1)} %copy-done.28, bf16[1280,1024]{1,0:T(8,128)(2,1)S(1)} %copy-done.29), kind=kOutput, calls=%fused_computation.9 | convolution fusion | flops 2684354560 | bytes 9437184 | tf_op jit(solution)/shard_map/dot_general | solution.py:22
  146.3 7.0 %collective-permute-done.14 = bf16[1280,256]{1,0:T(8,128)(2,1)S(1)} collective-permute-done((bf16[1280,256]{1,0:T(8,128)(2,1)}, bf16[1280,256]{1,0:T(8,128)(2,1)S(1)}, u32[]{:S(2)}, u32[]{:S(2)}) %collective-permute-start.14) | collective-permute-done | bytes 655392 | tf_op jit(solution)/shard_map/ppermute | solution.py:59
  155.4 6.0 %all-to-all-start.2 = ((bf16[8,160,256]{2,1,0:T(8,128)(2,1)}), bf16[8,160,256]{2,1,0:T(8,128)(2,1)S(1)}, u32[]{:S(2)}, u32[]{:S(2)}) async-start(bf16[8,160,256]{2,1,0:T(8,128)(2,1)} %bitcast.14), calls=%async_computation.2 | async-start | bytes 1310720 | tf_op jit(solution)/shard_map/all_to_all | solution.py:647
  163.1 6.1 %shard_map.280 = (f32[394,1024]{1,0:T(8,128)}, bf16[256,1024]{1,0:T(8,128)(2,1)}, bf16[394,256]{1,0:T(8,128)(2,1)S(1)}, f32[11,1024]{1,0:T(8,128)S(1)}) custom-call(s32[2]{0:T(128)S(1)} %pad_add_fusion.idx_ref.refs_0_, bf16[394,256]{1,0:T(8,128)(2,1)S(1)} %shard_map.279.refs_1_, bf16[394,256]{1,0:T(8,128)(2,1)S(1)} %collective-permute-done.19.refs_2_, ...), custom_call_target="tpu_custom_call" | custom-call | flops 413138944 | bytes 8293704 | tf_op jit(solution)/shard_map/pallas_call | solution.py:44
  172.3 7.9 %shard_map.281 = (bf16[3,1024,256]{2,1,0:T(8,128)(2,1)}, f32[2,256]{1,0:T(2,128)S(1)}, bf16[394,1024]{1,0:T(8,128)(2,1)}, bf16[394,256]{1,0:T(8,128)(2,1)}, bf16...) custom-call(bf16[394,256]{1,0:T(8,128)(2,1)S(1)} %get-tuple-element.92.q_ref, bf16[394,256]{1,0:T(8,128)(2,1)S(1)} %copy-done.13, ...), custom_call_target="tpu_custom_call" | custom-call | flops 1239416832 | bytes 6173696 | tf_op jit(solution)/shard_map/pallas_call | solution.py:44
  180.1 2.7 %fusion.14 = (bf16[1536,256]{1,0:T(8,128)(2,1)}, bf16[1536,256]{1,0:T(8,128)(2,1)}) fusion(bf16[3072,256]{1,0:T(8,128)(2,1)} %bitcast.51), kind=kLoop, calls=%fused_computation.60 | loop fusion | bytes 3145728 | tf_op jit(solution)/shard_map/slice | solution.py:706
  187.4 3.1 %collective-permute-done.16.refs_2_ = bf16[394,256]{1,0:T(8,128)(2,1)S(1)} collective-permute-done((bf16[394,256]{1,0:T(8,128)(2,1)S(1)}, bf16[394,256]{1,0:T(8,128)(2,1)S(1)}, u32[]{:S(2)}, u32[]{:S(2)}) %collective-permute-start.16) | collective-permute-done | bytes 201760 | tf_op jit(solution)/shard_map/ppermute | solution.py:59
  191.4 5.7 %collective-permute-done.27 = bf16[768,256]{1,0:T(8,128)(2,1)S(1)} collective-permute-done((bf16[768,256]{1,0:T(8,128)(2,1)S(1)}, bf16[768,256]{1,0:T(8,128)(2,1)S(1)}, u32[]{:S(2)}, u32[]{:S(2)}) %collective-permute-start.27) | collective-permute-done | bytes 393248 | tf_op jit(solution)/shard_map/ppermute | solution.py:59
  200.3 2.6 %collective-permute-done.41 = bf16[32,1024]{1,0:T(8,128)(2,1)S(1)} collective-permute-done((bf16[32,1024]{1,0:T(8,128)(2,1)S(1)}, bf16[32,1024]{1,0:T(8,128)(2,1)S(1)}, u32[]{:S(2)}, u32[]{:S(2)}) %collective-permute-start.41) | collective-permute-done | bytes 65568 | tf_op jit(solution)/shard_map/ppermute | solution.py:59
  206.2 2.5 shard_map.278
  208.9 2.6 %collective-permute-start.29 = (bf16[192,256]{1,0:T(8,128)(2,1)S(1)}, bf16[192,256]{1,0:T(8,128)(2,1)S(1)}, u32[]{:S(2)}, u32[]{:S(2)}) collective-permute-start(bf16[192,256]{1,0:T(8,128)(2,1)S(1)} %constant_dynamic-slice_fusion.6), channel_id=1, source_target_pairs={{0,16},{4,20},{8,24},{12,28},{16,0},{20,4},{24,8},{28,12},{1,17},{... | collective-permute-start | bytes 294920 | tf_op jit(solution)/shard_map/ppermute | solution.py:59
  212.0 4.7 %collective-permute-done.43 = bf16[64,1024]{1,0:T(8,128)(2,1)S(1)} collective-permute-done((bf16[64,1024]{1,0:T(8,128)(2,1)S(1)}, bf16[64,1024]{1,0:T(8,128)(2,1)S(1)}, u32[]{:S(2)}, u32[]{:S(2)}) %collective-permute-start.43) | collective-permute-done | bytes 131104 | tf_op jit(solution)/shard_map/ppermute | solution.py:59
  219.4 2.6 %collective-permute-done.35 = bf16[192,256]{1,0:T(8,128)(2,1)S(1)} collective-permute-done((bf16[192,256]{1,0:T(8,128)(2,1)S(1)}, bf16[192,256]{1,0:T(8,128)(2,1)S(1)}, u32[]{:S(2)}, u32[]{:S(2)}) %collective-permute-start.35) | collective-permute-done | bytes 98336 | tf_op jit(solution)/shard_map/ppermute | solution.py:59
  223.3 4.2 %collective-permute-start.31 = (bf16[384,256]{1,0:T(8,128)(2,1)S(1)}, bf16[384,256]{1,0:T(8,128)(2,1)S(1)}, u32[]{:S(2)}, u32[]{:S(2)}) collective-permute-start(bf16[384,256]{1,0:T(8,128)(2,1)S(1)} %maximum_select_fusion.10), channel_id=1, source_target_pairs={{0,8},{4,12},{8,0},{12,4},{16,24},{20,28},{24,16},{28,20},{1,9},{5... | collective-permute-start | bytes 589832 | tf_op jit(solution)/shard_map/ppermute | solution.py:59
  232.9 2.8 %collective-permute-done.37 = bf16[384,256]{1,0:T(8,128)(2,1)S(1)} collective-permute-done((bf16[384,256]{1,0:T(8,128)(2,1)S(1)}, bf16[384,256]{1,0:T(8,128)(2,1)S(1)}, u32[]{:S(2)}, u32[]{:S(2)}) %collective-permute-start.37) | collective-permute-done | bytes 196640 | tf_op jit(solution)/shard_map/ppermute | solution.py:59
  237.1 3.9 %shard_map.282 = (f32[394,1024]{1,0:T(8,128)}, f32[2,1024]{1,0:T(2,128)S(1)}) custom-call(bf16[394,1024]{1,0:T(8,128)(2,1)S(1)} %copy-done, f32[1,1024]{1,0:T(1,128)S(1)} %bitcast.45, bf16[394,1024]{1,0:T(8,128)(2,1)S(1)} %add_convert_fusion.grad_ref, f32[394,1024]{1,0:T(8,128)} %get-tuple-element.106.resid_ref), custom_call_target="tpu_custom_call" | custom-call | flops 403456 | bytes 4853760 | tf_op jit(solution)/shard_map/pallas_call | solution.py:44
  246.6 2.4 collective-permute-done.25
  (194 shorter events, 74.0 us)
Async XLA Ops:
  0.7 16.1 %collective-permute-start.4 = (bf16[256,1024]{1,0:T(8,128)(2,1)}, bf16[256,1024]{1,0:T(8,128)(2,1)S(1)}, u32[]{:S(2)}, u32[]{:S(2)}) collective-permute-start(bf16[256,1024]{1,0:T(8,128)(2,1)} %refs_13_.2), channel_id=1, source_target_pairs={{0,3},{1,2},{2,1},{3,0},{4,7},{5,6},{6,5},{7,4},{8,11},{9,10},{10,... | collective-permute-start | bytes 1572872 | tf_op jit(solution)/shard_map/ppermute | solution.py:59
  10.3 27.3 %all-to-all-start.1 = ((bf16[8,160,256]{2,1,0:T(8,128)(2,1)}), bf16[8,160,256]{2,1,0:T(8,128)(2,1)S(1)}, u32[]{:S(2)}, u32[]{:S(2)}) async-start(bf16[8,160,256]{2,1,0:T(8,128)(2,1)} %bitcast.10), calls=%async_computation.1 | async-start | bytes 1310720 | tf_op jit(solution)/shard_map/all_to_all | solution.py:506
  16.3 15.7 %collective-permute-start.3 = (bf16[256,1024]{1,0:T(8,128)(2,1)S(1)}, bf16[256,1024]{1,0:T(8,128)(2,1)}, u32[]{:S(2)}, u32[]{:S(2)}) collective-permute-start(bf16[256,1024]{1,0:T(8,128)(2,1)S(1)} %copy-done.2), channel_id=1, source_target_pairs={{0,1},{1,0},{2,3},{3,2},{4,5},{5,4},{6,7},{7,6},{8,9},{9,8},{10,11... | collective-permute-start | bytes 1572872 | tf_op jit(solution)/shard_map/ppermute | solution.py:59
  16.7 15.3 %collective-permute-start.5 = (bf16[256,1024]{1,0:T(8,128)(2,1)S(1)}, bf16[256,1024]{1,0:T(8,128)(2,1)}, u32[]{:S(2)}, u32[]{:S(2)}) collective-permute-start(bf16[256,1024]{1,0:T(8,128)(2,1)S(1)} %collective-permute-done.4.refs_8_), channel_id=1, source_target_pairs={{0,1},{1,0},{2,3},{3,2},{4,5},{5,4},{6,7},{7,6},{8,9},{9,8},{10,11... | collective-permute-start | bytes 1572872 | tf_op jit(solution)/shard_map/ppermute | solution.py:59
  23.2 7.3 %collective-permute-start.1 = (bf16[394,256]{1,0:T(8,128)(2,1)S(1)}, bf16[394,256]{1,0:T(8,128)(2,1)S(1)}, u32[]{:S(2)}, u32[]{:S(2)}) collective-permute-start(bf16[394,256]{1,0:T(8,128)(2,1)S(1)} %get-tuple-element.68.refs_1_.refs_14_), channel_id=1, source_target_pairs={{0,2},{1,3},{2,0},{3,1},{4,6},{5,7},{6,4},{7,5},{8,10},{9,11},{10,... | collective-permute-start | bytes 605192 | tf_op jit(solution)/shard_map/ppermute | solution.py:59
  37.6 37.5 %all-to-all-start = ((bf16[8,160,512]{2,1,0:T(8,128)(2,1)}), bf16[8,160,512]{2,1,0:T(8,128)(2,1)S(1)}, u32[]{:S(2)}, u32[]{:S(2)}) async-start(bf16[8,160,512]{2,1,0:T(8,128)(2,1)} %bitcast.55), calls=%async_computation | async-start | bytes 2621440 | tf_op jit(solution)/shard_map/all_to_all | solution.py:541
  43.4 17.0 %collective-permute-start.7 = (bf16[1280,256]{1,0:T(8,128)(2,1)S(1)}, bf16[1280,256]{1,0:T(8,128)(2,1)S(1)}, u32[]{:S(2)}, u32[]{:S(2)}) collective-permute-start(bf16[1280,256]{1,0:T(8,128)(2,1)S(1)} %bitcast.39), channel_id=1, source_target_pairs={{0,3},{1,2},{2,1},{3,0},{4,7},{5,6},{6,5},{7,4},{8,11},{9,10},{10,... | collective-permute-start | bytes 1966088 | tf_op jit(solution)/shard_map/ppermute | solution.py:59
  44.3 16.2 %collective-permute-start.6 = (bf16[1280,256]{1,0:T(8,128)(2,1)S(1)}, bf16[1280,256]{1,0:T(8,128)(2,1)S(1)}, u32[]{:S(2)}, u32[]{:S(2)}) collective-permute-start(bf16[1280,256]{1,0:T(8,128)(2,1)S(1)} %bitcast.40), channel_id=1, source_target_pairs={{0,1},{1,0},{2,3},{3,2},{4,5},{5,4},{6,7},{7,6},{8,9},{9,8},{10,11... | collective-permute-start | bytes 1966088 | tf_op jit(solution)/shard_map/ppermute | solution.py:59
  100.3 18.6 %collective-permute-start.18 = (bf16[8,176,256]{2,1,0:T(8,128)(2,1)}, bf16[8,176,256]{2,1,0:T(8,128)(2,1)}, u32[]{:S(2)}, u32[]{:S(2)}) collective-permute-start(bf16[8,176,256]{2,1,0:T(8,128)(2,1)} %add_convert_fusion.3), channel_id=1, source_target_pairs={{0,2},{1,3},{2,0},{3,1},{4,6},{5,7},{6,4},{7,5},{8,10},{9,11},{10,... | collective-permute-start | bytes 2162696 | tf_op jit(solution)/shard_map/ppermute | solution.py:59
  108.3 25.0 %collective-permute-start.13 = (bf16[1280,256]{1,0:T(8,128)(2,1)}, bf16[1280,256]{1,0:T(8,128)(2,1)}, u32[]{:S(2)}, u32[]{:S(2)}) collective-permute-start(bf16[1280,256]{1,0:T(8,128)(2,1)} %get-tuple-element.91), channel_id=1, source_target_pairs={{0,1},{1,0},{2,3},{3,2},{4,5},{5,4},{6,7},{7,6},{8,9},{9,8},{10,11... | collective-permute-start | bytes 1966088 | tf_op jit(solution)/shard_map/ppermute | solution.py:59
  108.3 38.0 %collective-permute-start.12 = (bf16[1280,256]{1,0:T(8,128)(2,1)}, bf16[1280,256]{1,0:T(8,128)(2,1)}, u32[]{:S(2)}, u32[]{:S(2)}) collective-permute-start(bf16[1280,256]{1,0:T(8,128)(2,1)} %get-tuple-element.89), channel_id=1, source_target_pairs={{0,1},{1,0},{2,3},{3,2},{4,5},{5,4},{6,7},{7,6},{8,9},{9,8},{10,11... | collective-permute-start | bytes 1966088 | tf_op jit(solution)/shard_map/ppermute | solution.py:59
  121.0 22.0 %all-to-all-start.3 = ((bf16[8,176,256]{2,1,0:T(8,128)(2,1)}), bf16[8,176,256]{2,1,0:T(8,128)(2,1)S(1)}, u32[]{:S(2)}, u32[]{:S(2)}) async-start(bf16[8,176,256]{2,1,0:T(8,128)(2,1)} %add_convert_fusion.2), calls=%async_computation.3 | async-start | bytes 1441792 | tf_op jit(solution)/shard_map/all_to_all | solution.py:621
  135.3 17.9 %collective-permute-start.14 = (bf16[1280,256]{1,0:T(8,128)(2,1)}, bf16[1280,256]{1,0:T(8,128)(2,1)S(1)}, u32[]{:S(2)}, u32[]{:S(2)}) collective-permute-start(bf16[1280,256]{1,0:T(8,128)(2,1)} %add_convert_fusion.6), channel_id=1, source_target_pairs={{0,2},{1,3},{2,0},{3,1},{4,6},{5,7},{6,4},{7,5},{8,10},{9,11},{10,... | collective-permute-start | bytes 1966088 | tf_op jit(solution)/shard_map/ppermute | solution.py:59
  144.8 16.7 %collective-permute-start.20 = (bf16[394,256]{1,0:T(8,128)(2,1)S(1)}, bf16[394,256]{1,0:T(8,128)(2,1)S(1)}, u32[]{:S(2)}, u32[]{:S(2)}) collective-permute-start(bf16[394,256]{1,0:T(8,128)(2,1)S(1)} %shard_map.279.refs_1_), channel_id=1, source_target_pairs={{0,2},{1,3},{2,0},{3,1},{4,6},{5,7},{6,4},{7,5},{8,10},{9,11},{10,... | collective-permute-start | bytes 605192 | tf_op jit(solution)/shard_map/ppermute | solution.py:59
  155.4 27.5 %all-to-all-start.2 = ((bf16[8,160,256]{2,1,0:T(8,128)(2,1)}), bf16[8,160,256]{2,1,0:T(8,128)(2,1)S(1)}, u32[]{:S(2)}, u32[]{:S(2)}) async-start(bf16[8,160,256]{2,1,0:T(8,128)(2,1)} %bitcast.14), calls=%async_computation.2 | async-start | bytes 1310720 | tf_op jit(solution)/shard_map/all_to_all | solution.py:647
  170.2 14.6 %collective-permute-start.39 = (bf16[128,1024]{1,0:T(8,128)(2,1)S(1)}, bf16[128,1024]{1,0:T(8,128)(2,1)S(1)}, u32[]{:S(2)}, u32[]{:S(2)}) collective-permute-start(bf16[128,1024]{1,0:T(8,128)(2,1)S(1)} %constant_dynamic-slice_fusion.2), channel_id=1, source_target_pairs={{0,4},{4,0},{8,12},{12,8},{16,20},{20,16},{24,28},{28,24},{1,5},{5... | collective-permute-start | bytes 786440 | tf_op jit(solution)/shard_map/ppermute | solution.py:59
  183.3 7.1 %collective-permute-start.16 = (bf16[394,256]{1,0:T(8,128)(2,1)S(1)}, bf16[394,256]{1,0:T(8,128)(2,1)S(1)}, u32[]{:S(2)}, u32[]{:S(2)}) collective-permute-start(bf16[394,256]{1,0:T(8,128)(2,1)S(1)} %shard_map.277.refs_0_), channel_id=1, source_target_pairs={{0,2},{1,3},{2,0},{3,1},{4,6},{5,7},{6,4},{7,5},{8,10},{9,11},{10,... | collective-permute-start | bytes 605192 | tf_op jit(solution)/shard_map/ppermute | solution.py:59
  186.5 10.6 %collective-permute-start.27 = (bf16[768,256]{1,0:T(8,128)(2,1)S(1)}, bf16[768,256]{1,0:T(8,128)(2,1)S(1)}, u32[]{:S(2)}, u32[]{:S(2)}) collective-permute-start(bf16[768,256]{1,0:T(8,128)(2,1)S(1)} %constant_dynamic-slice_fusion.8), channel_id=1, source_target_pairs={{0,4},{4,0},{8,12},{12,8},{16,20},{20,16},{24,28},{28,24},{1,5},{5... | collective-permute-start | bytes 1179656 | tf_op jit(solution)/shard_map/ppermute | solution.py:59
  187.2 12.4 %collective-permute-start.33 = (bf16[768,256]{1,0:T(8,128)(2,1)S(1)}, bf16[768,256]{1,0:T(8,128)(2,1)S(1)}, u32[]{:S(2)}, u32[]{:S(2)}) collective-permute-start(bf16[768,256]{1,0:T(8,128)(2,1)S(1)} %constant_dynamic-slice_fusion.5), channel_id=1, source_target_pairs={{0,8},{4,12},{8,0},{12,4},{16,24},{20,28},{24,16},{28,20},{1,9},{5... | collective-permute-start | bytes 1179656 | tf_op jit(solution)/shard_map/ppermute | solution.py:59
  187.3 31.0 %collective-permute-start.22 = (bf16[394,1024]{1,0:T(8,128)(2,1)S(1)}, bf16[394,1024]{1,0:T(8,128)(2,1)S(1)}, u32[]{:S(2)}, u32[]{:S(2)}) collective-permute-start(bf16[394,1024]{1,0:T(8,128)(2,1)S(1)} %copy-done.22), channel_id=1, source_target_pairs={{0,1},{1,0},{2,3},{3,2},{4,5},{5,4},{6,7},{7,6},{8,9},{9,8},{10,11... | collective-permute-start | bytes 2420744 | tf_op jit(solution)/shard_map/ppermute | solution.py:59
  190.4 15.0 %collective-permute-start.15 = (bf16[394,256]{1,0:T(8,128)(2,1)S(1)}, bf16[394,256]{1,0:T(8,128)(2,1)S(1)}, u32[]{:S(2)}, u32[]{:S(2)}) collective-permute-start(bf16[394,256]{1,0:T(8,128)(2,1)S(1)} %shard_map.277.refs_0_), channel_id=1, source_target_pairs={{0,1},{1,0},{2,3},{3,2},{4,5},{5,4},{6,7},{7,6},{8,9},{9,8},{10,11... | collective-permute-start | bytes 605192 | tf_op jit(solution)/shard_map/ppermute | solution.py:59
  191.3 14.9 %collective-permute-start.17 = (bf16[394,256]{1,0:T(8,128)(2,1)S(1)}, bf16[394,256]{1,0:T(8,128)(2,1)S(1)}, u32[]{:S(2)}, u32[]{:S(2)}) collective-permute-start(bf16[394,256]{1,0:T(8,128)(2,1)S(1)} %collective-permute-done.16.refs_2_), channel_id=1, source_target_pairs={{0,1},{1,0},{2,3},{3,2},{4,5},{5,4},{6,7},{7,6},{8,9},{9,8},{10,11... | collective-permute-start | bytes 605192 | tf_op jit(solution)/shard_map/ppermute | solution.py:59
  199.6 9.2 %collective-permute-start.28 = (bf16[384,256]{1,0:T(8,128)(2,1)S(1)}, bf16[384,256]{1,0:T(8,128)(2,1)S(1)}, u32[]{:S(2)}, u32[]{:S(2)}) collective-permute-start(bf16[384,256]{1,0:T(8,128)(2,1)S(1)} %constant_dynamic-slice_fusion.7), channel_id=1, source_target_pairs={{0,8},{4,12},{8,0},{12,4},{16,24},{20,28},{24,16},{28,20},{1,9},{5... | collective-permute-start | bytes 589832 | tf_op jit(solution)/shard_map/ppermute | solution.py:59
  208.7 8.0 %collective-permute-start.43 = (bf16[64,1024]{1,0:T(8,128)(2,1)S(1)}, bf16[64,1024]{1,0:T(8,128)(2,1)S(1)}, u32[]{:S(2)}, u32[]{:S(2)}) collective-permute-start(bf16[64,1024]{1,0:T(8,128)(2,1)S(1)} %maximum_select_fusion.12), channel_id=1, source_target_pairs={{0,8},{4,12},{8,0},{12,4},{16,24},{20,28},{24,16},{28,20},{1,9},{5... | collective-permute-start | bytes 393224 | tf_op jit(solution)/shard_map/ppermute | solution.py:59
  208.9 8.2 %collective-permute-start.29 = (bf16[192,256]{1,0:T(8,128)(2,1)S(1)}, bf16[192,256]{1,0:T(8,128)(2,1)S(1)}, u32[]{:S(2)}, u32[]{:S(2)}) collective-permute-start(bf16[192,256]{1,0:T(8,128)(2,1)S(1)} %constant_dynamic-slice_fusion.6), channel_id=1, source_target_pairs={{0,16},{4,20},{8,24},{12,28},{16,0},{20,4},{24,8},{28,12},{1,17},{... | collective-permute-start | bytes 294920 | tf_op jit(solution)/shard_map/ppermute | solution.py:59
  211.6 10.4 %collective-permute-start.35 = (bf16[192,256]{1,0:T(8,128)(2,1)S(1)}, bf16[192,256]{1,0:T(8,128)(2,1)S(1)}, u32[]{:S(2)}, u32[]{:S(2)}) collective-permute-start(bf16[192,256]{1,0:T(8,128)(2,1)S(1)} %constant_dynamic-slice_fusion.3), channel_id=1, source_target_pairs={{0,16},{4,20},{8,24},{12,28},{16,0},{20,4},{24,8},{28,12},{1,17},{... | collective-permute-start | bytes 294920 | tf_op jit(solution)/shard_map/ppermute | solution.py:59
  216.8 11.9 %collective-permute-start.44 = (bf16[128,1024]{1,0:T(8,128)(2,1)S(1)}, bf16[128,1024]{1,0:T(8,128)(2,1)S(1)}, u32[]{:S(2)}, u32[]{:S(2)}) collective-permute-start(bf16[128,1024]{1,0:T(8,128)(2,1)S(1)} %maximum_select_fusion.9), channel_id=1, source_target_pairs={{0,4},{4,0},{8,12},{12,8},{16,20},{20,16},{24,28},{28,24},{1,5},{5... | collective-permute-start | bytes 786440 | tf_op jit(solution)/shard_map/ppermute | solution.py:59
  218.6 18.2 %collective-permute-start.23 = (bf16[394,1024]{1,0:T(8,128)(2,1)S(1)}, bf16[394,1024]{1,0:T(8,128)(2,1)S(1)}, u32[]{:S(2)}, u32[]{:S(2)}) collective-permute-start(bf16[394,1024]{1,0:T(8,128)(2,1)S(1)} %add_convert_fusion.1), channel_id=1, source_target_pairs={{0,2},{1,3},{2,0},{3,1},{4,6},{5,7},{6,4},{7,5},{8,10},{9,11},{10,... | collective-permute-start | bytes 2420744 | tf_op jit(solution)/shard_map/ppermute | solution.py:59
  223.3 8.5 %collective-permute-start.31 = (bf16[384,256]{1,0:T(8,128)(2,1)S(1)}, bf16[384,256]{1,0:T(8,128)(2,1)S(1)}, u32[]{:S(2)}, u32[]{:S(2)}) collective-permute-start(bf16[384,256]{1,0:T(8,128)(2,1)S(1)} %maximum_select_fusion.10), channel_id=1, source_target_pairs={{0,8},{4,12},{8,0},{12,4},{16,24},{20,28},{24,16},{28,20},{1,9},{5... | collective-permute-start | bytes 589832 | tf_op jit(solution)/shard_map/ppermute | solution.py:59
  227.8 7.9 %collective-permute-start.37 = (bf16[384,256]{1,0:T(8,128)(2,1)S(1)}, bf16[384,256]{1,0:T(8,128)(2,1)S(1)}, u32[]{:S(2)}, u32[]{:S(2)}) collective-permute-start(bf16[384,256]{1,0:T(8,128)(2,1)S(1)} %maximum_select_fusion.11), channel_id=1, source_target_pairs={{0,4},{4,0},{8,12},{12,8},{16,20},{20,16},{24,28},{28,24},{1,5},{5... | collective-permute-start | bytes 589832 | tf_op jit(solution)/shard_map/ppermute | solution.py:59
  232.0 11.0 %collective-permute-start.32 = (bf16[768,256]{1,0:T(8,128)(2,1)S(1)}, bf16[768,256]{1,0:T(8,128)(2,1)S(1)}, u32[]{:S(2)}, u32[]{:S(2)}) collective-permute-start(bf16[768,256]{1,0:T(8,128)(2,1)S(1)} %maximum_select_fusion.7), channel_id=1, source_target_pairs={{0,4},{4,0},{8,12},{12,8},{16,20},{20,16},{24,28},{28,24},{1,5},{5... | collective-permute-start | bytes 1179656 | tf_op jit(solution)/shard_map/ppermute | solution.py:59
  235.8 10.4 %collective-permute-start.38 = (bf16[768,256]{1,0:T(8,128)(2,1)S(1)}, bf16[768,256]{1,0:T(8,128)(2,1)S(1)}, u32[]{:S(2)}, u32[]{:S(2)}) collective-permute-start(bf16[768,256]{1,0:T(8,128)(2,1)S(1)} %maximum_select_fusion.8), channel_id=1, source_target_pairs={{0,8},{4,12},{8,0},{12,4},{16,24},{20,28},{24,16},{28,20},{1,9},{5... | collective-permute-start | bytes 1179656 | tf_op jit(solution)/shard_map/ppermute | solution.py:59
  (47 other events, 340.3 us)
where the time goes:
time: 257 us; the launch traced here: 256 us
  waiting for transfers between devices  86 us (33%)
  Pallas kernels  67.7 us (26%)
  starting transfers between devices  63.1 us (25%)
  other arithmetic  14.5 us (6%)
  matrix products  13 us (5%)
  local copies, waits for them, and re-layouts  10.3 us (4%)
    ppermute x45, waiting for transfers between devices, swap(): return lax.ppermute(values, axis, [(i, i ^ bit) for i in range(count)])  78.5 us
    pallas_call x12, Pallas kernels, call(): pl.pallas_call(body, out_shape=outs, compiler_params=pltpu.CompilerParams...  67.7 us
    ppermute x45, starting transfers between devices, swap(): return lax.ppermute(values, axis, [(i, i ^ bit) for i in range(count)])  41.7 us
    dot_general x2, matrix products, dot(): lax.dot_general(left, right, (((left_dim,), (right_dim,)), ((), ())), pre...  13 us
    convert_element_type x9, other arithmetic, add(): return (left.astype(f32) + right.astype(f32)).astype(left.dtype)  9.5 us
    all_to_all x1, starting transfers between devices, on_device(): lax.all_to_all(out_sent.reshape(experts, capacity, piece), 'expert', 0, 0...  5.97 us
    all_to_all x1, starting transfers between devices, on_device(): lax.all_to_all(grad_send.reshape(experts, capacity, piece), 'expert', 0,...  5.97 us
    all_to_all x1, starting transfers between devices, on_device(): lax.all_to_all(send.reshape(experts, capacity, half), 'expert', 0, 0, til...  5.76 us
  transfers between devices with their start and end apart: 49, of which 25 were waited for; matrix products, arithmetic and copies ran while one was open for 13% of the time, Pallas kernels for 20%

commit v1 on v0

--- a/solution.py
+++ b/solution.py
@@ -12,6 +12,8 @@
 LANES = 128
 VMEM_LIMIT = 52 * 1024 * 1024
 EXTRA = 16
+MASKS = ((1, 2, 4), (2, 1, 5), (1, 3, 6))
+FLOPS_PER_US = 1.15e9
 
 epsilon = 1e-06
 f32 = jnp.float32
@@ -28,26 +30,34 @@
     )
 
 
-def call(body, outs, ins, flops, grid=None, in_specs=None, out_specs=None, scalars=0, scratch=()):
+def call(
+    body, outs, ins, us, grid=None, in_specs=None, out_specs=None, scalars=0, scratch=(), after=()
+):
     specs = {"scratch_shapes": list(scratch)}
     if grid is not None:
         specs["grid"] = grid
-        specs["in_specs"] = in_specs
         specs["out_specs"] = out_specs
     else:
-        specs["in_specs"] = [
+        in_specs = [
             pl.BlockSpec(memory_space=pltpu.SMEM if i < scalars else pltpu.VMEM)
             for i in range(len(ins))
         ]
         specs["out_specs"] = [pl.BlockSpec(memory_space=pltpu.VMEM) for _ in outs]
-    moved = sum(a.size * a.dtype.itemsize for a in list(ins) + list(outs))
+    specs["in_specs"] = in_specs + [pl.BlockSpec(memory_space=pl.ANY)] * len(after)
+    used = len(ins)
+
+    def run(*refs):
+        body(*refs[:used], *refs[used + len(after) :])
+
     return pl.pallas_call(
-        body,
+        run,
         out_shape=outs,
         compiler_params=pltpu.CompilerParams(vmem_limit_bytes=VMEM_LIMIT),
-        cost_estimate=pl.CostEstimate(flops=flops, bytes_accessed=moved, transcendentals=0),
+        cost_estimate=pl.CostEstimate(
+            flops=int(us * FLOPS_PER_US), bytes_accessed=0, transcendentals=0
+        ),
         **specs,
-    )(*ins)
+    )(*ins, *after)
 
 
 def sds(shape, dtype):
@@ -85,6 +95,18 @@
     return kept
 
 
+def scatter_sent(held, bits):
+    for bit in bits[1:-1]:
+        held = scatter_step(held, bit)
+    if len(bits) == 1:
+        return held
+    return {0: held[0], 1: swap(held[bits[-1]], "tensor", bits[-1])}
+
+
+def scatter_last(held, bits):
+    return held[0] if len(bits) == 1 else add(held[0], held[1])
+
+
 def butterfly(values, axis):
     for bit in bits_of(lax.axis_size(axis)):
         came = swap(values, axis, bit)
@@ -92,24 +114,52 @@
     return values
 
 
-def sum_experts(values, order):
+def chain_of(count, masks):
+    masks = [m for m in masks if m < count]
+    masks += bits_of(count)[len(masks) :]
+    parity = lambda value: bin(value).count("1") % 2
+    sides = []
+    for step in range(len(masks)):
+        wanted = [int(step == other) for other in range(len(masks))]
+        fits = [d for d in range(count) if [parity(d & m) for m in masks] == wanted]
+        sides.append(fits[0])
+    return list(zip(masks, sides))
+
+
+def side_of(bits):
     index = lax.axis_index("expert")
-    for bit in order:
+    total = sum(((index >> b) & 1 for b in range(bits.bit_length()) if (bits >> b) & 1))
+    return (total & 1).astype(jnp.int32)
+
+
+def reduce_experts(values, chain):
+    sums = [values]
+    for mask, bits in chain[1:]:
         half = values.shape[0] // 2
-        side = (index & bit) // bit
+        side = side_of(bits)
         keep = lax.dynamic_slice_in_dim(values, side * half, half, 0)
         send = lax.dynamic_slice_in_dim(values, (1 - side) * half, half, 0)
-        came = swap(send, "expert", bit)
-        values = (keep.astype(f32) + came.astype(f32)).astype(bf16)
-    for bit in reversed(order):
-        side = (index & bit) // bit
-        came = swap(values, "expert", bit)
+        values = add(keep, swap(send, "expert", mask))
+        sums.append(values)
+    return sums
+
+
+def spread_experts(values, chain, rider=None):
+    count = 0 if rider is None else rider.shape[0]
+    for mask, bits in reversed(chain):
+        rows = values.shape[0]
+        sent = values if rider is None else jnp.concatenate([values, rider], 0)
+        came = swap(sent, "expert", mask)
+        if rider is not None:
+            rider = add(rider, came[rows : rows + count])
+        came = came[:rows]
+        if (mask, bits) == chain[0]:
+            return values, came, rider
         values = jnp.where(
-            side == 0,
+            side_of(bits) == 0,
             jnp.concatenate([values, came], 0),
             jnp.concatenate([came, values], 0),
         )
-    return values
 
 
 def norm_parts(values):
@@ -187,27 +237,13 @@
     return table.astype(bf16)
 
 
-def route_kernel(
-    idx_ref,
-    routes_ref,
-    flipped_ref,
-    dout_ref,
-    plain_ref,
-    padded_ref,
-    dispatch_ref,
-    send_ref,
-    *,
-    experts,
-    capacity,
-):
-    rows = plain_ref.shape[0]
+def route_kernel(idx_ref, flipped_ref, dout_ref, dispatch_ref, send_ref, *, experts, capacity):
+    rows = dispatch_ref.shape[1]
     width = send_ref.shape[1]
-    top = routes_ref.shape[1]
     first = lax.broadcasted_iota(jnp.int32, (rows, rows), 0)
     second = lax.broadcasted_iota(jnp.int32, (rows, rows), 1)
-
     ids = lax.broadcasted_iota(jnp.int32, (experts, rows), 0)
-    named = [flipped_ref[k : k + 1, :] == ids for k in range(top)]
+    named = [flipped_ref[k : k + 1, :] == ids for k in range(flipped_ref.shape[0])]
     tally = sum(m.astype(f32) for m in named).astype(bf16)
     earlier = dot(tally, (first < second).astype(f32).astype(bf16), 1, 0)
     numbers = slot_numbers(named, earlier, ids, 0, capacity)
@@ -215,8 +251,13 @@
     start = pl.multiple_of(idx_ref[0] * width, LANES)
     send_ref[...] = dot(dispatch_ref[...], dout_ref[:, pl.ds(start, width)], 1, 0).astype(bf16)
 
+
+def place_kernel(routes_ref, plain_ref, padded_ref, *, experts, capacity):
+    rows = plain_ref.shape[0]
+    first = lax.broadcasted_iota(jnp.int32, (rows, rows), 0)
+    second = lax.broadcasted_iota(jnp.int32, (rows, rows), 1)
     ids = lax.broadcasted_iota(jnp.int32, (rows, experts), 1)
-    named = [routes_ref[:, k : k + 1] == ids for k in range(top)]
+    named = [routes_ref[:, k : k + 1] == ids for k in range(routes_ref.shape[1])]
     tally = sum(m.astype(f32) for m in named).astype(bf16)
     earlier = dot((second < first).astype(f32).astype(bf16), tally, 1, 0)
     for ref, stride in ((plain_ref, capacity), (padded_ref, capacity + EXTRA)):
@@ -246,13 +287,16 @@
 
 
 def early_kernel(*refs, blocks):
-    idx_ref, piece_refs, w_ref = refs[0], refs[1 : 1 + blocks], refs[1 + blocks]
-    rows_ref, unscaled_ref = refs[2 + blocks :]
+    idx_ref, piece_refs = refs[0], refs[1 : 1 + blocks]
+    w_ref, bias_ref, rows_ref, unscaled_ref, bias_dot_ref = refs[1 + blocks :]
     piece = piece_refs[0].shape[-1]
     for key, piece_ref in enumerate(piece_refs):
         cols = pl.ds(pl.multiple_of((idx_ref[0] ^ key) * piece, LANES), piece)
         rows_ref[:, cols] = piece_ref[...]
     unscaled_ref[...] = dot(rows_ref[...], w_ref[...], 1, 1)
+    bias_dot_ref[...] = jnp.sum(
+        rows_ref[...].astype(f32) * bias_ref[...], axis=1, keepdims=True
+    ) * (1.0 / blocks)
 
 
 def expert_kernel(
@@ -261,9 +305,9 @@
     other_ref,
     grad_ref,
     unscaled_ref,
+    bias_dot_ref,
     w_in_ref,
     b_in_ref,
-    b_back_ref,
     router_ref,
     *outs,
     blocks,
@@ -300,9 +344,7 @@
     grad_pre = (gate * unscaled * (cdf + pre_act * density)).astype(bf16)
     pre_ref[...] = grad_pre
     grad_rows = grad_ref[...].astype(f32)
-    gate_grads = jnp.sum(act.astype(f32) * unscaled, axis=1, keepdims=True) + jnp.sum(
-        grad_rows * b_back_ref[...], axis=1, keepdims=True
-    ) * (1.0 / blocks)
+    gate_grads = jnp.sum(act.astype(f32) * unscaled, axis=1, keepdims=True) + bias_dot_ref[...]
     gate_grads = jnp.broadcast_to(gate_grads, (gate_grads.shape[0], LANES)).T
     grad_y = (gate * grad_rows).astype(bf16)
     grady_ref[...] = grad_y
@@ -312,8 +354,9 @@
         dbin_ref[...] = jnp.zeros_like(dbin_ref)
         dbback_ref[...] = jnp.zeros_like(dbback_ref)
 
-    dbin_ref[...] += jnp.sum(grad_pre.astype(f32), axis=0, keepdims=True)
-    dbback_ref[...] += jnp.sum(grad_y.astype(f32), axis=0, keepdims=True)
+    ones = jnp.ones((8, grad_pre.shape[0]), bf16)
+    dbin_ref[...] += dot(ones, grad_pre, 1, 0)[0:1, :]
+    dbback_ref[...] += dot(ones, grad_y, 1, 0)[0:1, :]
     for key, piece_ref in enumerate(piece_refs):
         start = pl.multiple_of((tensor_id ^ key) * piece, LANES)
         rows = dot(grad_pre, w_in_ref[pl.ds(start, piece), :], 1, 1)
@@ -339,6 +382,32 @@
         piece_ref[...] = (gate_ref[...] * rows).astype(bf16)
 
 
+def outer_kernel(left_ref, right_ref, out_ref):
+    out_ref[...] = dot(left_ref[...], right_ref[...], 0, 0)
+
+
+def outer_halves_kernel(idx_ref, own_ref, other_ref, right_ref, out_ref):
+    mine = (idx_ref[0] & 1) == pl.program_id(0) // 2
+
+    @pl.when(mine)
+    def _():
+        out_ref[...] = dot(own_ref[...], right_ref[...], 0, 0)
+
+    @pl.when(jnp.logical_not(mine))
+    def _():
+        out_ref[...] = dot(other_ref[...], right_ref[...], 0, 0)
+
+
+def add_pairs_kernel(*refs):
+    count = len(refs) // 3
+    for left_ref, right_ref, out_ref in zip(refs[:count], refs[count : 2 * count], refs[2 * count :]):
+        out_ref[...] = (left_ref[...].astype(f32) + right_ref[...].astype(f32)).astype(bf16)
+
+
+def add_kernel(left_ref, right_ref, out_ref):
+    out_ref[...] = (left_ref[...].astype(f32) + right_ref[...].astype(f32)).astype(bf16)
+
+
 def combine_kernel(place_ref, home_ref, out_ref):
     out_ref[...] = dot(place_ref[...], home_ref[...], 1, 0).astype(bf16)
 
@@ -370,7 +439,8 @@
     w_ref,
     mix_ref,
     grad_ref,
-    dw_ref,
+    dw_keep_ref,
+    dw_send_ref,
     gmix_ref,
     small_ref,
     disp_ref,
@@ -399,7 +469,18 @@
     grad_ref[...] = grad_resid
     branch = grad_resid.astype(bf16)
     gmix_ref[...] = dot(branch, w_ref[...], 1, 1).astype(bf16)
-    dw_ref[...] = dot(mix_ref[...], branch, 0, 0).astype(bf16)
+    local = dw_keep_ref.shape[1]
+    part = local // 2
+    for ref, side in ((dw_keep_ref, idx_ref[4]), (dw_send_ref, 1 - idx_ref[4])):
+        if part % LANES == 0:
+            left = mix_ref[:, pl.ds(pl.multiple_of(side * part, LANES), part)]
+        else:
+            left = jnp.where(side == 0, mix_ref[:, 0:part], mix_ref[:, part:])
+        product = dot(left, branch, 0, 0).astype(bf16)
+        for block in range(product.shape[1] // local):
+            ref[block * part : (block + 1) * part, :] = product[
+                :, block * local : (block + 1) * local
+            ]
     small_ref[0:experts, :] = dot(grad_logits, second_ref[...], 0, 0)
     small_ref[experts : experts + 1, :] = jnp.sum(second_grad * normal, axis=0, keepdims=True)
     small_ref[experts + 1 : experts + 2, :] = jnp.sum(second_grad, axis=0, keepdims=True)
@@ -407,7 +488,25 @@
 
 
 def attend_back_kernel(
-    q_ref, k_ref, v_ref, gmix_ref, norm_ref, w_ref, dw_ref, db_ref, part_ref, gq_ref, gk_ref, gv_ref
+    idx_ref,
+    q_ref,
+    k_ref,
+    v_ref,
+    gmix_ref,
+    norm_ref,
+    w_ref,
+    tok_ref,
+    first_keep_ref,
+    first_send_ref,
+    second_keep_ref,
+    second_send_ref,
+    db_ref,
+    part_keep_ref,
+    part_send_ref,
+    gq_ref,
+    gk_ref,
+    gv_ref,
+    part_ref,
 ):
     rows = q_ref.shape[0]
     inside = same_image(rows)
@@ -433,24 +532,88 @@
         gq_ref[:, cols] = (grad_q * scale).astype(bf16)
         gk_ref[:, cols] = (grad_k * scale).astype(bf16)
         gv_ref[:, cols] = grad_v.astype(bf16)
-    normed = norm_ref[...]
+    quarter = norm_ref.shape[1] // 4
     total = None
     for part, ref in enumerate((gq_ref, gk_ref, gv_ref)):
         grads = ref[...]
-        dw_ref[part] = dot(normed, grads, 0, 0).astype(bf16)
+        here = slice(part * quarter, (part + 1) * quarter)
+        for side, base, keep_ref, send_ref in (
+            (idx_ref[2], 0, first_keep_ref, first_send_ref),
+            (idx_ref[3], 2, second_keep_ref, second_send_ref),
+        ):
+            for target, block in ((keep_ref, base + side), (send_ref, base + 1 - side)):
+                cols = pl.ds(pl.multiple_of(block * quarter, LANES), quarter)
+                target[here, :] = dot(norm_ref[:, cols], grads, 0, 0).astype(bf16)
         term = dot(grads, w_ref[part], 1, 1)
         total = term if total is None else total + term
-    part_ref[...] = total.astype(bf16)
+    normal, _ = norm_parts(tok_ref[...].astype(f32))
+    part_ref[0:rows, :] = total.astype(bf16)
+    part_ref[rows:, :] = jnp.zeros((part_ref.shape[0] - rows, total.shape[1]), bf16)
+    part_ref[rows : rows + 1, :] = jnp.sum(total * normal, axis=0, keepdims=True).astype(bf16)
+    part_ref[rows + 1 : rows + 2, :] = jnp.sum(total, axis=0, keepdims=True).astype(bf16)
+    half = part_keep_ref.shape[1]
+    side = idx_ref[0] & 1
+    part_keep_ref[...] = part_ref[:, pl.ds(pl.multiple_of(side * half, LANES), half)]
+    part_send_ref[...] = part_ref[:, pl.ds(pl.multiple_of((1 - side) * half, LANES), half)]
     db_ref[0:1, :] = jnp.sum(gq_ref[...].astype(f32), axis=0, keepdims=True)
     db_ref[1:2, :] = jnp.sum(gv_ref[...].astype(f32), axis=0, keepdims=True)
 
 
-def first_kernel(tok_ref, gain_ref, grad_ref, resid_ref, out_ref, small_ref):
+def pack_kernel(idx_ref, mine_ref, theirs_ref, small_ref, bias_ref, out_ref, line_ref):
+    lines, width = line_ref.shape
+    local = out_ref.shape[1]
+    half = width // 2
+    side = idx_ref[0] & 1
+    count = small_ref.shape[0]
+    line_ref[...] = jnp.zeros_like(line_ref)
+    line_ref[0:count, :] = small_ref[...]
+    mine = pl.ds(pl.multiple_of(side * half, LANES), half)
+    line_ref[count : count + 2, mine] = mine_ref[0:2, :].astype(f32)
+    theirs = pl.ds(pl.multiple_of((1 - side) * half, LANES), half)
+    line_ref[count : count + 2, theirs] = theirs_ref[0:2, :].astype(f32)
+    line_ref[count + 2 : count + 4, 0:local] = bias_ref[...]
+    for block in range(width // local):
+        out_ref[block * lines : (block + 1) * lines, :] = line_ref[
+            :, block * local : (block + 1) * local
+        ].astype(bf16)
+
+
+def first_kernel(idx_ref, tok_ref, gain_ref, mine_ref, theirs_ref, resid_ref, out_ref, grad_ref):
+    rows, width = tok_ref.shape
+    half = width // 2
+    side = idx_ref[0] & 1
+    grad_ref[:, pl.ds(pl.multiple_of(side * half, LANES), half)] = mine_ref[...]
+    grad_ref[:, pl.ds(pl.multiple_of((1 - side) * half, LANES), half)] = theirs_ref[...]
     normal, rstd = norm_parts(tok_ref[...].astype(f32))
-    grad = grad_ref[...].astype(f32)
+    grad = grad_ref[0:rows, :].astype(f32)
     out_ref[...] = resid_ref[...] + norm_back(grad, normal, rstd, gain_ref[...])
-    small_ref[0:1, :] = jnp.sum(grad * normal, axis=0, keepdims=True)
-    small_ref[1:2, :] = jnp.sum(grad, axis=0, keepdims=True)
+
+
+def assemble_kernel(idx_ref, *refs):
+    out_ref = refs[-1]
+    quarter = out_ref.shape[1] // 4
+    for chunk in range(2):
+        low = idx_ref[2 + chunk] == 0
+        for part in range(3):
+            rows = slice(part * quarter, (part + 1) * quarter)
+            mine = refs[2 * chunk][rows, :].astype(f32)
+            came = refs[2 * chunk + 1][rows, :].astype(f32)
+            base = 2 * chunk * quarter
+            out_ref[part, base : base + quarter, :] = jnp.where(low, mine, came)
+            out_ref[part, base + quarter : base + 2 * quarter, :] = jnp.where(low, came, mine)
+
+
+def assemble_out_kernel(idx_ref, mine_ref, came_ref, out_ref):
+    local = out_ref.shape[0]
+    part = local // 2
+    low = idx_ref[4] == 0
+    for block in range(out_ref.shape[1] // local):
+        rows = slice(block * part, (block + 1) * part)
+        cols = slice(block * local, (block + 1) * local)
+        mine = mine_ref[rows, :].astype(f32)
+        came = came_ref[rows, :].astype(f32)
+        out_ref[0:part, cols] = jnp.where(low, mine, came)
+        out_ref[part:, cols] = jnp.where(low, came, mine)
 
 
 def on_device(
@@ -485,20 +648,16 @@
     row = lambda vec: vec.reshape(1, -1)
     tensor_id = lax.axis_index("tensor").astype(jnp.int32)
     expert_id = lax.axis_index("expert").astype(jnp.int32)
-    ids = jnp.stack([tensor_id, expert_id])
+    chains = [chain_of(groups, masks) for masks in MASKS]
+    ids = jnp.stack([tensor_id, expert_id] + [side_of(chain[0][1]) for chain in chains])
     stride = capacity + EXTRA
     row_bits = bits_of(blocks)
 
-    plain, padded, dispatch_place, grad_send = call(
+    dispatch_place, grad_send = call(
         functools.partial(route_kernel, experts=experts, capacity=capacity),
-        [
-            sds((rows, slots), bf16),
-            sds((rows, experts * stride), bf16),
-            sds((slots, rows), bf16),
-            sds((slots, piece), bf16),
-        ],
-        [ids, routes, routes.T, d_out],
-        2 * rows * slots * piece,
+        [sds((slots, rows), bf16), sds((slots, piece), bf16)],
+        [ids, routes.T, d_out],
+        2.5,
         scalars=1,
     )
     w_out_all = gather_tensor(w_out, diagonal=True)
@@ -511,7 +670,7 @@
         attend_kernel,
         [sds((rows, width), bf16)] + [sds((rows, local), bf16)] * 4,
         [tokens_in, row(gain_attn), row(shift_attn), w_qkv, b_qv],
-        6 * rows * width * local,
+        4.7,
     )
     mixed_all = gather_tensor(mixed)
     residual, second_low, router_probs, send = call(
@@ -533,9 +692,17 @@
             w_router,
             dispatch_place,
         ],
-        2 * rows * width * width + 2 * rows * slots * half,
+        5.5,
         scalars=1,
         scratch=[pltpu.VMEM((blocks, rows, width), f32)],
+    )
+
+    plain, padded = call(
+        functools.partial(place_kernel, experts=experts, capacity=capacity),
+        [sds((rows, slots), bf16), sds((rows, experts * stride), bf16)],
+        [routes],
+        2.5,
+        after=[send],
     )
 
     own = lax.all_to_all(
@@ -552,14 +719,14 @@
     def by_row(cols):
         return pl.BlockSpec((tile, cols), lambda i: (i, 0))
 
-    grad_rows, unscaled = call(
+    grad_rows, unscaled, bias_dot = call(
         functools.partial(early_kernel, blocks=blocks),
-        [sds((slots, width), bf16), sds((slots, hidden), f32)],
-        [ids, *gather_tensor(grad_came, diagonal=True), w_back[0]],
-        2 * slots * width * hidden,
+        [sds((slots, width), bf16), sds((slots, hidden), f32), sds((slots, 1), f32)],
+        [ids, *gather_tensor(grad_came, diagonal=True), w_back[0], b_back],
+        7.0,
         grid=(steps,),
-        in_specs=[smem] + [by_row(piece)] * blocks + [whole((hidden, width))],
-        out_specs=[by_row(width), by_row(hidden)],
+        in_specs=[smem] + [by_row(piece)] * blocks + [whole((hidden, width)), whole((1, width))],
+        out_specs=[by_row(width), by_row(hidden), by_row(1)],
     )
     own, grad_rows, unscaled = lax.optimization_barrier((own, grad_rows, unscaled))
     other = swap(own, "tensor", 1)
@@ -575,8 +742,8 @@
             sds((1, hidden), f32),
             sds((1, width), f32),
         ],
-        [ids, own, other, grad_rows, unscaled, w_in[0], b_in, b_back, w_router],
-        4 * slots * width * hidden,
+        [ids, own, other, grad_rows, unscaled, bias_dot, w_in[0], b_in, w_router],
+        17.0,
         grid=(steps,),
         in_specs=[
             smem,
@@ -584,9 +751,9 @@
             by_row(half),
             by_row(width),
             by_row(hidden),
+            by_row(1),
             whole((width, hidden)),
             whole((1, hidden)),
-            whole((1, width)),
             whole((width, experts)),
         ],
         out_specs=[pl.BlockSpec((count, stride, piece), lambda i: (i, 0, 0))] * blocks
@@ -609,34 +776,61 @@
         back_kernel,
         [sds((slots, piece), bf16)] * blocks,
         [ids, activated, gate, w_back[0], b_back],
-        2 * slots * width * hidden,
+        6.5,
         grid=(steps,),
         in_specs=[smem, by_row(hidden), by_row(1), whole((hidden, width)), whole((1, width))],
         out_specs=[by_row(piece)] * blocks,
     )
-    out_held = scatter_step(dict(enumerate(out_pieces)), row_bits[0])
+    kept = [key for key in range(blocks) if not key & 1]
+    out_came = [swap(out_pieces[key | 1], "tensor", 1) for key in kept]
 
     for bit in row_bits[1:]:
         held = scatter_step(held, bit)
     home = lax.all_to_all(held[0], "expert", 0, 0, tiled=True)
-    for bit in row_bits[1:]:
-        out_held = scatter_step(out_held, bit)
-
-    d_w_back = dot(activated, grad_y, 0, 0)[None]
-    side = tensor_id & 1
-    rows_in = jnp.where(
-        side == 0,
-        jnp.concatenate([own, other], axis=1),
-        jnp.concatenate([other, own], axis=1),
-    )
-    d_w_in = dot(rows_in, grad_pre, 0, 0)[None]
-    home, d_w_back, d_w_in = lax.optimization_barrier((home, d_w_back, d_w_in))
-    out_sent = out_held[0]
+    out_sums = call(
+        add_pairs_kernel,
+        [sds((slots, piece), bf16)] * len(kept),
+        [out_pieces[key] for key in kept] + out_came,
+        2.0,
+        grid=(steps,),
+        in_specs=[by_row(piece)] * (2 * len(kept)),
+        out_specs=[by_row(piece)] * len(kept),
+        after=[held[0]],
+    )
+    out_held = scatter_sent(dict(zip(kept, out_sums)), row_bits)
+
+    cut = min(256, hidden)
+    d_w_back = call(
+        outer_kernel,
+        [sds((hidden, width), f32)],
+        [activated, grad_y],
+        7.0,
+        grid=(hidden // cut,),
+        in_specs=[pl.BlockSpec((slots, cut), lambda i: (0, i)), whole((slots, width))],
+        out_specs=[pl.BlockSpec((cut, width), lambda i: (i, 0))],
+        after=out_sums,
+    )[0][None]
+    d_w_in = call(
+        outer_halves_kernel,
+        [sds((width, hidden), f32)],
+        [ids, own, other, grad_pre],
+        7.0,
+        grid=(4,),
+        in_specs=[
+            smem,
+            pl.BlockSpec((slots, half // 2), lambda i: (0, i % 2)),
+            pl.BlockSpec((slots, half // 2), lambda i: (0, i % 2)),
+            whole((slots, hidden)),
+        ],
+        out_specs=[pl.BlockSpec((half // 2, hidden), lambda i: (i, 0))],
+        after=out_sums,
+    )[0][None]
     dispatch = call(
         combine_kernel,
         [sds((rows, piece), bf16)],
         [padded, home.reshape(experts * stride, piece)],
-        2 * rows * slots * piece,
+        1.8,
+        after=[d_w_back, d_w_in],
     )[0]
     dispatch_all = gather_tensor(dispatch)
     gate_lines = -(-capacity // piece)
@@ -644,25 +838,27 @@
     gate_grads = jnp.pad(gate_grads[:, :capacity].astype(f32), ((0, 0), (0, EXTRA)))
     gate_grads = gate_grads.reshape(1, experts * stride)
 
+    out_sent = scatter_last(out_held, row_bits)
+
     out_home = lax.all_to_all(
         out_sent.reshape(experts, capacity, piece), "expert", 0, 0, tiled=True
     ).reshape(slots, piece)
     mixture = call(
-        combine_kernel, [sds((rows, piece), bf16)], [plain, out_home], 2 * rows * slots * piece
-    )[0]
+        combine_kernel, [sds((rows, piece), bf16)], [plain, out_home], 1.8    )[0]
     activations = call(
         finish_kernel,
         [sds((rows, width), bf16)],
         [ids, residual, *gather_tensor(mixture)],
-        rows * width,
+        2.6,
         scalars=1,
     )[0]
 
-    grad_resid, d_w_out, grad_mixed, small = call(
+    grad_resid, out_keep, out_give, grad_mixed, small = call(
         functools.partial(residual_kernel, blocks=blocks, capacity=capacity),
         [
             sds((rows, width), f32),
-            sds((local, width), bf16),
+            sds((half, local), bf16),
+            sds((half, local), bf16),
             sds((rows, local), bf16),
             sds((experts + 3, width), f32),
         ],
@@ -680,53 +876,98 @@
             w_out,
             mixed,
         ],
-        4 * rows * width * local,
+        6.0,
         scalars=1,
         scratch=[pltpu.VMEM((rows, width), bf16)],
     )
-    d_w_qkv, d_b_qv, partial_grad, _, _, _ = call(
+    out_came = swap(out_give, "expert", chains[2][0][0])
+    quarter = width // 4
+    padded_rows = -(-(rows + 2) // EXTRA) * EXTRA
+    outs = call(
         attend_back_kernel,
-        [
-            sds((3, width, local), bf16),
+        [sds((3 * quarter, local), bf16)] * 4
+        + [
             sds((2, local), f32),
-            sds((rows, width), bf16),
+            sds((padded_rows, half), bf16),
+            sds((padded_rows, half), bf16),
             sds((rows, local), bf16),
             sds((rows, local), bf16),
             sds((rows, local), bf16),
         ],
-        [queries, keys, value_rows, grad_mixed, normed, w_qkv],
-        12 * rows * width * local,
-    )
-    order = bits_of(groups)
-    d_w_out = sum_experts(d_w_out, order)
-    cut = 3 * width // 2
-    d_w_qkv = d_w_qkv.reshape(3 * width, local)
-    d_w_qkv = jnp.concatenate(
-        [
-            sum_experts(d_w_qkv[:cut], order),
-            sum_experts(d_w_qkv[cut:], order[1:2] + order[:1] + order[2:]),
-        ],
-        axis=0,
-    ).reshape(3, width, local)
-
-    grad_normed = butterfly(partial_grad, "tensor")
-    d_tokens, first_small = call(
+        [ids, queries, keys, value_rows, grad_mixed, normed, w_qkv, tokens],
+        8.0,
+        scalars=1,
+        scratch=[pltpu.VMEM((padded_rows, width), bf16)],
+    )
+    first_came = swap(outs[1], "expert", chains[0][0][0])
+    second_came = swap(outs[3], "expert", chains[1][0][0])
+    d_b_qv, part_keep, part_send = outs[4:7]
+
+    mine = add(part_keep, swap(part_send, "tensor", 1))
+    part_sum = mine
+    for bit in row_bits[1:]:
+        mine = add(mine, swap(mine, "tensor", bit))
+    theirs = swap(mine, "tensor", 1)
+    theirs = swap(mine, "tensor", 1)
+    lines = -(-(experts + 7) // EXTRA) * EXTRA
+    packed = call(
+        pack_kernel,
+        [sds((lines * (width // local), local), bf16)],
+        [ids, mine[rows:], theirs[rows:], small, d_b_qv],
+        1.0,
+        scalars=1,
+        scratch=[pltpu.VMEM((lines, width), f32)],
+    )[0]
+    first_sum = call(
+        add_kernel, [sds(first_came.shape, bf16)], [outs[0], first_came], 0.8, after=[part_sum]
+    )[0]
+    first_sums = reduce_experts(first_sum, chains[0])
+    second_sums = reduce_experts(add(outs[2], second_came), chains[1])
+    out_sum = call(
+        add_kernel,
+        [sds(out_keep.shape, bf16)],
+        [out_keep, out_came],
+        0.8,
+        after=[second_came],
+    )[0]
+    out_sums = reduce_experts(out_sum, chains[2])
+    *first, packed = spread_experts(first_sums[-1], chains[0], packed)
+    second = spread_experts(second_sums[-1], chains[1])[:2]
+    d_w_out = spread_experts(out_sums[-1], chains[2])[:2]
+    packed = packed.reshape(width // local, lines, local).transpose(1, 0, 2)
+    packed = packed.reshape(lines, width).astype(f32)
+
+    d_tokens = call(
         first_kernel,
-        [sds((rows, width), f32), sds((2, width), f32)],
-        [tokens, row(gain_attn), grad_normed, grad_resid],
-        rows * width,
-    )
-    bias_row = jnp.pad(d_b_qv, ((0, 0), (0, width - local)))
-    packed = jnp.concatenate([small, first_small, bias_row], axis=0).astype(bf16)
-    packed = butterfly(packed, "expert").astype(f32)
+        [sds((rows, width), f32)],
+        [ids, tokens, row(gain_attn), mine, theirs, grad_resid],
+        3.9,
+        scalars=1,
+        scratch=[pltpu.VMEM((padded_rows, width), bf16)],
+    )[0]
+    d_w_qkv = call(
+        assemble_kernel,
+        [sds((3, width, local), f32)],
+        [ids, *first, *second],
+        2.0,
+        scalars=1,
+        after=[d_tokens],
+    )[0]
+    d_w_out = call(
+        assemble_out_kernel,
+        [sds((local, width), f32)],
+        [ids, *d_w_out],
+        1.0,
+        scalars=1,
+    )[0]
     return (
         activations,
         d_tokens,
         packed[experts + 3],
         packed[experts + 4],
-        d_w_qkv.astype(f32),
+        d_w_qkv,
         packed[experts + 5 : experts + 7, :local],
-        d_w_out.astype(f32),
+        d_w_out,
         packed[experts + 2],
         packed[experts],
         packed[experts + 1],

time: 257 us -> 253 us (0.984)
  Pallas kernels: 67.7 us -> 91.1 us
  matrix products: 13 us -> 0 us
  waiting for transfers between devices: 86 us -> 75.1 us
  other arithmetic: 14.5 us -> 8.77 us
  local copies, waits for them, and re-layouts: 10.3 us -> 13.5 us
    pallas_call x12 -> x21, Pallas kernels: 67.7 us -> 91.1 us  [call(): pl.pallas_call(run, out_shape=outs, compiler_params=pltpu.CompilerParams(...]
    dot_general x2 -> x0, matrix products: 13 us -> none  [dot(): lax.dot_general(left, right, (((left_dim,), (right_dim,)), ((), ())), pre...]
    ppermute x45 -> x43, waiting for transfers between devices: 78.5 us -> 70.8 us  [swap(): return lax.ppermute(values, axis, [(i, i ^ bit) for i in range(count)])]
    unnamed x63 -> x85, local copies, waits for them, and re-layouts: 4.51 us -> 11.4 us
    convert_element_type x12 -> x0, other arithmetic: 3.58 us -> none  [the longest x1 1.93 us: on_device(): d_w_qkv.astype(f32)]
    convert_element_type x9 -> x16, other arithmetic: 9.5 us -> 8.12 us  [add(): return (left.astype(f32) + right.astype(f32)).astype(left.dtype)]
    ppermute x45 -> x43, starting transfers between devices: 41.7 us -> 40.8 us  [swap(): return lax.ppermute(values, axis, [(i, i ^ bit) for i in range(count)])]
  transfers between devices with their start and end apart: 49 -> 47, of which waited for: 25 -> 24; matrix products, arithmetic and copies ran while one was open for 13% -> 4% of each run, Pallas kernels for 20% -> 29%
where the time goes in v1:
time: 253 us; the launch traced here: 252 us
  Pallas kernels  91.1 us (36%)
  waiting for transfers between devices  75.1 us (30%)
  starting transfers between devices  62.4 us (25%)
  local copies, waits for them, and re-layouts  13.5 us (5%)
  other arithmetic  8.77 us (3%)
    pallas_call x21, Pallas kernels, call(): pl.pallas_call(run, out_shape=outs, compiler_params=pltpu.CompilerParams(...  91.1 us
    ppermute x43, waiting for transfers between devices, swap(): return lax.ppermute(values, axis, [(i, i ^ bit) for i in range(count)])  70.8 us
    ppermute x43, starting transfers between devices, swap(): return lax.ppermute(values, axis, [(i, i ^ bit) for i in range(count)])  40.8 us
    unnamed x85, local copies, waits for them, and re-layouts  11.4 us
    convert_element_type x16, other arithmetic, add(): return (left.astype(f32) + right.astype(f32)).astype(left.dtype)  8.12 us
    all_to_all x1, starting transfers between devices, on_device(): lax.all_to_all(send.reshape(experts, capacity, half), 'expert', 0, 0, til...  6.18 us
    all_to_all x1, starting transfers between devices, on_device(): lax.all_to_all(out_sent.reshape(experts, capacity, piece), 'expert', 0, 0...  5.99 us
    all_to_all x1, starting transfers between devices, on_device(): lax.all_to_all(grad_send.reshape(experts, capacity, piece), 'expert', 0,...  5.83 us
  transfers between devices with their start and end apart: 47, of which 24 were waited for; matrix products, arithmetic and copies ran while one was open for 4% of the time, Pallas kernels for 29%

profile of v1, /device:TPU:0, one launch (start us, length us, event | category | flops | bytes accessed | tf_op | source)
XLA Modules:
  0.0 252.1 jit_solution(15472482827748294265)
XLA Ops:
  5.7 2.7 %shard_map.271 = (bf16[1280,394]{1,0:T(8,128)(2,1)}, bf16[1280,256]{1,0:T(8,128)(2,1)}) custom-call(s32[5]{0:T(128)S(1)} %stack.23.refs_0_, s32[2,394]{1,0:T(2,128)S(1)} %bitcast.45, bf16[394,1024]{1,0:T(8,128)(2,1)S(1)} %copy-done.3), custom_call_target="tpu_custom_call" | custom-call | flops 2875000064 | tf_op jit(solution)/shard_map/pallas_call | solution.py:52
  8.3 5.8 %all-to-all-start.1 = ((bf16[8,160,256]{2,1,0:T(8,128)(2,1)}), bf16[8,160,256]{2,1,0:T(8,128)(2,1)S(1)}, u32[]{:S(2)}, u32[]{:S(2)}) async-start(bf16[8,160,256]{2,1,0:T(8,128)(2,1)} %bitcast.13), calls=%async_computation.1 | async-start | bytes 1310720 | tf_op jit(solution)/shard_map/all_to_all | solution.py:665
  15.9 4.8 %shard_map.272 = (bf16[394,1024]{1,0:T(8,128)(2,1)S(1)}, bf16[394,256]{1,0:T(8,128)(2,1)S(1)}, bf16[394,256]{1,0:T(8,128)(2,1)S(1)}, bf16[394,256]{1,0:T(8,128)(2,1)S(1)}, bf16[394,256]{1,0:T(8,128)(2,1)S(1)}) custom-call(bf16[394,1024]{1,0:T(8,128)(2,1)} %refs_1_.1, f32[1,1024]{1,0:T(1,128)S(1)} %bitcast.51, f32[1,1024]{1,0:T(1,128)S(1)} %bitcast.46, ...), custom_call_target="tpu_custom_call" | custom-call | flops 5405000192 | tf_op jit(solution)/shard_map/pallas_call | solution.py:52
  24.7 5.5 %collective-permute-done.1.refs_3_ = bf16[394,256]{1,0:T(8,128)(2,1)S(1)} collective-permute-done((bf16[394,256]{1,0:T(8,128)(2,1)S(1)}, bf16[394,256]{1,0:T(8,128)(2,1)S(1)}, u32[]{:S(2)}, u32[]{:S(2)}) %collective-permute-start.1) | collective-permute-done | bytes 201760 | tf_op jit(solution)/shard_map/ppermute | solution.py:69
  31.7 5.6 %shard_map.273 = (f32[394,1024]{1,0:T(8,128)}, bf16[394,1024]{1,0:T(8,128)(2,1)}, f32[394,8]{1,0:T(8,128)S(1)}, bf16[1280,512]{1,0:T(8,128)(2,1)}) custom-call(s32[5]{0:T(128)S(1)} %stack.23.refs_0_, bf16[394,256]{1,0:T(8,128)(2,1)S(1)} %get-tuple-element.71.refs_1_.refs_14_, bf16[394,256]{1,0:T(8,128)(2,1)S(1)} %collective-permute-done.refs_2_, ...), custom_call_target="tpu_custom_call" | custom-call | flops 6325000192 | tf_op jit(solution)/shard_map/pallas_call | solution.py:52
  38.0 6.2 %all-to-all-start = ((bf16[8,160,512]{2,1,0:T(8,128)(2,1)}), bf16[8,160,512]{2,1,0:T(8,128)(2,1)S(1)}, u32[]{:S(2)}, u32[]{:S(2)}) async-start(bf16[8,160,512]{2,1,0:T(8,128)(2,1)} %bitcast.60), calls=%async_computation | async-start | bytes 2621440 | tf_op jit(solution)/shard_map/all_to_all | solution.py:708
  45.8 15.3 %collective-permute-done.7.refs_4_ = bf16[1280,256]{1,0:T(8,128)(2,1)S(1)} collective-permute-done((bf16[1280,256]{1,0:T(8,128)(2,1)S(1)}, bf16[1280,256]{1,0:T(8,128)(2,1)S(1)}, u32[]{:S(2)}, u32[]{:S(2)}) %collective-permute-start.7) | collective-permute-done | bytes 655392 | tf_op jit(solution)/shard_map/ppermute | solution.py:69
  64.0 7.5 %shard_map.275 = (bf16[1280,1024]{1,0:T(8,128)(2,1)}, f32[1280,1024]{1,0:T(8,128)}, f32[1280,1]{1,0:T(8,128)S(1)}) custom-call(s32[5]{0:T(128)S(1)} %stack.23.refs_0_, bf16[1280,256]{1,0:T(8,128)(2,1)S(1)} %bitcast.43, bf16[1280,256]{1,0:T(8,128)(2,1)S(1)} %collective-permute-done.6.refs_2_, bf16[1280,256]{1,0:T(8,128)(2,1)} %copy-done.36, ...), custom_call_target="tpu_custom_call" | custom-call | flops 8049999872 | tf_op jit(solution)/shard_map/pallas_call | solution.py:52
  71.5 4.3 %all-to-all-done = bf16[8,160,512]{2,1,0:T(8,128)(2,1)S(1)} async-done(((bf16[8,160,512]{2,1,0:T(8,128)(2,1)}), bf16[8,160,512]{2,1,0:T(8,128)(2,1)S(1)}, u32[]{:S(2)}, u32[]{:S(2)}) %all-to-all-start) | async-done | bytes 1310752 | tf_op jit(solution)/shard_map/all_to_all | solution.py:708
  75.8 3.0 %collective-permute-done.9.refs_2_ = bf16[1280,512]{1,0:T(8,128)(2,1)S(1)} collective-permute-done((bf16[1280,512]{1,0:T(8,128)(2,1)S(1)}, bf16[1280,512]{1,0:T(8,128)(2,1)S(1)}, u32[]{:S(2)}, u32[]{:S(2)}) %collective-permute-start.9) | collective-permute-done | bytes 1310752 | tf_op jit(solution)/shard_map/ppermute | solution.py:69
  79.9 16.7 %shard_map.276 = (bf16[8,176,256]{2,1,0:T(8,128)(2,1)}, bf16[8,176,256]{2,1,0:T(8,128)(2,1)}, bf16[8,176,256]{2,1,0:T(8,128)(2,1)}, bf16[8,176,256]{2,1,0:T(8,12...) custom-call(s32[5]{0:T(128)S(1)} %stack.23.refs_0_, ...), custom_call_target="tpu_custom_call" | custom-call | flops 19549999104 | tf_op jit(solution)/shard_map/pallas_call | solution.py:52
  103.9 6.5 %shard_map.277 = (bf16[1280,256]{1,0:T(8,128)(2,1)S(1)}, bf16[1280,256]{1,0:T(8,128)(2,1)S(1)}, bf16[1280,256]{1,0:T(8,128)(2,1)S(1)}, bf16[1280,256]{1,0:T(8,128)(2,1)}) custom-call(s32[5]{0:T(128)S(1)} %stack.23.refs_0_, bf16[1280,1024]{1,0:T(8,128)(2,1)} %get-tuple-element.90.refs_1_.refs_0_, f32[1280,1]{1,0:T(8,128)} %copy-done.20, ...), custom_call_target="tpu_custom_call" | custom-call | flops 7474999808 | tf_op jit(solution)/shard_map/pallas_call | solution.py:52
  115.1 5.7 %collective-permute-done.14 = bf16[8,176,256]{2,1,0:T(8,128)(2,1)} collective-permute-done((bf16[8,176,256]{2,1,0:T(8,128)(2,1)}, bf16[8,176,256]{2,1,0:T(8,128)(2,1)}, u32[]{:S(2)}, u32[]{:S(2)}) %collective-permute-start.14) | collective-permute-done | bytes 720928 | tf_op jit(solution)/shard_map/ppermute | solution.py:69
  123.0 3.6 %all-to-all-start.3 = ((bf16[8,176,256]{2,1,0:T(8,128)(2,1)}), bf16[8,176,256]{2,1,0:T(8,128)(2,1)S(1)}, u32[]{:S(2)}, u32[]{:S(2)}) async-start(bf16[8,176,256]{2,1,0:T(8,128)(2,1)} %add_convert_fusion.refs_4_), calls=%async_computation.3 | async-start | bytes 1441792 | tf_op jit(solution)/shard_map/all_to_all | solution.py:789
  127.7 2.6 %shard_map.278 = (bf16[1280,256]{1,0:T(8,128)(2,1)S(1)}, bf16[1280,256]{1,0:T(8,128)(2,1)S(1)}) custom-call(bf16[1280,256]{1,0:T(8,128)(2,1)S(1)} %copy-done.17, bf16[1280,256]{1,0:T(8,128)(2,1)} %copy-done.18, bf16[1280,256]{1,0:T(8,128)(2,1)} %collective-permute-done.12.refs_2_, bf16[1280,256]{1,0:T(8,128)(2,1)} %collective-permute-done.13.refs_3_, ...), custom_call_target="tpu_custom_call" | custom-call | flops 2300000000 | tf_op jit(solution)/shard_map/pallas_call | solution.py:52
  131.9 7.1 %shard_map.281 = f32[1024,1024]{1,0:T(8,128)} custom-call(bf16[1280,1024]{1,0:T(8,128)(2,1)} %get-tuple-element.90.refs_1_.refs_0_, bf16[1280,1024]{1,0:T(8,128)(2,1)} %get-tuple-element.104.refs_1_, bf16[1280,256]{1,0:T(8,128)(2,1)S(1)} %get-tuple-element.98.refs_2_.refs_4_, bf16[1280,256]{1,0:T(8,128)(2,1)S(1)} %get-tuple-element.99.refs_3_.refs_5_), custom_call_target="tpu_custom_call" | custom-call | flops 8049999872 | tf_op jit(solution)/shard_map/pallas_call | solution.py:52
  139.0 7.6 %shard_map.282 = f32[1024,1024]{1,0:T(8,128)} custom-call(s32[5]{0:T(128)S(1)} %stack.23.refs_0_, bf16[1280,512]{1,0:T(8,128)(2,1)} %bitcast.59, bf16[1280,512]{1,0:T(8,128)(2,1)} %copy-done.34, bf16[1280,1024]{1,0:T(8,128)(2,1)} %get-tuple-element.105.refs_3_, bf16[1280,256]{1,0:T(8,128)(2,1)S(1)} %get-tuple-element.98.refs_2_.refs_4_, ...), custom_call_target="tpu_custom_call" | custom-call | flops 8049999872 | tf_op jit(solution)/shard_map/pallas_call | solution.py:52
  151.1 6.0 %all-to-all-start.2 = ((bf16[8,160,256]{2,1,0:T(8,128)(2,1)}), bf16[8,160,256]{2,1,0:T(8,128)(2,1)S(1)}, u32[]{:S(2)}, u32[]{:S(2)}) async-start(bf16[8,160,256]{2,1,0:T(8,128)(2,1)} %bitcast.17), calls=%async_computation.2 | async-start | bytes 1310720 | tf_op jit(solution)/shard_map/all_to_all | solution.py:843
  159.8 6.1 %shard_map.284 = (f32[394,1024]{1,0:T(8,128)}, bf16[512,256]{1,0:T(8,128)(2,1)S(1)}, bf16[512,256]{1,0:T(8,128)(2,1)}, bf16[394,256]{1,0:T(8,128)(2,1)S(1)}, f32[11,1024]{1,0:T(8,128)S(1)}) custom-call(s32[5]{0:T(128)S(1)} %stack.23.refs_0_, bf16[394,256]{1,0:T(8,128)(2,1)S(1)} %shard_map.283.refs_1_, bf16[394,256]{1,0:T(8,128)(2,1)S(1)} %collective-permute-done.19.refs_2_, ...), custom_call_target="tpu_custom_call" | custom-call | flops 6899999744 | tf_op jit(solution)/shard_map/pallas_call | solution.py:52
  165.9 8.2 %shard_map.285 = (bf16[768,256]{1,0:T(8,128)(2,1)S(1)}, bf16[768,256]{1,0:T(8,128)(2,1)}, bf16[768,256]{1,0:T(8,128)(2,1)}, bf16[768,256]{1,0:T(8,128)(2,1)}, f3...) custom-call(s32[5]{0:T(128)S(1)} %stack.23.refs_0_, ...), custom_call_target="tpu_custom_call" | custom-call | flops 9200000000 | tf_op jit(solution)/shard_map/pallas_call | solution.py:52
  181.5 3.2 %collective-permute-done.37.refs_1_ = bf16[512,256]{1,0:T(8,128)(2,1)S(1)} collective-permute-done((bf16[512,256]{1,0:T(8,128)(2,1)S(1)}, bf16[512,256]{1,0:T(8,128)(2,1)S(1)}, u32[]{:S(2)}, u32[]{:S(2)}) %collective-permute-start.37) | collective-permute-done | bytes 262176 | tf_op jit(solution)/shard_map/ppermute | solution.py:69
  186.2 2.6 %collective-permute-start.38 = (bf16[256,256]{1,0:T(8,128)(2,1)S(1)}, bf16[256,256]{1,0:T(8,128)(2,1)S(1)}, u32[]{:S(2)}, u32[]{:S(2)}) collective-permute-start(bf16[256,256]{1,0:T(8,128)(2,1)S(1)} %constant_dynamic-slice_fusion.1), channel_id=1, source_target_pairs={{0,12},{4,8},{8,4},{12,0},{16,28},{20,24},{24,20},{28,16},{1,13},{... | collective-permute-start | bytes 393224 | tf_op jit(solution)/shard_map/ppermute | solution.py:69
  189.6 6.3 %collective-permute-done.25.refs_1_ = bf16[768,256]{1,0:T(8,128)(2,1)S(1)} collective-permute-done((bf16[768,256]{1,0:T(8,128)(2,1)S(1)}, bf16[768,256]{1,0:T(8,128)(2,1)S(1)}, u32[]{:S(2)}, u32[]{:S(2)}) %collective-permute-start.25) | collective-permute-done | bytes 393248 | tf_op jit(solution)/shard_map/ppermute | solution.py:69
  198.4 3.9 %collective-permute-start.39 = (bf16[128,256]{1,0:T(8,128)(2,1)S(1)}, bf16[128,256]{1,0:T(8,128)(2,1)S(1)}, u32[]{:S(2)}, u32[]{:S(2)}) collective-permute-start(bf16[128,256]{1,0:T(8,128)(2,1)S(1)} %constant_dynamic-slice_fusion), channel_id=1, source_target_pairs={{0,24},{4,28},{8,16},{12,20},{16,8},{20,12},{24,0},{28,4},{1,25},{... | collective-permute-start | bytes 196616 | tf_op jit(solution)/shard_map/ppermute | solution.py:69
  202.2 2.5 shard_map.280
  208.7 3.9 %collective-permute-start.27 = (bf16[192,256]{1,0:T(8,128)(2,1)S(1)}, bf16[192,256]{1,0:T(8,128)(2,1)S(1)}, u32[]{:S(2)}, u32[]{:S(2)}) collective-permute-start(bf16[192,256]{1,0:T(8,128)(2,1)S(1)} %constant_dynamic-slice_fusion.4), channel_id=1, source_target_pairs={{0,16},{4,20},{8,24},{12,28},{16,0},{20,4},{24,8},{28,12},{1,17},{... | collective-permute-start | bytes 294920 | tf_op jit(solution)/shard_map/ppermute | solution.py:69
  212.7 6.2 %collective-permute-done.33 = bf16[192,256]{1,0:T(8,128)(2,1)S(1)} collective-permute-done((bf16[192,256]{1,0:T(8,128)(2,1)S(1)}, bf16[192,256]{1,0:T(8,128)(2,1)S(1)}, u32[]{:S(2)}, u32[]{:S(2)}) %collective-permute-start.33) | collective-permute-done | bytes 98336 | tf_op jit(solution)/shard_map/ppermute | solution.py:69
  224.2 3.0 %collective-permute-done.34 = bf16[192,256]{1,0:T(8,128)(2,1)S(1)} collective-permute-done((bf16[192,256]{1,0:T(8,128)(2,1)S(1)}, bf16[192,256]{1,0:T(8,128)(2,1)S(1)}, u32[]{:S(2)}, u32[]{:S(2)}) %collective-permute-start.34) | collective-permute-done | bytes 98336 | tf_op jit(solution)/shard_map/ppermute | solution.py:69
  231.8 3.0 %collective-permute-done.35 = bf16[384,256]{1,0:T(8,128)(2,1)S(1)} collective-permute-done((bf16[384,256]{1,0:T(8,128)(2,1)S(1)}, bf16[384,256]{1,0:T(8,128)(2,1)S(1)}, u32[]{:S(2)}, u32[]{:S(2)}) %collective-permute-start.35) | collective-permute-done | bytes 196640 | tf_op jit(solution)/shard_map/ppermute | solution.py:69
  237.3 2.6 %collective-permute-start.30 = (bf16[832,256]{1,0:T(8,128)(2,1)S(1)}, bf16[832,256]{1,0:T(8,128)(2,1)S(1)}, u32[]{:S(2)}, u32[]{:S(2)}) collective-permute-start(bf16[832,256]{1,0:T(8,128)(2,1)S(1)} %pad_maximum_fusion), channel_id=1, source_target_pairs={{0,4},{4,0},{8,12},{12,8},{16,20},{20,16},{24,28},{28,24},{1,5},{5... | collective-permute-start | bytes 1277960 | tf_op jit(solution)/shard_map/ppermute | solution.py:69
  242.0 3.9 %shard_map.286.refs_5_ = f32[394,1024]{1,0:T(8,128)} custom-call(s32[5]{0:T(128)S(1)} %stack.23.refs_0_, bf16[394,1024]{1,0:T(8,128)(2,1)S(1)} %copy-done.4, f32[1,1024]{1,0:T(1,128)S(1)} %bitcast.52, bf16[400,512]{1,0:T(8,128)(2,1)S(1)} %add_convert_fusion.4.refs_3_, bf16[400,512]{1,0:T(8,128)(2,1)S(1)} %collective-permute-done.24.refs_4_, ...), custom_call_target="tpu_custom_call" | custom-call | flops 4485000192 | tf_op jit(solution)/shard_map/pallas_call | solution.py:52
  249.6 2.5 %shard_map.289 = f32[3,1024,256]{2,1,0:T(8,128)} custom-call(s32[5]{0:T(128)S(1)} %stack.23.refs_0_, bf16[768,256]{1,0:T(8,128)(2,1)S(1)} %maximum_select_fusion.refs_1_, bf16[768,256]{1,0:T(8,128)(2,1)S(1)} %slice.89.refs_2_, bf16[768,256]{1,0:T(8,128)(2,1)S(1)} %maximum_select_fusion.1.refs_3_, bf16[768,256]{1,0:T(8,128)(2,1)S(1)} %collective-permute-done.36.refs_4_, ...), custom_call_target="tpu_custom_call" | custom-call | flops 2300000000 | tf_op jit(solution)/shard_map/pallas_call | solution.py:52
  (213 shorter events, 76.7 us)
Async XLA Ops:
  0.6 15.1 %collective-permute-start.4 = (bf16[256,1024]{1,0:T(8,128)(2,1)}, bf16[256,1024]{1,0:T(8,128)(2,1)S(1)}, u32[]{:S(2)}, u32[]{:S(2)}) collective-permute-start(bf16[256,1024]{1,0:T(8,128)(2,1)} %refs_13_.2), channel_id=1, source_target_pairs={{0,3},{1,2},{2,1},{3,0},{4,7},{5,6},{6,5},{7,4},{8,11},{9,10},{10,... | collective-permute-start | bytes 1572872 | tf_op jit(solution)/shard_map/ppermute | solution.py:69
  3.1 28.6 %collective-permute-start.3 = (bf16[256,1024]{1,0:T(8,128)(2,1)}, bf16[256,1024]{1,0:T(8,128)(2,1)}, u32[]{:S(2)}, u32[]{:S(2)}) collective-permute-start(bf16[256,1024]{1,0:T(8,128)(2,1)} %refs_13_.2), channel_id=1, source_target_pairs={{0,1},{1,0},{2,3},{3,2},{4,5},{5,4},{6,7},{7,6},{8,9},{9,8},{10,11... | collective-permute-start | bytes 1572872 | tf_op jit(solution)/shard_map/ppermute | solution.py:69
  8.3 29.6 %all-to-all-start.1 = ((bf16[8,160,256]{2,1,0:T(8,128)(2,1)}), bf16[8,160,256]{2,1,0:T(8,128)(2,1)S(1)}, u32[]{:S(2)}, u32[]{:S(2)}) async-start(bf16[8,160,256]{2,1,0:T(8,128)(2,1)} %bitcast.13), calls=%async_computation.1 | async-start | bytes 1310720 | tf_op jit(solution)/shard_map/all_to_all | solution.py:665
  15.7 16.0 %collective-permute-start.5 = (bf16[256,1024]{1,0:T(8,128)(2,1)S(1)}, bf16[256,1024]{1,0:T(8,128)(2,1)}, u32[]{:S(2)}, u32[]{:S(2)}) collective-permute-start(bf16[256,1024]{1,0:T(8,128)(2,1)S(1)} %collective-permute-done.4.refs_8_), channel_id=1, source_target_pairs={{0,1},{1,0},{2,3},{3,2},{4,5},{5,4},{6,7},{7,6},{8,9},{9,8},{10,11... | collective-permute-start | bytes 1572872 | tf_op jit(solution)/shard_map/ppermute | solution.py:69
  38.0 37.9 %all-to-all-start = ((bf16[8,160,512]{2,1,0:T(8,128)(2,1)}), bf16[8,160,512]{2,1,0:T(8,128)(2,1)S(1)}, u32[]{:S(2)}, u32[]{:S(2)}) async-start(bf16[8,160,512]{2,1,0:T(8,128)(2,1)} %bitcast.60), calls=%async_computation | async-start | bytes 2621440 | tf_op jit(solution)/shard_map/all_to_all | solution.py:708
  44.1 16.9 %collective-permute-start.7 = (bf16[1280,256]{1,0:T(8,128)(2,1)S(1)}, bf16[1280,256]{1,0:T(8,128)(2,1)S(1)}, u32[]{:S(2)}, u32[]{:S(2)}) collective-permute-start(bf16[1280,256]{1,0:T(8,128)(2,1)S(1)} %bitcast.41), channel_id=1, source_target_pairs={{0,3},{1,2},{2,1},{3,0},{4,7},{5,6},{6,5},{7,4},{8,11},{9,10},{10,... | collective-permute-start | bytes 1966088 | tf_op jit(solution)/shard_map/ppermute | solution.py:69
  45.1 16.2 %collective-permute-start.6 = (bf16[1280,256]{1,0:T(8,128)(2,1)S(1)}, bf16[1280,256]{1,0:T(8,128)(2,1)S(1)}, u32[]{:S(2)}, u32[]{:S(2)}) collective-permute-start(bf16[1280,256]{1,0:T(8,128)(2,1)S(1)} %bitcast.42), channel_id=1, source_target_pairs={{0,1},{1,0},{2,3},{3,2},{4,5},{5,4},{6,7},{7,6},{8,9},{9,8},{10,11... | collective-permute-start | bytes 1966088 | tf_op jit(solution)/shard_map/ppermute | solution.py:69
  102.3 18.5 %collective-permute-start.14 = (bf16[8,176,256]{2,1,0:T(8,128)(2,1)}, bf16[8,176,256]{2,1,0:T(8,128)(2,1)}, u32[]{:S(2)}, u32[]{:S(2)}) collective-permute-start(bf16[8,176,256]{2,1,0:T(8,128)(2,1)} %add_convert_fusion.1), channel_id=1, source_target_pairs={{0,2},{1,3},{2,0},{3,1},{4,6},{5,7},{6,4},{7,5},{8,10},{9,11},{10,... | collective-permute-start | bytes 2162696 | tf_op jit(solution)/shard_map/ppermute | solution.py:69
  112.0 14.6 %collective-permute-start.12 = (bf16[1280,256]{1,0:T(8,128)(2,1)S(1)}, bf16[1280,256]{1,0:T(8,128)(2,1)}, u32[]{:S(2)}, u32[]{:S(2)}) collective-permute-start(bf16[1280,256]{1,0:T(8,128)(2,1)S(1)} %get-tuple-element.94), channel_id=1, source_target_pairs={{0,1},{1,0},{2,3},{3,2},{4,5},{5,4},{6,7},{7,6},{8,9},{9,8},{10,11... | collective-permute-start | bytes 1966088 | tf_op jit(solution)/shard_map/ppermute | solution.py:69
  112.0 14.6 %collective-permute-start.13 = (bf16[1280,256]{1,0:T(8,128)(2,1)}, bf16[1280,256]{1,0:T(8,128)(2,1)}, u32[]{:S(2)}, u32[]{:S(2)}) collective-permute-start(bf16[1280,256]{1,0:T(8,128)(2,1)} %get-tuple-element.95), channel_id=1, source_target_pairs={{0,1},{1,0},{2,3},{3,2},{4,5},{5,4},{6,7},{7,6},{8,9},{9,8},{10,11... | collective-permute-start | bytes 1966088 | tf_op jit(solution)/shard_map/ppermute | solution.py:69
  123.0 23.6 %all-to-all-start.3 = ((bf16[8,176,256]{2,1,0:T(8,128)(2,1)}), bf16[8,176,256]{2,1,0:T(8,128)(2,1)S(1)}, u32[]{:S(2)}, u32[]{:S(2)}) async-start(bf16[8,176,256]{2,1,0:T(8,128)(2,1)} %add_convert_fusion.refs_4_), calls=%async_computation.3 | async-start | bytes 1441792 | tf_op jit(solution)/shard_map/all_to_all | solution.py:789
  130.3 18.6 %collective-permute-start.15 = (bf16[1280,256]{1,0:T(8,128)(2,1)S(1)}, bf16[1280,256]{1,0:T(8,128)(2,1)}, u32[]{:S(2)}, u32[]{:S(2)}) collective-permute-start(bf16[1280,256]{1,0:T(8,128)(2,1)S(1)} %get-tuple-element.99.refs_3_.refs_5_), channel_id=1, source_target_pairs={{0,2},{1,3},{2,0},{3,1},{4,6},{5,7},{6,4},{7,5},{8,10},{9,11},{10,... | collective-permute-start | bytes 1966088 | tf_op jit(solution)/shard_map/ppermute | solution.py:69
  148.4 8.7 %collective-permute-start.20 = (bf16[394,256]{1,0:T(8,128)(2,1)S(1)}, bf16[394,256]{1,0:T(8,128)(2,1)S(1)}, u32[]{:S(2)}, u32[]{:S(2)}) collective-permute-start(bf16[394,256]{1,0:T(8,128)(2,1)S(1)} %shard_map.283.refs_1_), channel_id=1, source_target_pairs={{0,2},{1,3},{2,0},{3,1},{4,6},{5,7},{6,4},{7,5},{8,10},{9,11},{10,... | collective-permute-start | bytes 605192 | tf_op jit(solution)/shard_map/ppermute | solution.py:69
  151.1 26.5 %all-to-all-start.2 = ((bf16[8,160,256]{2,1,0:T(8,128)(2,1)}), bf16[8,160,256]{2,1,0:T(8,128)(2,1)S(1)}, u32[]{:S(2)}, u32[]{:S(2)}) async-start(bf16[8,160,256]{2,1,0:T(8,128)(2,1)} %bitcast.17), calls=%async_computation.2 | async-start | bytes 1310720 | tf_op jit(solution)/shard_map/all_to_all | solution.py:843
  174.1 12.0 %collective-permute-start.31 = (bf16[768,256]{1,0:T(8,128)(2,1)}, bf16[768,256]{1,0:T(8,128)(2,1)S(1)}, u32[]{:S(2)}, u32[]{:S(2)}) collective-permute-start(bf16[768,256]{1,0:T(8,128)(2,1)} %get-tuple-element.118), channel_id=1, source_target_pairs={{0,8},{4,12},{8,0},{12,4},{16,24},{20,28},{24,16},{28,20},{1,9},{5... | collective-permute-start | bytes 1179656 | tf_op jit(solution)/shard_map/ppermute | solution.py:69
  176.1 8.6 %collective-permute-start.37 = (bf16[512,256]{1,0:T(8,128)(2,1)S(1)}, bf16[512,256]{1,0:T(8,128)(2,1)S(1)}, u32[]{:S(2)}, u32[]{:S(2)}) collective-permute-start(bf16[512,256]{1,0:T(8,128)(2,1)S(1)} %copy-done.40), channel_id=1, source_target_pairs={{0,4},{4,0},{8,12},{12,8},{16,20},{20,16},{24,28},{28,24},{1,5},{5... | collective-permute-start | bytes 786440 | tf_op jit(solution)/shard_map/ppermute | solution.py:69
  180.9 15.1 %collective-permute-start.25 = (bf16[768,256]{1,0:T(8,128)(2,1)S(1)}, bf16[768,256]{1,0:T(8,128)(2,1)S(1)}, u32[]{:S(2)}, u32[]{:S(2)}) collective-permute-start(bf16[768,256]{1,0:T(8,128)(2,1)S(1)} %copy-done.39), channel_id=1, source_target_pairs={{0,4},{4,0},{8,12},{12,8},{16,20},{20,16},{24,28},{28,24},{1,5},{5... | collective-permute-start | bytes 1179656 | tf_op jit(solution)/shard_map/ppermute | solution.py:69
  184.7 13.7 %collective-permute-start.16 = (bf16[394,256]{1,0:T(8,128)(2,1)S(1)}, bf16[394,256]{1,0:T(8,128)(2,1)S(1)}, u32[]{:S(2)}, u32[]{:S(2)}) collective-permute-start(bf16[394,256]{1,0:T(8,128)(2,1)S(1)} %shard_map.279.refs_2_), channel_id=1, source_target_pairs={{0,1},{1,0},{2,3},{3,2},{4,5},{5,4},{6,7},{7,6},{8,9},{9,8},{10,11... | collective-permute-start | bytes 605192 | tf_op jit(solution)/shard_map/ppermute | solution.py:69
  186.1 16.2 %collective-permute-start.18 = (bf16[394,256]{1,0:T(8,128)(2,1)S(1)}, bf16[394,256]{1,0:T(8,128)(2,1)S(1)}, u32[]{:S(2)}, u32[]{:S(2)}) collective-permute-start(bf16[394,256]{1,0:T(8,128)(2,1)S(1)} %collective-permute-done.17.refs_4_), channel_id=1, source_target_pairs={{0,1},{1,0},{2,3},{3,2},{4,5},{5,4},{6,7},{7,6},{8,9},{9,8},{10,11... | collective-permute-start | bytes 605192 | tf_op jit(solution)/shard_map/ppermute | solution.py:69
  186.2 12.0 %collective-permute-start.38 = (bf16[256,256]{1,0:T(8,128)(2,1)S(1)}, bf16[256,256]{1,0:T(8,128)(2,1)S(1)}, u32[]{:S(2)}, u32[]{:S(2)}) collective-permute-start(bf16[256,256]{1,0:T(8,128)(2,1)S(1)} %constant_dynamic-slice_fusion.1), channel_id=1, source_target_pairs={{0,12},{4,8},{8,4},{12,0},{16,28},{20,24},{24,20},{28,16},{1,13},{... | collective-permute-start | bytes 393224 | tf_op jit(solution)/shard_map/ppermute | solution.py:69
  188.9 19.5 %collective-permute-start.32 = (bf16[384,256]{1,0:T(8,128)(2,1)S(1)}, bf16[384,256]{1,0:T(8,128)(2,1)S(1)}, u32[]{:S(2)}, u32[]{:S(2)}) collective-permute-start(bf16[384,256]{1,0:T(8,128)(2,1)S(1)} %constant_dynamic-slice_fusion.3), channel_id=1, source_target_pairs={{0,4},{4,0},{8,12},{12,8},{16,20},{20,16},{24,28},{28,24},{1,5},{5... | collective-permute-start | bytes 589832 | tf_op jit(solution)/shard_map/ppermute | solution.py:69
  196.0 16.6 %collective-permute-start.23 = (bf16[400,512]{1,0:T(8,128)(2,1)S(1)}, bf16[400,512]{1,0:T(8,128)(2,1)S(1)}, u32[]{:S(2)}, u32[]{:S(2)}) collective-permute-start(bf16[400,512]{1,0:T(8,128)(2,1)S(1)} %add_convert_fusion.5.refs_2_), channel_id=1, source_target_pairs={{0,2},{1,3},{2,0},{3,1},{4,6},{5,7},{6,4},{7,5},{8,10},{9,11},{10,... | collective-permute-start | bytes 1228808 | tf_op jit(solution)/shard_map/ppermute | solution.py:69
  198.2 10.4 %collective-permute-start.26 = (bf16[384,256]{1,0:T(8,128)(2,1)S(1)}, bf16[384,256]{1,0:T(8,128)(2,1)S(1)}, u32[]{:S(2)}, u32[]{:S(2)}) collective-permute-start(bf16[384,256]{1,0:T(8,128)(2,1)S(1)} %constant_dynamic-slice_fusion.5), channel_id=1, source_target_pairs={{0,8},{4,12},{8,0},{12,4},{16,24},{20,28},{24,16},{28,20},{1,9},{5... | collective-permute-start | bytes 589832 | tf_op jit(solution)/shard_map/ppermute | solution.py:69
  206.5 15.7 %collective-permute-start.40 = (bf16[128,256]{1,0:T(8,128)(2,1)S(1)}, bf16[128,256]{1,0:T(8,128)(2,1)S(1)}, u32[]{:S(2)}, u32[]{:S(2)}) collective-permute-start(bf16[128,256]{1,0:T(8,128)(2,1)S(1)} %add_convert_fusion.12), channel_id=1, source_target_pairs={{0,24},{4,28},{8,16},{12,20},{16,8},{20,12},{24,0},{28,4},{1,25},{... | collective-permute-start | bytes 196616 | tf_op jit(solution)/shard_map/ppermute | solution.py:69
  208.5 10.4 %collective-permute-start.33 = (bf16[192,256]{1,0:T(8,128)(2,1)S(1)}, bf16[192,256]{1,0:T(8,128)(2,1)S(1)}, u32[]{:S(2)}, u32[]{:S(2)}) collective-permute-start(bf16[192,256]{1,0:T(8,128)(2,1)S(1)} %constant_dynamic-slice_fusion.2), channel_id=1, source_target_pairs={{0,20},{4,16},{8,28},{12,24},{16,4},{20,0},{24,12},{28,8},{1,21},{... | collective-permute-start | bytes 294920 | tf_op jit(solution)/shard_map/ppermute | solution.py:69
  208.7 12.0 %collective-permute-start.27 = (bf16[192,256]{1,0:T(8,128)(2,1)S(1)}, bf16[192,256]{1,0:T(8,128)(2,1)S(1)}, u32[]{:S(2)}, u32[]{:S(2)}) collective-permute-start(bf16[192,256]{1,0:T(8,128)(2,1)S(1)} %constant_dynamic-slice_fusion.4), channel_id=1, source_target_pairs={{0,16},{4,20},{8,24},{12,28},{16,0},{20,4},{24,8},{28,12},{1,17},{... | collective-permute-start | bytes 294920 | tf_op jit(solution)/shard_map/ppermute | solution.py:69
  218.9 8.2 %collective-permute-start.34 = (bf16[192,256]{1,0:T(8,128)(2,1)S(1)}, bf16[192,256]{1,0:T(8,128)(2,1)S(1)}, u32[]{:S(2)}, u32[]{:S(2)}) collective-permute-start(bf16[192,256]{1,0:T(8,128)(2,1)S(1)} %add_convert_fusion.10), channel_id=1, source_target_pairs={{0,20},{4,16},{8,28},{12,24},{16,4},{20,0},{24,12},{28,8},{1,21},{... | collective-permute-start | bytes 294920 | tf_op jit(solution)/shard_map/ppermute | solution.py:69
  222.2 8.5 %collective-permute-start.41 = (bf16[256,256]{1,0:T(8,128)(2,1)S(1)}, bf16[256,256]{1,0:T(8,128)(2,1)S(1)}, u32[]{:S(2)}, u32[]{:S(2)}) collective-permute-start(bf16[256,256]{1,0:T(8,128)(2,1)S(1)} %maximum_select_fusion.5), channel_id=1, source_target_pairs={{0,12},{4,8},{8,4},{12,0},{16,28},{20,24},{24,20},{28,16},{1,13},{... | collective-permute-start | bytes 393224 | tf_op jit(solution)/shard_map/ppermute | solution.py:69
  228.9 8.2 %collective-permute-start.29 = (bf16[448,256]{1,0:T(8,128)(2,1)S(1)}, bf16[448,256]{1,0:T(8,128)(2,1)S(1)}, u32[]{:S(2)}, u32[]{:S(2)}) collective-permute-start(bf16[448,256]{1,0:T(8,128)(2,1)S(1)} %pad_maximum_fusion.1), channel_id=1, source_target_pairs={{0,8},{4,12},{8,0},{12,4},{16,24},{20,28},{24,16},{28,20},{1,9},{5... | collective-permute-start | bytes 688136 | tf_op jit(solution)/shard_map/ppermute | solution.py:69
  230.7 9.6 %collective-permute-start.42 = (bf16[512,256]{1,0:T(8,128)(2,1)S(1)}, bf16[512,256]{1,0:T(8,128)(2,1)S(1)}, u32[]{:S(2)}, u32[]{:S(2)}) collective-permute-start(bf16[512,256]{1,0:T(8,128)(2,1)S(1)} %maximum_select_fusion.2.refs_1_), channel_id=1, source_target_pairs={{0,4},{4,0},{8,12},{12,8},{16,20},{20,16},{24,28},{28,24},{1,5},{5... | collective-permute-start | bytes 786440 | tf_op jit(solution)/shard_map/ppermute | solution.py:69
  235.0 14.6 %collective-permute-start.36 = (bf16[768,256]{1,0:T(8,128)(2,1)S(1)}, bf16[768,256]{1,0:T(8,128)(2,1)S(1)}, u32[]{:S(2)}, u32[]{:S(2)}) collective-permute-start(bf16[768,256]{1,0:T(8,128)(2,1)S(1)} %maximum_select_fusion.1.refs_3_), channel_id=1, source_target_pairs={{0,8},{4,12},{8,0},{12,4},{16,24},{20,28},{24,16},{28,20},{1,9},{5... | collective-permute-start | bytes 1179656 | tf_op jit(solution)/shard_map/ppermute | solution.py:69
  237.3 10.4 %collective-permute-start.30 = (bf16[832,256]{1,0:T(8,128)(2,1)S(1)}, bf16[832,256]{1,0:T(8,128)(2,1)S(1)}, u32[]{:S(2)}, u32[]{:S(2)}) collective-permute-start(bf16[832,256]{1,0:T(8,128)(2,1)S(1)} %pad_maximum_fusion), channel_id=1, source_target_pairs={{0,4},{4,0},{8,12},{12,8},{16,20},{20,16},{24,28},{28,24},{1,5},{5... | collective-permute-start | bytes 1277960 | tf_op jit(solution)/shard_map/ppermute | solution.py:69
  (56 other events, 392.7 us)

commit v2 on v1

--- a/solution.py
+++ b/solution.py
@@ -237,7 +237,20 @@
     return table.astype(bf16)
 
 
-def route_kernel(idx_ref, flipped_ref, dout_ref, dispatch_ref, send_ref, *, experts, capacity):
+def route_kernel(
+    idx_ref,
+    routes_ref,
+    flipped_ref,
+    dout_ref,
+    plain_ref,
+    padded_ref,
+    dispatch_ref,
+    send_ref,
+    *,
+    experts,
+    capacity,
+):
+    place_kernel(routes_ref, plain_ref, padded_ref, experts=experts, capacity=capacity)
     rows = dispatch_ref.shape[1]
     width = send_ref.shape[1]
     first = lax.broadcasted_iota(jnp.int32, (rows, rows), 0)
@@ -653,11 +666,16 @@
     stride = capacity + EXTRA
     row_bits = bits_of(blocks)
 
-    dispatch_place, grad_send = call(
+    plain, padded, dispatch_place, grad_send = call(
         functools.partial(route_kernel, experts=experts, capacity=capacity),
-        [sds((slots, rows), bf16), sds((slots, piece), bf16)],
-        [ids, routes.T, d_out],
-        2.5,
+        [
+            sds((rows, slots), bf16),
+            sds((rows, experts * stride), bf16),
+            sds((slots, rows), bf16),
+            sds((slots, piece), bf16),
+        ],
+        [ids, routes, routes.T, d_out],
+        4.4,
         scalars=1,
     )
     w_out_all = gather_tensor(w_out, diagonal=True)
@@ -695,14 +713,6 @@
         5.5,
         scalars=1,
         scratch=[pltpu.VMEM((blocks, rows, width), f32)],
-    )
-
-    plain, padded = call(
-        functools.partial(place_kernel, experts=experts, capacity=capacity),
-        [sds((rows, slots), bf16), sds((rows, experts * stride), bf16)],
-        [routes],
-        2.5,
-        after=[send],
     )
 
     own = lax.all_to_all(

time: 253 us -> 251 us (level)
  waiting for transfers between devices: 75.1 us -> 80 us
  starting transfers between devices: 62.4 us -> 58 us
  other arithmetic: 8.77 us -> 6 us
    ppermute x43, waiting for transfers between devices: 70.8 us -> 75.8 us  [swap(): return lax.ppermute(values, axis, [(i, i ^ bit) for i in range(count)])]
    ppermute x43, starting transfers between devices: 40.8 us -> 36.4 us  [swap(): return lax.ppermute(values, axis, [(i, i ^ bit) for i in range(count)])]
    convert_element_type x16, other arithmetic: 8.12 us -> 5.35 us  [add(): return (left.astype(f32) + right.astype(f32)).astype(left.dtype)]
    unnamed x85 -> x81, local copies, waits for them, and re-layouts: 11.4 us -> 12 us
    pallas_call x21 -> x20, Pallas kernels: 91.1 us -> 90.5 us  [call(): pl.pallas_call(run, out_shape=outs, compiler_params=pltpu.CompilerParams(...]
  transfers between devices with their start and end apart: 47 -> 47, of which waited for: 24 -> 23; matrix products, arithmetic and copies ran while one was open for 4% -> 4% of each run, Pallas kernels for 29% -> 29%
where the time goes in v2:
time: 251 us; the launch traced here: 250 us
  Pallas kernels  90.5 us (36%)
  waiting for transfers between devices  80 us (32%)
  starting transfers between devices  58 us (23%)
  local copies, waits for them, and re-layouts  14.2 us (6%)
  other arithmetic  6 us (2%)
    pallas_call x20, Pallas kernels, call(): pl.pallas_call(run, out_shape=outs, compiler_params=pltpu.CompilerParams(...  90.5 us
    ppermute x43, waiting for transfers between devices, swap(): return lax.ppermute(values, axis, [(i, i ^ bit) for i in range(count)])  75.8 us
    ppermute x43, starting transfers between devices, swap(): return lax.ppermute(values, axis, [(i, i ^ bit) for i in range(count)])  36.4 us
    unnamed x81, local copies, waits for them, and re-layouts  12 us
    all_to_all x1, starting transfers between devices, on_device(): lax.all_to_all(send.reshape(experts, capacity, half), 'expert', 0, 0, til...  6.12 us
    all_to_all x1, starting transfers between devices, on_device(): lax.all_to_all(out_sent.reshape(experts, capacity, piece), 'expert', 0, 0...  6 us
    all_to_all x1, starting transfers between devices, on_device(): lax.all_to_all(grad_send.reshape(experts, capacity, piece), 'expert', 0,...  5.84 us
    convert_element_type x16, other arithmetic, add(): return (left.astype(f32) + right.astype(f32)).astype(left.dtype)  5.35 us
  transfers between devices with their start and end apart: 47, of which 23 were waited for; matrix products, arithmetic and copies ran while one was open for 4% of the time, Pallas kernels for 29%

profile of v2, /device:TPU:0, one launch (start us, length us, event | category | flops | bytes accessed | tf_op | source)
XLA Modules:
  0.0 250.0 jit_solution(1147452415302075149)
XLA Ops:
  6.5 4.5 %shard_map.271 = (bf16[394,1280]{1,0:T(8,128)(2,1)}, bf16[394,1408]{1,0:T(8,128)(2,1)}, bf16[1280,394]{1,0:T(8,128)(2,1)}, bf16[1280,256]{1,0:T(8,128)(2,1)}) custom-call(s32[5]{0:T(128)S(1)} %stack.23.refs_0_, s32[394,2]{1,0:T(8,128)S(1)} %copy.36.refs_1_, s32[2,394]{1,0:T(2,128)S(1)} %bitcast.45, bf16[394,1024]{1,0:T(8,128)(2,1)S(1)} %copy-done.2), custom_call_target="tpu_custom_call" | custom-call | flops 5059999744 | tf_op jit(solution)/shard_map/pallas_call | solution.py:52
  11.0 5.8 %all-to-all-start.1 = ((bf16[8,160,256]{2,1,0:T(8,128)(2,1)}), bf16[8,160,256]{2,1,0:T(8,128)(2,1)S(1)}, u32[]{:S(2)}, u32[]{:S(2)}) async-start(bf16[8,160,256]{2,1,0:T(8,128)(2,1)} %bitcast.13), calls=%async_computation.1 | async-start | bytes 1310720 | tf_op jit(solution)/shard_map/all_to_all | solution.py:683
  17.0 4.8 %shard_map.272 = (bf16[394,1024]{1,0:T(8,128)(2,1)S(1)}, bf16[394,256]{1,0:T(8,128)(2,1)S(1)}, bf16[394,256]{1,0:T(8,128)(2,1)S(1)}, bf16[394,256]{1,0:T(8,128)(2,1)S(1)}, bf16[394,256]{1,0:T(8,128)(2,1)S(1)}) custom-call(bf16[394,1024]{1,0:T(8,128)(2,1)} %refs_1_.2, f32[1,1024]{1,0:T(1,128)S(1)} %bitcast.51, f32[1,1024]{1,0:T(1,128)S(1)} %bitcast.46, ...), custom_call_target="tpu_custom_call" | custom-call | flops 5405000192 | tf_op jit(solution)/shard_map/pallas_call | solution.py:52
  24.7 6.1 %collective-permute-done.1.refs_3_ = bf16[394,256]{1,0:T(8,128)(2,1)S(1)} collective-permute-done((bf16[394,256]{1,0:T(8,128)(2,1)S(1)}, bf16[394,256]{1,0:T(8,128)(2,1)S(1)}, u32[]{:S(2)}, u32[]{:S(2)}) %collective-permute-start.1) | collective-permute-done | bytes 201760 | tf_op jit(solution)/shard_map/ppermute | solution.py:69
  32.3 5.6 %shard_map.273 = (f32[394,1024]{1,0:T(8,128)}, bf16[394,1024]{1,0:T(8,128)(2,1)}, f32[394,8]{1,0:T(8,128)S(1)}, bf16[1280,512]{1,0:T(8,128)(2,1)}) custom-call(s32[5]{0:T(128)S(1)} %stack.23.refs_0_, bf16[394,256]{1,0:T(8,128)(2,1)S(1)} %get-tuple-element.71.refs_1_.refs_14_, bf16[394,256]{1,0:T(8,128)(2,1)S(1)} %collective-permute-done.refs_2_, ...), custom_call_target="tpu_custom_call" | custom-call | flops 6325000192 | tf_op jit(solution)/shard_map/pallas_call | solution.py:52
  38.6 6.1 %all-to-all-start = ((bf16[8,160,512]{2,1,0:T(8,128)(2,1)}), bf16[8,160,512]{2,1,0:T(8,128)(2,1)S(1)}, u32[]{:S(2)}, u32[]{:S(2)}) async-start(bf16[8,160,512]{2,1,0:T(8,128)(2,1)} %bitcast.60), calls=%async_computation | async-start | bytes 2621440 | tf_op jit(solution)/shard_map/all_to_all | solution.py:718
  45.8 15.9 %collective-permute-done.7.refs_4_ = bf16[1280,256]{1,0:T(8,128)(2,1)S(1)} collective-permute-done((bf16[1280,256]{1,0:T(8,128)(2,1)S(1)}, bf16[1280,256]{1,0:T(8,128)(2,1)S(1)}, u32[]{:S(2)}, u32[]{:S(2)}) %collective-permute-start.7) | collective-permute-done | bytes 655392 | tf_op jit(solution)/shard_map/ppermute | solution.py:69
  64.6 7.5 %shard_map.274 = (bf16[1280,1024]{1,0:T(8,128)(2,1)}, f32[1280,1024]{1,0:T(8,128)}, f32[1280,1]{1,0:T(8,128)S(1)}) custom-call(s32[5]{0:T(128)S(1)} %stack.23.refs_0_, bf16[1280,256]{1,0:T(8,128)(2,1)S(1)} %bitcast.43, bf16[1280,256]{1,0:T(8,128)(2,1)S(1)} %collective-permute-done.6.refs_2_, bf16[1280,256]{1,0:T(8,128)(2,1)} %copy-done.34, ...), custom_call_target="tpu_custom_call" | custom-call | flops 8049999872 | tf_op jit(solution)/shard_map/pallas_call | solution.py:52
  72.2 4.2 %all-to-all-done = bf16[8,160,512]{2,1,0:T(8,128)(2,1)S(1)} async-done(((bf16[8,160,512]{2,1,0:T(8,128)(2,1)}), bf16[8,160,512]{2,1,0:T(8,128)(2,1)S(1)}, u32[]{:S(2)}, u32[]{:S(2)}) %all-to-all-start) | async-done | bytes 1310752 | tf_op jit(solution)/shard_map/all_to_all | solution.py:718
  76.4 3.0 %collective-permute-done.9.refs_2_ = bf16[1280,512]{1,0:T(8,128)(2,1)S(1)} collective-permute-done((bf16[1280,512]{1,0:T(8,128)(2,1)S(1)}, bf16[1280,512]{1,0:T(8,128)(2,1)S(1)}, u32[]{:S(2)}, u32[]{:S(2)}) %collective-permute-start.9) | collective-permute-done | bytes 1310752 | tf_op jit(solution)/shard_map/ppermute | solution.py:69
  80.5 16.7 %shard_map.275 = (bf16[8,176,256]{2,1,0:T(8,128)(2,1)}, bf16[8,176,256]{2,1,0:T(8,128)(2,1)}, bf16[8,176,256]{2,1,0:T(8,128)(2,1)}, bf16[8,176,256]{2,1,0:T(8,12...) custom-call(s32[5]{0:T(128)S(1)} %stack.23.refs_0_, ...), custom_call_target="tpu_custom_call" | custom-call | flops 19549999104 | tf_op jit(solution)/shard_map/pallas_call | solution.py:52
  102.3 6.5 %shard_map.276 = (bf16[1280,256]{1,0:T(8,128)(2,1)S(1)}, bf16[1280,256]{1,0:T(8,128)(2,1)S(1)}, bf16[1280,256]{1,0:T(8,128)(2,1)S(1)}, bf16[1280,256]{1,0:T(8,128)(2,1)}) custom-call(s32[5]{0:T(128)S(1)} %stack.23.refs_0_, bf16[1280,1024]{1,0:T(8,128)(2,1)} %get-tuple-element.90.refs_1_.refs_0_, f32[1280,1]{1,0:T(8,128)} %copy-done.18, ...), custom_call_target="tpu_custom_call" | custom-call | flops 7474999808 | tf_op jit(solution)/shard_map/pallas_call | solution.py:52
  110.2 9.4 %collective-permute-done.14 = bf16[8,176,256]{2,1,0:T(8,128)(2,1)S(1)} collective-permute-done((bf16[8,176,256]{2,1,0:T(8,128)(2,1)S(1)}, bf16[8,176,256]{2,1,0:T(8,128)(2,1)S(1)}, u32[]{:S(2)}, u32[]{:S(2)}) %collective-permute-start.14) | collective-permute-done | bytes 720928 | tf_op jit(solution)/shard_map/ppermute | solution.py:69
  120.6 3.6 %all-to-all-start.3 = ((bf16[8,176,256]{2,1,0:T(8,128)(2,1)}), bf16[8,176,256]{2,1,0:T(8,128)(2,1)S(1)}, u32[]{:S(2)}, u32[]{:S(2)}) async-start(bf16[8,176,256]{2,1,0:T(8,128)(2,1)} %add_convert_fusion.refs_4_), calls=%async_computation.3 | async-start | bytes 1441792 | tf_op jit(solution)/shard_map/all_to_all | solution.py:799
  126.2 2.6 %shard_map.277 = (bf16[1280,256]{1,0:T(8,128)(2,1)S(1)}, bf16[1280,256]{1,0:T(8,128)(2,1)S(1)}) custom-call(bf16[1280,256]{1,0:T(8,128)(2,1)S(1)} %copy-done.15, bf16[1280,256]{1,0:T(8,128)(2,1)} %copy-done.16, bf16[1280,256]{1,0:T(8,128)(2,1)} %copy-done.32, bf16[1280,256]{1,0:T(8,128)(2,1)} %collective-permute-done.13.refs_3_, ...), custom_call_target="tpu_custom_call" | custom-call | flops 2300000000 | tf_op jit(solution)/shard_map/pallas_call | solution.py:52
  129.8 7.1 %shard_map.280 = f32[1024,1024]{1,0:T(8,128)} custom-call(bf16[1280,1024]{1,0:T(8,128)(2,1)} %get-tuple-element.90.refs_1_.refs_0_, bf16[1280,1024]{1,0:T(8,128)(2,1)} %get-tuple-element.104.refs_1_, bf16[1280,256]{1,0:T(8,128)(2,1)S(1)} %get-tuple-element.98.refs_2_.refs_4_, bf16[1280,256]{1,0:T(8,128)(2,1)S(1)} %get-tuple-element.99.refs_3_.refs_5_), custom_call_target="tpu_custom_call" | custom-call | flops 8049999872 | tf_op jit(solution)/shard_map/pallas_call | solution.py:52
  136.9 7.6 %shard_map.281 = f32[1024,1024]{1,0:T(8,128)} custom-call(s32[5]{0:T(128)S(1)} %stack.23.refs_0_, bf16[1280,512]{1,0:T(8,128)(2,1)} %bitcast.59, bf16[1280,512]{1,0:T(8,128)(2,1)} %copy-done.31, bf16[1280,1024]{1,0:T(8,128)(2,1)} %get-tuple-element.105.refs_3_, bf16[1280,256]{1,0:T(8,128)(2,1)S(1)} %get-tuple-element.98.refs_2_.refs_4_, ...), custom_call_target="tpu_custom_call" | custom-call | flops 8049999872 | tf_op jit(solution)/shard_map/pallas_call | solution.py:52
  149.5 6.0 %all-to-all-start.2 = ((bf16[8,160,256]{2,1,0:T(8,128)(2,1)}), bf16[8,160,256]{2,1,0:T(8,128)(2,1)S(1)}, u32[]{:S(2)}, u32[]{:S(2)}) async-start(bf16[8,160,256]{2,1,0:T(8,128)(2,1)} %bitcast.17), calls=%async_computation.2 | async-start | bytes 1310720 | tf_op jit(solution)/shard_map/all_to_all | solution.py:853
  158.2 6.1 %shard_map.283 = (f32[394,1024]{1,0:T(8,128)}, bf16[512,256]{1,0:T(8,128)(2,1)S(1)}, bf16[512,256]{1,0:T(8,128)(2,1)}, bf16[394,256]{1,0:T(8,128)(2,1)S(1)}, f32[11,1024]{1,0:T(8,128)S(1)}) custom-call(s32[5]{0:T(128)S(1)} %stack.23.refs_0_, bf16[394,256]{1,0:T(8,128)(2,1)S(1)} %shard_map.282.refs_1_, bf16[394,256]{1,0:T(8,128)(2,1)S(1)} %collective-permute-done.19.refs_2_, ...), custom_call_target="tpu_custom_call" | custom-call | flops 6899999744 | tf_op jit(solution)/shard_map/pallas_call | solution.py:52
  164.3 8.2 %shard_map.284 = (bf16[768,256]{1,0:T(8,128)(2,1)S(1)}, bf16[768,256]{1,0:T(8,128)(2,1)}, bf16[768,256]{1,0:T(8,128)(2,1)}, bf16[768,256]{1,0:T(8,128)(2,1)}, f3...) custom-call(s32[5]{0:T(128)S(1)} %stack.23.refs_0_, ...), custom_call_target="tpu_custom_call" | custom-call | flops 9200000000 | tf_op jit(solution)/shard_map/pallas_call | solution.py:52
  179.4 4.4 %collective-permute-done.37.refs_1_ = bf16[512,256]{1,0:T(8,128)(2,1)S(1)} collective-permute-done((bf16[512,256]{1,0:T(8,128)(2,1)S(1)}, bf16[512,256]{1,0:T(8,128)(2,1)S(1)}, u32[]{:S(2)}, u32[]{:S(2)}) %collective-permute-start.37) | collective-permute-done | bytes 262176 | tf_op jit(solution)/shard_map/ppermute | solution.py:69
  184.6 2.6 %collective-permute-start.38 = (bf16[256,256]{1,0:T(8,128)(2,1)S(1)}, bf16[256,256]{1,0:T(8,128)(2,1)S(1)}, u32[]{:S(2)}, u32[]{:S(2)}) collective-permute-start(bf16[256,256]{1,0:T(8,128)(2,1)S(1)} %constant_dynamic-slice_fusion.1), channel_id=1, source_target_pairs={{0,12},{4,8},{8,4},{12,0},{16,28},{20,24},{24,20},{28,16},{1,13},{... | collective-permute-start | bytes 393224 | tf_op jit(solution)/shard_map/ppermute | solution.py:69
  188.1 6.9 %collective-permute-done.25.refs_1_ = bf16[768,256]{1,0:T(8,128)(2,1)S(1)} collective-permute-done((bf16[768,256]{1,0:T(8,128)(2,1)S(1)}, bf16[768,256]{1,0:T(8,128)(2,1)S(1)}, u32[]{:S(2)}, u32[]{:S(2)}) %collective-permute-start.25) | collective-permute-done | bytes 393248 | tf_op jit(solution)/shard_map/ppermute | solution.py:69
  196.3 3.8 %collective-permute-start.39 = (bf16[128,256]{1,0:T(8,128)(2,1)S(1)}, bf16[128,256]{1,0:T(8,128)(2,1)S(1)}, u32[]{:S(2)}, u32[]{:S(2)}) collective-permute-start(bf16[128,256]{1,0:T(8,128)(2,1)S(1)} %constant_dynamic-slice_fusion), channel_id=1, source_target_pairs={{0,24},{4,28},{8,16},{12,20},{16,8},{20,12},{24,0},{28,4},{1,25},{... | collective-permute-start | bytes 196616 | tf_op jit(solution)/shard_map/ppermute | solution.py:69
  200.0 2.5 %shard_map.279 = bf16[394,1024]{1,0:T(8,128)(2,1)} custom-call(s32[5]{0:T(128)S(1)} %stack.23.refs_0_, f32[394,1024]{1,0:T(8,128)} %get-tuple-element.73.refs_1_.refs_10_, bf16[394,256]{1,0:T(8,128)(2,1)S(1)} %shard_map.278.refs_2_, bf16[394,256]{1,0:T(8,128)(2,1)S(1)} %collective-permute-done.16.refs_3_, ...), custom_call_target="tpu_custom_call" | custom-call | flops 2990000128 | tf_op jit(solution)/shard_map/pallas_call | solution.py:52
  206.5 4.0 %collective-permute-start.27 = (bf16[192,256]{1,0:T(8,128)(2,1)S(1)}, bf16[192,256]{1,0:T(8,128)(2,1)S(1)}, u32[]{:S(2)}, u32[]{:S(2)}) collective-permute-start(bf16[192,256]{1,0:T(8,128)(2,1)S(1)} %constant_dynamic-slice_fusion.4), channel_id=1, source_target_pairs={{0,16},{4,20},{8,24},{12,28},{16,0},{20,4},{24,8},{28,12},{1,17},{... | collective-permute-start | bytes 294920 | tf_op jit(solution)/shard_map/ppermute | solution.py:69
  210.6 6.1 %collective-permute-done.33 = bf16[192,256]{1,0:T(8,128)(2,1)S(1)} collective-permute-done((bf16[192,256]{1,0:T(8,128)(2,1)S(1)}, bf16[192,256]{1,0:T(8,128)(2,1)S(1)}, u32[]{:S(2)}, u32[]{:S(2)}) %collective-permute-start.33) | collective-permute-done | bytes 98336 | tf_op jit(solution)/shard_map/ppermute | solution.py:69
  222.0 3.0 %collective-permute-done.34 = bf16[192,256]{1,0:T(8,128)(2,1)S(1)} collective-permute-done((bf16[192,256]{1,0:T(8,128)(2,1)S(1)}, bf16[192,256]{1,0:T(8,128)(2,1)S(1)}, u32[]{:S(2)}, u32[]{:S(2)}) %collective-permute-start.34) | collective-permute-done | bytes 98336 | tf_op jit(solution)/shard_map/ppermute | solution.py:69
  229.6 3.1 %collective-permute-done.35 = bf16[384,256]{1,0:T(8,128)(2,1)S(1)} collective-permute-done((bf16[384,256]{1,0:T(8,128)(2,1)S(1)}, bf16[384,256]{1,0:T(8,128)(2,1)S(1)}, u32[]{:S(2)}, u32[]{:S(2)}) %collective-permute-start.35) | collective-permute-done | bytes 196640 | tf_op jit(solution)/shard_map/ppermute | solution.py:69
  232.9 2.5 collective-permute-done.29
  239.8 3.8 %shard_map.285.refs_5_ = f32[394,1024]{1,0:T(8,128)} custom-call(s32[5]{0:T(128)S(1)} %stack.23.refs_0_, bf16[394,1024]{1,0:T(8,128)(2,1)S(1)} %copy-done.3, f32[1,1024]{1,0:T(1,128)S(1)} %bitcast.52, bf16[400,512]{1,0:T(8,128)(2,1)S(1)} %add_convert_fusion.4.refs_3_, bf16[400,512]{1,0:T(8,128)(2,1)S(1)} %collective-permute-done.24.refs_4_, ...), custom_call_target="tpu_custom_call" | custom-call | flops 4485000192 | tf_op jit(solution)/shard_map/pallas_call | solution.py:52
  247.5 2.5 %shard_map.288 = f32[3,1024,256]{2,1,0:T(8,128)} custom-call(s32[5]{0:T(128)S(1)} %stack.23.refs_0_, bf16[768,256]{1,0:T(8,128)(2,1)S(1)} %maximum_select_fusion.refs_1_, bf16[768,256]{1,0:T(8,128)(2,1)S(1)} %slice.89.refs_2_, bf16[768,256]{1,0:T(8,128)(2,1)S(1)} %maximum_select_fusion.1.refs_3_, bf16[768,256]{1,0:T(8,128)(2,1)S(1)} %collective-permute-done.36.refs_4_, ...), custom_call_target="tpu_custom_call" | custom-call | flops 2300000000 | tf_op jit(solution)/shard_map/pallas_call | solution.py:52
  (208 shorter events, 66.2 us)
Async XLA Ops:
  0.6 16.2 %collective-permute-start.4 = (bf16[256,1024]{1,0:T(8,128)(2,1)}, bf16[256,1024]{1,0:T(8,128)(2,1)S(1)}, u32[]{:S(2)}, u32[]{:S(2)}) collective-permute-start(bf16[256,1024]{1,0:T(8,128)(2,1)} %refs_13_.2), channel_id=1, source_target_pairs={{0,3},{1,2},{2,1},{3,0},{4,7},{5,6},{6,5},{7,4},{8,11},{9,10},{10,... | collective-permute-start | bytes 1572872 | tf_op jit(solution)/shard_map/ppermute | solution.py:69
  3.1 29.2 %collective-permute-start.3 = (bf16[256,1024]{1,0:T(8,128)(2,1)}, bf16[256,1024]{1,0:T(8,128)(2,1)}, u32[]{:S(2)}, u32[]{:S(2)}) collective-permute-start(bf16[256,1024]{1,0:T(8,128)(2,1)} %refs_13_.2), channel_id=1, source_target_pairs={{0,1},{1,0},{2,3},{3,2},{4,5},{5,4},{6,7},{7,6},{8,9},{9,8},{10,11... | collective-permute-start | bytes 1572872 | tf_op jit(solution)/shard_map/ppermute | solution.py:69
  11.0 27.6 %all-to-all-start.1 = ((bf16[8,160,256]{2,1,0:T(8,128)(2,1)}), bf16[8,160,256]{2,1,0:T(8,128)(2,1)S(1)}, u32[]{:S(2)}, u32[]{:S(2)}) async-start(bf16[8,160,256]{2,1,0:T(8,128)(2,1)} %bitcast.13), calls=%async_computation.1 | async-start | bytes 1310720 | tf_op jit(solution)/shard_map/all_to_all | solution.py:683
  16.9 15.5 %collective-permute-start.5 = (bf16[256,1024]{1,0:T(8,128)(2,1)S(1)}, bf16[256,1024]{1,0:T(8,128)(2,1)}, u32[]{:S(2)}, u32[]{:S(2)}) collective-permute-start(bf16[256,1024]{1,0:T(8,128)(2,1)S(1)} %collective-permute-done.4.refs_8_), channel_id=1, source_target_pairs={{0,1},{1,0},{2,3},{3,2},{4,5},{5,4},{6,7},{7,6},{8,9},{9,8},{10,11... | collective-permute-start | bytes 1572872 | tf_op jit(solution)/shard_map/ppermute | solution.py:69
  38.6 37.8 %all-to-all-start = ((bf16[8,160,512]{2,1,0:T(8,128)(2,1)}), bf16[8,160,512]{2,1,0:T(8,128)(2,1)S(1)}, u32[]{:S(2)}, u32[]{:S(2)}) async-start(bf16[8,160,512]{2,1,0:T(8,128)(2,1)} %bitcast.60), calls=%async_computation | async-start | bytes 2621440 | tf_op jit(solution)/shard_map/all_to_all | solution.py:718
  44.7 17.0 %collective-permute-start.7 = (bf16[1280,256]{1,0:T(8,128)(2,1)S(1)}, bf16[1280,256]{1,0:T(8,128)(2,1)S(1)}, u32[]{:S(2)}, u32[]{:S(2)}) collective-permute-start(bf16[1280,256]{1,0:T(8,128)(2,1)S(1)} %bitcast.41), channel_id=1, source_target_pairs={{0,3},{1,2},{2,1},{3,0},{4,7},{5,6},{6,5},{7,4},{8,11},{9,10},{10,... | collective-permute-start | bytes 1966088 | tf_op jit(solution)/shard_map/ppermute | solution.py:69
  45.2 16.7 %collective-permute-start.6 = (bf16[1280,256]{1,0:T(8,128)(2,1)S(1)}, bf16[1280,256]{1,0:T(8,128)(2,1)S(1)}, u32[]{:S(2)}, u32[]{:S(2)}) collective-permute-start(bf16[1280,256]{1,0:T(8,128)(2,1)S(1)} %bitcast.42), channel_id=1, source_target_pairs={{0,1},{1,0},{2,3},{3,2},{4,5},{5,4},{6,7},{7,6},{8,9},{9,8},{10,11... | collective-permute-start | bytes 1966088 | tf_op jit(solution)/shard_map/ppermute | solution.py:69
  101.3 18.3 %collective-permute-start.14 = (bf16[8,176,256]{2,1,0:T(8,128)(2,1)S(1)}, bf16[8,176,256]{2,1,0:T(8,128)(2,1)S(1)}, u32[]{:S(2)}, u32[]{:S(2)}) collective-permute-start(bf16[8,176,256]{2,1,0:T(8,128)(2,1)S(1)} %add_convert_fusion.1), channel_id=1, source_target_pairs={{0,2},{1,3},{2,0},{3,1},{4,6},{5,7},{6,4},{7,5},{8,10},{9,11},{10,... | collective-permute-start | bytes 2162696 | tf_op jit(solution)/shard_map/ppermute | solution.py:69
  109.7 14.6 %collective-permute-start.12 = (bf16[1280,256]{1,0:T(8,128)(2,1)S(1)}, bf16[1280,256]{1,0:T(8,128)(2,1)S(1)}, u32[]{:S(2)}, u32[]{:S(2)}) collective-permute-start(bf16[1280,256]{1,0:T(8,128)(2,1)S(1)} %get-tuple-element.94), channel_id=1, source_target_pairs={{0,1},{1,0},{2,3},{3,2},{4,5},{5,4},{6,7},{7,6},{8,9},{9,8},{10,11... | collective-permute-start | bytes 1966088 | tf_op jit(solution)/shard_map/ppermute | solution.py:69
  109.7 14.6 %collective-permute-start.13 = (bf16[1280,256]{1,0:T(8,128)(2,1)}, bf16[1280,256]{1,0:T(8,128)(2,1)}, u32[]{:S(2)}, u32[]{:S(2)}) collective-permute-start(bf16[1280,256]{1,0:T(8,128)(2,1)} %get-tuple-element.95), channel_id=1, source_target_pairs={{0,1},{1,0},{2,3},{3,2},{4,5},{5,4},{6,7},{7,6},{8,9},{9,8},{10,11... | collective-permute-start | bytes 1966088 | tf_op jit(solution)/shard_map/ppermute | solution.py:69
  120.6 23.9 %all-to-all-start.3 = ((bf16[8,176,256]{2,1,0:T(8,128)(2,1)}), bf16[8,176,256]{2,1,0:T(8,128)(2,1)S(1)}, u32[]{:S(2)}, u32[]{:S(2)}) async-start(bf16[8,176,256]{2,1,0:T(8,128)(2,1)} %add_convert_fusion.refs_4_), calls=%async_computation.3 | async-start | bytes 1441792 | tf_op jit(solution)/shard_map/all_to_all | solution.py:799
  128.8 18.6 %collective-permute-start.15 = (bf16[1280,256]{1,0:T(8,128)(2,1)S(1)}, bf16[1280,256]{1,0:T(8,128)(2,1)}, u32[]{:S(2)}, u32[]{:S(2)}) collective-permute-start(bf16[1280,256]{1,0:T(8,128)(2,1)S(1)} %get-tuple-element.99.refs_3_.refs_5_), channel_id=1, source_target_pairs={{0,2},{1,3},{2,0},{3,1},{4,6},{5,7},{6,4},{7,5},{8,10},{9,11},{10,... | collective-permute-start | bytes 1966088 | tf_op jit(solution)/shard_map/ppermute | solution.py:69
  146.3 9.3 %collective-permute-start.20 = (bf16[394,256]{1,0:T(8,128)(2,1)S(1)}, bf16[394,256]{1,0:T(8,128)(2,1)S(1)}, u32[]{:S(2)}, u32[]{:S(2)}) collective-permute-start(bf16[394,256]{1,0:T(8,128)(2,1)S(1)} %shard_map.282.refs_1_), channel_id=1, source_target_pairs={{0,2},{1,3},{2,0},{3,1},{4,6},{5,7},{6,4},{7,5},{8,10},{9,11},{10,... | collective-permute-start | bytes 605192 | tf_op jit(solution)/shard_map/ppermute | solution.py:69
  149.5 26.5 %all-to-all-start.2 = ((bf16[8,160,256]{2,1,0:T(8,128)(2,1)}), bf16[8,160,256]{2,1,0:T(8,128)(2,1)S(1)}, u32[]{:S(2)}, u32[]{:S(2)}) async-start(bf16[8,160,256]{2,1,0:T(8,128)(2,1)} %bitcast.17), calls=%async_computation.2 | async-start | bytes 1310720 | tf_op jit(solution)/shard_map/all_to_all | solution.py:853
  172.5 12.0 %collective-permute-start.31 = (bf16[768,256]{1,0:T(8,128)(2,1)}, bf16[768,256]{1,0:T(8,128)(2,1)S(1)}, u32[]{:S(2)}, u32[]{:S(2)}) collective-permute-start(bf16[768,256]{1,0:T(8,128)(2,1)} %get-tuple-element.118), channel_id=1, source_target_pairs={{0,8},{4,12},{8,0},{12,4},{16,24},{20,28},{24,16},{28,20},{1,9},{5... | collective-permute-start | bytes 1179656 | tf_op jit(solution)/shard_map/ppermute | solution.py:69
  174.6 9.2 %collective-permute-start.37 = (bf16[512,256]{1,0:T(8,128)(2,1)S(1)}, bf16[512,256]{1,0:T(8,128)(2,1)S(1)}, u32[]{:S(2)}, u32[]{:S(2)}) collective-permute-start(bf16[512,256]{1,0:T(8,128)(2,1)S(1)} %copy-done.38), channel_id=1, source_target_pairs={{0,4},{4,0},{8,12},{12,8},{16,20},{20,16},{24,28},{28,24},{1,5},{5... | collective-permute-start | bytes 786440 | tf_op jit(solution)/shard_map/ppermute | solution.py:69
  178.7 8.6 %collective-permute-start.22 = (bf16[400,512]{1,0:T(8,128)(2,1)S(1)}, bf16[400,512]{1,0:T(8,128)(2,1)S(1)}, u32[]{:S(2)}, u32[]{:S(2)}) collective-permute-start(bf16[400,512]{1,0:T(8,128)(2,1)S(1)} %copy-done.36), channel_id=1, source_target_pairs={{0,1},{1,0},{2,3},{3,2},{4,5},{5,4},{6,7},{7,6},{8,9},{9,8},{10,11... | collective-permute-start | bytes 1228808 | tf_op jit(solution)/shard_map/ppermute | solution.py:69
  178.7 16.2 %collective-permute-start.25 = (bf16[768,256]{1,0:T(8,128)(2,1)S(1)}, bf16[768,256]{1,0:T(8,128)(2,1)S(1)}, u32[]{:S(2)}, u32[]{:S(2)}) collective-permute-start(bf16[768,256]{1,0:T(8,128)(2,1)S(1)} %copy-done.37), channel_id=1, source_target_pairs={{0,4},{4,0},{8,12},{12,8},{16,20},{20,16},{24,28},{28,24},{1,5},{5... | collective-permute-start | bytes 1179656 | tf_op jit(solution)/shard_map/ppermute | solution.py:69
  183.7 12.5 %collective-permute-start.16 = (bf16[394,256]{1,0:T(8,128)(2,1)S(1)}, bf16[394,256]{1,0:T(8,128)(2,1)S(1)}, u32[]{:S(2)}, u32[]{:S(2)}) collective-permute-start(bf16[394,256]{1,0:T(8,128)(2,1)S(1)} %shard_map.278.refs_2_), channel_id=1, source_target_pairs={{0,1},{1,0},{2,3},{3,2},{4,5},{5,4},{6,7},{7,6},{8,9},{9,8},{10,11... | collective-permute-start | bytes 605192 | tf_op jit(solution)/shard_map/ppermute | solution.py:69
  184.5 15.5 %collective-permute-start.18 = (bf16[394,256]{1,0:T(8,128)(2,1)S(1)}, bf16[394,256]{1,0:T(8,128)(2,1)S(1)}, u32[]{:S(2)}, u32[]{:S(2)}) collective-permute-start(bf16[394,256]{1,0:T(8,128)(2,1)S(1)} %collective-permute-done.17.refs_4_), channel_id=1, source_target_pairs={{0,1},{1,0},{2,3},{3,2},{4,5},{5,4},{6,7},{7,6},{8,9},{9,8},{10,11... | collective-permute-start | bytes 605192 | tf_op jit(solution)/shard_map/ppermute | solution.py:69
  184.6 11.3 %collective-permute-start.38 = (bf16[256,256]{1,0:T(8,128)(2,1)S(1)}, bf16[256,256]{1,0:T(8,128)(2,1)S(1)}, u32[]{:S(2)}, u32[]{:S(2)}) collective-permute-start(bf16[256,256]{1,0:T(8,128)(2,1)S(1)} %constant_dynamic-slice_fusion.1), channel_id=1, source_target_pairs={{0,12},{4,8},{8,4},{12,0},{16,28},{20,24},{24,20},{28,16},{1,13},{... | collective-permute-start | bytes 393224 | tf_op jit(solution)/shard_map/ppermute | solution.py:69
  187.3 18.8 %collective-permute-start.32 = (bf16[384,256]{1,0:T(8,128)(2,1)S(1)}, bf16[384,256]{1,0:T(8,128)(2,1)S(1)}, u32[]{:S(2)}, u32[]{:S(2)}) collective-permute-start(bf16[384,256]{1,0:T(8,128)(2,1)S(1)} %constant_dynamic-slice_fusion.3), channel_id=1, source_target_pairs={{0,4},{4,0},{8,12},{12,8},{16,20},{20,16},{24,28},{28,24},{1,5},{5... | collective-permute-start | bytes 589832 | tf_op jit(solution)/shard_map/ppermute | solution.py:69
  195.0 15.4 %collective-permute-start.23 = (bf16[400,512]{1,0:T(8,128)(2,1)S(1)}, bf16[400,512]{1,0:T(8,128)(2,1)S(1)}, u32[]{:S(2)}, u32[]{:S(2)}) collective-permute-start(bf16[400,512]{1,0:T(8,128)(2,1)S(1)} %add_convert_fusion.5.refs_2_), channel_id=1, source_target_pairs={{0,2},{1,3},{2,0},{3,1},{4,6},{5,7},{6,4},{7,5},{8,10},{9,11},{10,... | collective-permute-start | bytes 1228808 | tf_op jit(solution)/shard_map/ppermute | solution.py:69
  196.0 10.4 %collective-permute-start.26 = (bf16[384,256]{1,0:T(8,128)(2,1)S(1)}, bf16[384,256]{1,0:T(8,128)(2,1)S(1)}, u32[]{:S(2)}, u32[]{:S(2)}) collective-permute-start(bf16[384,256]{1,0:T(8,128)(2,1)S(1)} %constant_dynamic-slice_fusion.5), channel_id=1, source_target_pairs={{0,8},{4,12},{8,0},{12,4},{16,24},{20,28},{24,16},{28,20},{1,9},{5... | collective-permute-start | bytes 589832 | tf_op jit(solution)/shard_map/ppermute | solution.py:69
  204.3 15.9 %collective-permute-start.40 = (bf16[128,256]{1,0:T(8,128)(2,1)S(1)}, bf16[128,256]{1,0:T(8,128)(2,1)S(1)}, u32[]{:S(2)}, u32[]{:S(2)}) collective-permute-start(bf16[128,256]{1,0:T(8,128)(2,1)S(1)} %add_convert_fusion.12), channel_id=1, source_target_pairs={{0,24},{4,28},{8,16},{12,20},{16,8},{20,12},{24,0},{28,4},{1,25},{... | collective-permute-start | bytes 196616 | tf_op jit(solution)/shard_map/ppermute | solution.py:69
  206.3 10.5 %collective-permute-start.33 = (bf16[192,256]{1,0:T(8,128)(2,1)S(1)}, bf16[192,256]{1,0:T(8,128)(2,1)S(1)}, u32[]{:S(2)}, u32[]{:S(2)}) collective-permute-start(bf16[192,256]{1,0:T(8,128)(2,1)S(1)} %constant_dynamic-slice_fusion.2), channel_id=1, source_target_pairs={{0,20},{4,16},{8,28},{12,24},{16,4},{20,0},{24,12},{28,8},{1,21},{... | collective-permute-start | bytes 294920 | tf_op jit(solution)/shard_map/ppermute | solution.py:69
  206.5 12.0 %collective-permute-start.27 = (bf16[192,256]{1,0:T(8,128)(2,1)S(1)}, bf16[192,256]{1,0:T(8,128)(2,1)S(1)}, u32[]{:S(2)}, u32[]{:S(2)}) collective-permute-start(bf16[192,256]{1,0:T(8,128)(2,1)S(1)} %constant_dynamic-slice_fusion.4), channel_id=1, source_target_pairs={{0,16},{4,20},{8,24},{12,28},{16,0},{20,4},{24,8},{28,12},{1,17},{... | collective-permute-start | bytes 294920 | tf_op jit(solution)/shard_map/ppermute | solution.py:69
  220.2 8.4 %collective-permute-start.41 = (bf16[256,256]{1,0:T(8,128)(2,1)S(1)}, bf16[256,256]{1,0:T(8,128)(2,1)S(1)}, u32[]{:S(2)}, u32[]{:S(2)}) collective-permute-start(bf16[256,256]{1,0:T(8,128)(2,1)S(1)} %maximum_select_fusion.5), channel_id=1, source_target_pairs={{0,12},{4,8},{8,4},{12,0},{16,28},{20,24},{24,20},{28,16},{1,13},{... | collective-permute-start | bytes 393224 | tf_op jit(solution)/shard_map/ppermute | solution.py:69
  227.0 8.5 %collective-permute-start.29 = (bf16[448,256]{1,0:T(8,128)(2,1)S(1)}, bf16[448,256]{1,0:T(8,128)(2,1)S(1)}, u32[]{:S(2)}, u32[]{:S(2)}) collective-permute-start(bf16[448,256]{1,0:T(8,128)(2,1)S(1)} %pad_maximum_fusion.1), channel_id=1, source_target_pairs={{0,8},{4,12},{8,0},{12,4},{16,24},{20,28},{24,16},{28,20},{1,9},{5... | collective-permute-start | bytes 688136 | tf_op jit(solution)/shard_map/ppermute | solution.py:69
  228.6 9.6 %collective-permute-start.42 = (bf16[512,256]{1,0:T(8,128)(2,1)S(1)}, bf16[512,256]{1,0:T(8,128)(2,1)S(1)}, u32[]{:S(2)}, u32[]{:S(2)}) collective-permute-start(bf16[512,256]{1,0:T(8,128)(2,1)S(1)} %maximum_select_fusion.2.refs_1_), channel_id=1, source_target_pairs={{0,4},{4,0},{8,12},{12,8},{16,20},{20,16},{24,28},{28,24},{1,5},{5... | collective-permute-start | bytes 786440 | tf_op jit(solution)/shard_map/ppermute | solution.py:69
  232.9 14.6 %collective-permute-start.36 = (bf16[768,256]{1,0:T(8,128)(2,1)S(1)}, bf16[768,256]{1,0:T(8,128)(2,1)S(1)}, u32[]{:S(2)}, u32[]{:S(2)}) collective-permute-start(bf16[768,256]{1,0:T(8,128)(2,1)S(1)} %maximum_select_fusion.1.refs_3_), channel_id=1, source_target_pairs={{0,8},{4,12},{8,0},{12,4},{16,24},{20,28},{24,16},{28,20},{1,9},{5... | collective-permute-start | bytes 1179656 | tf_op jit(solution)/shard_map/ppermute | solution.py:69
  235.7 9.9 %collective-permute-start.30 = (bf16[832,256]{1,0:T(8,128)(2,1)S(1)}, bf16[832,256]{1,0:T(8,128)(2,1)S(1)}, u32[]{:S(2)}, u32[]{:S(2)}) collective-permute-start(bf16[832,256]{1,0:T(8,128)(2,1)S(1)} %pad_maximum_fusion), channel_id=1, source_target_pairs={{0,4},{4,0},{8,12},{12,8},{16,20},{20,16},{24,28},{28,24},{1,5},{5... | collective-permute-start | bytes 1277960 | tf_op jit(solution)/shard_map/ppermute | solution.py:69
  (54 other events, 372.8 us)

commit v3 on v2

--- a/solution.py
+++ b/solution.py
@@ -12,7 +12,7 @@
 LANES = 128
 VMEM_LIMIT = 52 * 1024 * 1024
 EXTRA = 16
-MASKS = ((1, 2, 4), (2, 1, 5), (1, 3, 6))
+MASKS = ((1, 2, 4), (2, 1, 4), (1, 2, 4))
 FLOPS_PER_US = 1.15e9
 
 epsilon = 1e-06

time: 251 us -> 247 us (0.984)
  waiting for transfers between devices: 80 us -> 72.4 us
  starting transfers between devices: 58 us -> 61.1 us
    ppermute x43, waiting for transfers between devices: 75.8 us -> 68.1 us  [swap(): return lax.ppermute(values, axis, [(i, i ^ bit) for i in range(count)])]
    ppermute x43, starting transfers between devices: 36.4 us -> 39.5 us  [swap(): return lax.ppermute(values, axis, [(i, i ^ bit) for i in range(count)])]
  transfers between devices with their start and end apart: 47 -> 47, of which waited for: 23 -> 19; matrix products, arithmetic and copies ran while one was open for 4% -> 4% of each run, Pallas kernels for 29% -> 29%
where the time goes in v3:
time: 247 us; the launch traced here: 245 us
  Pallas kernels  90.5 us (37%)
  waiting for transfers between devices  72.4 us (29%)
  starting transfers between devices  61.1 us (25%)
  local copies, waits for them, and re-layouts  14.2 us (6%)
  other arithmetic  5.91 us (2%)
    pallas_call x20, Pallas kernels, call(): pl.pallas_call(run, out_shape=outs, compiler_params=pltpu.CompilerParams(...  90.5 us
    ppermute x43, waiting for transfers between devices, swap(): return lax.ppermute(values, axis, [(i, i ^ bit) for i in range(count)])  68.1 us
    ppermute x43, starting transfers between devices, swap(): return lax.ppermute(values, axis, [(i, i ^ bit) for i in range(count)])  39.5 us
    unnamed x81, local copies, waits for them, and re-layouts  12 us
    all_to_all x1, starting transfers between devices, on_device(): lax.all_to_all(send.reshape(experts, capacity, half), 'expert', 0, 0, til...  6.12 us
    all_to_all x1, starting transfers between devices, on_device(): lax.all_to_all(out_sent.reshape(experts, capacity, piece), 'expert', 0, 0...  5.99 us
    all_to_all x1, starting transfers between devices, on_device(): lax.all_to_all(grad_send.reshape(experts, capacity, piece), 'expert', 0,...  5.83 us
    convert_element_type x16, other arithmetic, add(): return (left.astype(f32) + right.astype(f32)).astype(left.dtype)  5.26 us
  transfers between devices with their start and end apart: 47, of which 19 were waited for; matrix products, arithmetic and copies ran while one was open for 4% of the time, Pallas kernels for 29%

profile of v3, /device:TPU:0, one launch (start us, length us, event | category | flops | bytes accessed | tf_op | source)
XLA Modules:
  0.0 245.4 jit_solution(5110653417397409297)
XLA Ops:
  0.6 2.4 collective-permute-start.4
  6.5 4.5 %shard_map.271 = (bf16[394,1280]{1,0:T(8,128)(2,1)}, bf16[394,1408]{1,0:T(8,128)(2,1)}, bf16[1280,394]{1,0:T(8,128)(2,1)}, bf16[1280,256]{1,0:T(8,128)(2,1)}) custom-call(s32[5]{0:T(128)S(1)} %stack.20.refs_0_, s32[394,2]{1,0:T(8,128)S(1)} %copy.36.refs_1_, s32[2,394]{1,0:T(2,128)S(1)} %bitcast.44, bf16[394,1024]{1,0:T(8,128)(2,1)S(1)} %copy-done.2), custom_call_target="tpu_custom_call" | custom-call | flops 5059999744 | tf_op jit(solution)/shard_map/pallas_call | solution.py:52
  11.0 5.8 %all-to-all-start.1 = ((bf16[8,160,256]{2,1,0:T(8,128)(2,1)}), bf16[8,160,256]{2,1,0:T(8,128)(2,1)S(1)}, u32[]{:S(2)}, u32[]{:S(2)}) async-start(bf16[8,160,256]{2,1,0:T(8,128)(2,1)} %bitcast.12), calls=%async_computation.1 | async-start | bytes 1310720 | tf_op jit(solution)/shard_map/all_to_all | solution.py:683
  17.0 4.8 %shard_map.272 = (bf16[394,1024]{1,0:T(8,128)(2,1)S(1)}, bf16[394,256]{1,0:T(8,128)(2,1)S(1)}, bf16[394,256]{1,0:T(8,128)(2,1)S(1)}, bf16[394,256]{1,0:T(8,128)(2,1)S(1)}, bf16[394,256]{1,0:T(8,128)(2,1)S(1)}) custom-call(bf16[394,1024]{1,0:T(8,128)(2,1)} %refs_1_.2, f32[1,1024]{1,0:T(1,128)S(1)} %bitcast.50, f32[1,1024]{1,0:T(1,128)S(1)} %bitcast.45, ...), custom_call_target="tpu_custom_call" | custom-call | flops 5405000192 | tf_op jit(solution)/shard_map/pallas_call | solution.py:52
  24.7 6.1 %collective-permute-done.1.refs_3_ = bf16[394,256]{1,0:T(8,128)(2,1)S(1)} collective-permute-done((bf16[394,256]{1,0:T(8,128)(2,1)S(1)}, bf16[394,256]{1,0:T(8,128)(2,1)S(1)}, u32[]{:S(2)}, u32[]{:S(2)}) %collective-permute-start.1) | collective-permute-done | bytes 201760 | tf_op jit(solution)/shard_map/ppermute | solution.py:69
  32.4 5.6 %shard_map.273 = (f32[394,1024]{1,0:T(8,128)}, bf16[394,1024]{1,0:T(8,128)(2,1)}, f32[394,8]{1,0:T(8,128)S(1)}, bf16[1280,512]{1,0:T(8,128)(2,1)}) custom-call(s32[5]{0:T(128)S(1)} %stack.20.refs_0_, bf16[394,256]{1,0:T(8,128)(2,1)S(1)} %get-tuple-element.71.refs_1_.refs_14_, bf16[394,256]{1,0:T(8,128)(2,1)S(1)} %collective-permute-done.refs_2_, ...), custom_call_target="tpu_custom_call" | custom-call | flops 6325000192 | tf_op jit(solution)/shard_map/pallas_call | solution.py:52
  38.6 6.1 %all-to-all-start = ((bf16[8,160,512]{2,1,0:T(8,128)(2,1)}), bf16[8,160,512]{2,1,0:T(8,128)(2,1)S(1)}, u32[]{:S(2)}, u32[]{:S(2)}) async-start(bf16[8,160,512]{2,1,0:T(8,128)(2,1)} %bitcast.59), calls=%async_computation | async-start | bytes 2621440 | tf_op jit(solution)/shard_map/all_to_all | solution.py:718
  45.8 15.9 %collective-permute-done.7.refs_4_ = bf16[1280,256]{1,0:T(8,128)(2,1)S(1)} collective-permute-done((bf16[1280,256]{1,0:T(8,128)(2,1)S(1)}, bf16[1280,256]{1,0:T(8,128)(2,1)S(1)}, u32[]{:S(2)}, u32[]{:S(2)}) %collective-permute-start.7) | collective-permute-done | bytes 655392 | tf_op jit(solution)/shard_map/ppermute | solution.py:69
  64.7 7.5 %shard_map.274 = (bf16[1280,1024]{1,0:T(8,128)(2,1)}, f32[1280,1024]{1,0:T(8,128)}, f32[1280,1]{1,0:T(8,128)S(1)}) custom-call(s32[5]{0:T(128)S(1)} %stack.20.refs_0_, bf16[1280,256]{1,0:T(8,128)(2,1)S(1)} %bitcast.42, bf16[1280,256]{1,0:T(8,128)(2,1)S(1)} %collective-permute-done.6.refs_2_, bf16[1280,256]{1,0:T(8,128)(2,1)} %copy-done.34, ...), custom_call_target="tpu_custom_call" | custom-call | flops 8049999872 | tf_op jit(solution)/shard_map/pallas_call | solution.py:52
  72.2 4.2 %all-to-all-done = bf16[8,160,512]{2,1,0:T(8,128)(2,1)S(1)} async-done(((bf16[8,160,512]{2,1,0:T(8,128)(2,1)}), bf16[8,160,512]{2,1,0:T(8,128)(2,1)S(1)}, u32[]{:S(2)}, u32[]{:S(2)}) %all-to-all-start) | async-done | bytes 1310752 | tf_op jit(solution)/shard_map/all_to_all | solution.py:718
  76.4 3.0 %collective-permute-done.9.refs_2_ = bf16[1280,512]{1,0:T(8,128)(2,1)S(1)} collective-permute-done((bf16[1280,512]{1,0:T(8,128)(2,1)S(1)}, bf16[1280,512]{1,0:T(8,128)(2,1)S(1)}, u32[]{:S(2)}, u32[]{:S(2)}) %collective-permute-start.9) | collective-permute-done | bytes 1310752 | tf_op jit(solution)/shard_map/ppermute | solution.py:69
  80.5 16.7 %shard_map.275 = (bf16[8,176,256]{2,1,0:T(8,128)(2,1)}, bf16[8,176,256]{2,1,0:T(8,128)(2,1)}, bf16[8,176,256]{2,1,0:T(8,128)(2,1)}, bf16[8,176,256]{2,1,0:T(8,12...) custom-call(s32[5]{0:T(128)S(1)} %stack.20.refs_0_, ...), custom_call_target="tpu_custom_call" | custom-call | flops 19549999104 | tf_op jit(solution)/shard_map/pallas_call | solution.py:52
  102.2 6.5 %shard_map.276 = (bf16[1280,256]{1,0:T(8,128)(2,1)S(1)}, bf16[1280,256]{1,0:T(8,128)(2,1)S(1)}, bf16[1280,256]{1,0:T(8,128)(2,1)S(1)}, bf16[1280,256]{1,0:T(8,128)(2,1)}) custom-call(s32[5]{0:T(128)S(1)} %stack.20.refs_0_, bf16[1280,1024]{1,0:T(8,128)(2,1)} %get-tuple-element.90.refs_1_.refs_0_, f32[1280,1]{1,0:T(8,128)} %copy-done.18, ...), custom_call_target="tpu_custom_call" | custom-call | flops 7474999808 | tf_op jit(solution)/shard_map/pallas_call | solution.py:52
  110.1 9.4 %collective-permute-done.14 = bf16[8,176,256]{2,1,0:T(8,128)(2,1)S(1)} collective-permute-done((bf16[8,176,256]{2,1,0:T(8,128)(2,1)S(1)}, bf16[8,176,256]{2,1,0:T(8,128)(2,1)S(1)}, u32[]{:S(2)}, u32[]{:S(2)}) %collective-permute-start.14) | collective-permute-done | bytes 720928 | tf_op jit(solution)/shard_map/ppermute | solution.py:69
  120.5 3.6 %all-to-all-start.3 = ((bf16[8,176,256]{2,1,0:T(8,128)(2,1)}), bf16[8,176,256]{2,1,0:T(8,128)(2,1)S(1)}, u32[]{:S(2)}, u32[]{:S(2)}) async-start(bf16[8,176,256]{2,1,0:T(8,128)(2,1)} %add_convert_fusion.refs_4_), calls=%async_computation.3 | async-start | bytes 1441792 | tf_op jit(solution)/shard_map/all_to_all | solution.py:799
  126.1 2.6 %shard_map.277 = (bf16[1280,256]{1,0:T(8,128)(2,1)S(1)}, bf16[1280,256]{1,0:T(8,128)(2,1)S(1)}) custom-call(bf16[1280,256]{1,0:T(8,128)(2,1)S(1)} %copy-done.15, bf16[1280,256]{1,0:T(8,128)(2,1)} %copy-done.16, bf16[1280,256]{1,0:T(8,128)(2,1)} %copy-done.32, bf16[1280,256]{1,0:T(8,128)(2,1)} %collective-permute-done.13.refs_3_, ...), custom_call_target="tpu_custom_call" | custom-call | flops 2300000000 | tf_op jit(solution)/shard_map/pallas_call | solution.py:52
  129.7 7.1 %shard_map.280 = f32[1024,1024]{1,0:T(8,128)} custom-call(bf16[1280,1024]{1,0:T(8,128)(2,1)} %get-tuple-element.90.refs_1_.refs_0_, bf16[1280,1024]{1,0:T(8,128)(2,1)} %get-tuple-element.104.refs_1_, bf16[1280,256]{1,0:T(8,128)(2,1)S(1)} %get-tuple-element.98.refs_2_.refs_4_, bf16[1280,256]{1,0:T(8,128)(2,1)S(1)} %get-tuple-element.99.refs_3_.refs_5_), custom_call_target="tpu_custom_call" | custom-call | flops 8049999872 | tf_op jit(solution)/shard_map/pallas_call | solution.py:52
  136.8 7.6 %shard_map.281 = f32[1024,1024]{1,0:T(8,128)} custom-call(s32[5]{0:T(128)S(1)} %stack.20.refs_0_, bf16[1280,512]{1,0:T(8,128)(2,1)} %bitcast.58, bf16[1280,512]{1,0:T(8,128)(2,1)} %copy-done.31, bf16[1280,1024]{1,0:T(8,128)(2,1)} %get-tuple-element.105.refs_3_, bf16[1280,256]{1,0:T(8,128)(2,1)S(1)} %get-tuple-element.98.refs_2_.refs_4_, ...), custom_call_target="tpu_custom_call" | custom-call | flops 8049999872 | tf_op jit(solution)/shard_map/pallas_call | solution.py:52
  149.5 6.0 %all-to-all-start.2 = ((bf16[8,160,256]{2,1,0:T(8,128)(2,1)}), bf16[8,160,256]{2,1,0:T(8,128)(2,1)S(1)}, u32[]{:S(2)}, u32[]{:S(2)}) async-start(bf16[8,160,256]{2,1,0:T(8,128)(2,1)} %bitcast.16), calls=%async_computation.2 | async-start | bytes 1310720 | tf_op jit(solution)/shard_map/all_to_all | solution.py:853
  158.1 6.1 %shard_map.283 = (f32[394,1024]{1,0:T(8,128)}, bf16[512,256]{1,0:T(8,128)(2,1)S(1)}, bf16[512,256]{1,0:T(8,128)(2,1)}, bf16[394,256]{1,0:T(8,128)(2,1)S(1)}, f32[11,1024]{1,0:T(8,128)S(1)}) custom-call(s32[5]{0:T(128)S(1)} %stack.20.refs_0_, bf16[394,256]{1,0:T(8,128)(2,1)S(1)} %shard_map.282.refs_1_, bf16[394,256]{1,0:T(8,128)(2,1)S(1)} %collective-permute-done.19.refs_2_, ...), custom_call_target="tpu_custom_call" | custom-call | flops 6899999744 | tf_op jit(solution)/shard_map/pallas_call | solution.py:52
  164.2 8.2 %shard_map.284 = (bf16[768,256]{1,0:T(8,128)(2,1)S(1)}, bf16[768,256]{1,0:T(8,128)(2,1)}, bf16[768,256]{1,0:T(8,128)(2,1)}, bf16[768,256]{1,0:T(8,128)(2,1)}, f3...) custom-call(s32[5]{0:T(128)S(1)} %stack.20.refs_0_, ...), custom_call_target="tpu_custom_call" | custom-call | flops 9200000000 | tf_op jit(solution)/shard_map/pallas_call | solution.py:52
  179.3 4.4 %collective-permute-done.37.refs_1_ = bf16[512,256]{1,0:T(8,128)(2,1)S(1)} collective-permute-done((bf16[512,256]{1,0:T(8,128)(2,1)S(1)}, bf16[512,256]{1,0:T(8,128)(2,1)S(1)}, u32[]{:S(2)}, u32[]{:S(2)}) %collective-permute-start.37) | collective-permute-done | bytes 262176 | tf_op jit(solution)/shard_map/ppermute | solution.py:69
  188.0 4.1 %collective-permute-done.25.refs_1_ = bf16[768,256]{1,0:T(8,128)(2,1)S(1)} collective-permute-done((bf16[768,256]{1,0:T(8,128)(2,1)S(1)}, bf16[768,256]{1,0:T(8,128)(2,1)S(1)}, u32[]{:S(2)}, u32[]{:S(2)}) %collective-permute-start.25) | collective-permute-done | bytes 393248 | tf_op jit(solution)/shard_map/ppermute | solution.py:69
  193.4 2.9 %collective-permute-start.39 = (bf16[128,256]{1,0:T(8,128)(2,1)S(1)}, bf16[128,256]{1,0:T(8,128)(2,1)S(1)}, u32[]{:S(2)}, u32[]{:S(2)}) collective-permute-start(bf16[128,256]{1,0:T(8,128)(2,1)S(1)} %constant_dynamic-slice_fusion), channel_id=1, source_target_pairs={{0,16},{4,20},{8,24},{12,28},{16,0},{20,4},{24,8},{28,12},{1,17},{... | collective-permute-start | bytes 196616 | tf_op jit(solution)/shard_map/ppermute | solution.py:69
  196.2 2.5 %shard_map.279 = bf16[394,1024]{1,0:T(8,128)(2,1)} custom-call(s32[5]{0:T(128)S(1)} %stack.20.refs_0_, f32[394,1024]{1,0:T(8,128)} %get-tuple-element.73.refs_1_.refs_10_, bf16[394,256]{1,0:T(8,128)(2,1)S(1)} %shard_map.278.refs_2_, bf16[394,256]{1,0:T(8,128)(2,1)S(1)} %collective-permute-done.16.refs_3_, ...), custom_call_target="tpu_custom_call" | custom-call | flops 2990000128 | tf_op jit(solution)/shard_map/pallas_call | solution.py:52
  199.4 2.2 collective-permute-start.40
  205.0 8.0 %collective-permute-done.33 = bf16[192,256]{1,0:T(8,128)(2,1)S(1)} collective-permute-done((bf16[192,256]{1,0:T(8,128)(2,1)S(1)}, bf16[192,256]{1,0:T(8,128)(2,1)S(1)}, u32[]{:S(2)}, u32[]{:S(2)}) %collective-permute-start.33) | collective-permute-done | bytes 98336 | tf_op jit(solution)/shard_map/ppermute | solution.py:69
  217.9 3.9 %collective-permute-done.34 = bf16[192,256]{1,0:T(8,128)(2,1)S(1)} collective-permute-done((bf16[192,256]{1,0:T(8,128)(2,1)S(1)}, bf16[192,256]{1,0:T(8,128)(2,1)S(1)}, u32[]{:S(2)}, u32[]{:S(2)}) %collective-permute-start.34) | collective-permute-done | bytes 98336 | tf_op jit(solution)/shard_map/ppermute | solution.py:69
  224.3 4.1 %collective-permute-start.42 = (bf16[512,256]{1,0:T(8,128)(2,1)S(1)}, bf16[512,256]{1,0:T(8,128)(2,1)S(1)}, u32[]{:S(2)}, u32[]{:S(2)}) collective-permute-start(bf16[512,256]{1,0:T(8,128)(2,1)S(1)} %maximum_select_fusion.2.refs_1_), channel_id=1, source_target_pairs={{0,4},{4,0},{8,12},{12,8},{16,20},{20,16},{24,28},{28,24},{1,5},{5... | collective-permute-start | bytes 786440 | tf_op jit(solution)/shard_map/ppermute | solution.py:69
  233.3 2.3 collective-permute-done.42.refs_2_
  237.2 3.9 %shard_map.285.refs_5_ = f32[394,1024]{1,0:T(8,128)} custom-call(s32[5]{0:T(128)S(1)} %stack.20.refs_0_, bf16[394,1024]{1,0:T(8,128)(2,1)S(1)} %copy-done.3, f32[1,1024]{1,0:T(1,128)S(1)} %bitcast.51, bf16[400,512]{1,0:T(8,128)(2,1)S(1)} %add_convert_fusion.4.refs_3_, bf16[400,512]{1,0:T(8,128)(2,1)S(1)} %collective-permute-done.24.refs_4_, ...), custom_call_target="tpu_custom_call" | custom-call | flops 4485000192 | tf_op jit(solution)/shard_map/pallas_call | solution.py:52
  242.9 2.5 %shard_map.288 = f32[3,1024,256]{2,1,0:T(8,128)} custom-call(s32[5]{0:T(128)S(1)} %stack.20.refs_0_, bf16[768,256]{1,0:T(8,128)(2,1)S(1)} %maximum_select_fusion.refs_1_, bf16[768,256]{1,0:T(8,128)(2,1)S(1)} %slice.89.refs_2_, bf16[768,256]{1,0:T(8,128)(2,1)S(1)} %maximum_select_fusion.1.refs_3_, bf16[768,256]{1,0:T(8,128)(2,1)S(1)} %collective-permute-done.36.refs_4_, ...), custom_call_target="tpu_custom_call" | custom-call | flops 2300000000 | tf_op jit(solution)/shard_map/pallas_call | solution.py:52
  (208 shorter events, 63.7 us)
Async XLA Ops:
  0.6 16.2 %collective-permute-start.4 = (bf16[256,1024]{1,0:T(8,128)(2,1)}, bf16[256,1024]{1,0:T(8,128)(2,1)S(1)}, u32[]{:S(2)}, u32[]{:S(2)}) collective-permute-start(bf16[256,1024]{1,0:T(8,128)(2,1)} %refs_13_.2), channel_id=1, source_target_pairs={{0,3},{1,2},{2,1},{3,0},{4,7},{5,6},{6,5},{7,4},{8,11},{9,10},{10,... | collective-permute-start | bytes 1572872 | tf_op jit(solution)/shard_map/ppermute | solution.py:69
  3.1 29.2 %collective-permute-start.3 = (bf16[256,1024]{1,0:T(8,128)(2,1)}, bf16[256,1024]{1,0:T(8,128)(2,1)}, u32[]{:S(2)}, u32[]{:S(2)}) collective-permute-start(bf16[256,1024]{1,0:T(8,128)(2,1)} %refs_13_.2), channel_id=1, source_target_pairs={{0,1},{1,0},{2,3},{3,2},{4,5},{5,4},{6,7},{7,6},{8,9},{9,8},{10,11... | collective-permute-start | bytes 1572872 | tf_op jit(solution)/shard_map/ppermute | solution.py:69
  11.0 27.6 %all-to-all-start.1 = ((bf16[8,160,256]{2,1,0:T(8,128)(2,1)}), bf16[8,160,256]{2,1,0:T(8,128)(2,1)S(1)}, u32[]{:S(2)}, u32[]{:S(2)}) async-start(bf16[8,160,256]{2,1,0:T(8,128)(2,1)} %bitcast.12), calls=%async_computation.1 | async-start | bytes 1310720 | tf_op jit(solution)/shard_map/all_to_all | solution.py:683
  16.9 15.5 %collective-permute-start.5 = (bf16[256,1024]{1,0:T(8,128)(2,1)S(1)}, bf16[256,1024]{1,0:T(8,128)(2,1)}, u32[]{:S(2)}, u32[]{:S(2)}) collective-permute-start(bf16[256,1024]{1,0:T(8,128)(2,1)S(1)} %collective-permute-done.4.refs_8_), channel_id=1, source_target_pairs={{0,1},{1,0},{2,3},{3,2},{4,5},{5,4},{6,7},{7,6},{8,9},{9,8},{10,11... | collective-permute-start | bytes 1572872 | tf_op jit(solution)/shard_map/ppermute | solution.py:69
  38.6 37.8 %all-to-all-start = ((bf16[8,160,512]{2,1,0:T(8,128)(2,1)}), bf16[8,160,512]{2,1,0:T(8,128)(2,1)S(1)}, u32[]{:S(2)}, u32[]{:S(2)}) async-start(bf16[8,160,512]{2,1,0:T(8,128)(2,1)} %bitcast.59), calls=%async_computation | async-start | bytes 2621440 | tf_op jit(solution)/shard_map/all_to_all | solution.py:718
  44.7 17.0 %collective-permute-start.7 = (bf16[1280,256]{1,0:T(8,128)(2,1)S(1)}, bf16[1280,256]{1,0:T(8,128)(2,1)S(1)}, u32[]{:S(2)}, u32[]{:S(2)}) collective-permute-start(bf16[1280,256]{1,0:T(8,128)(2,1)S(1)} %bitcast.40), channel_id=1, source_target_pairs={{0,3},{1,2},{2,1},{3,0},{4,7},{5,6},{6,5},{7,4},{8,11},{9,10},{10,... | collective-permute-start | bytes 1966088 | tf_op jit(solution)/shard_map/ppermute | solution.py:69
  45.2 16.7 %collective-permute-start.6 = (bf16[1280,256]{1,0:T(8,128)(2,1)S(1)}, bf16[1280,256]{1,0:T(8,128)(2,1)S(1)}, u32[]{:S(2)}, u32[]{:S(2)}) collective-permute-start(bf16[1280,256]{1,0:T(8,128)(2,1)S(1)} %bitcast.41), channel_id=1, source_target_pairs={{0,1},{1,0},{2,3},{3,2},{4,5},{5,4},{6,7},{7,6},{8,9},{9,8},{10,11... | collective-permute-start | bytes 1966088 | tf_op jit(solution)/shard_map/ppermute | solution.py:69
  101.2 18.2 %collective-permute-start.14 = (bf16[8,176,256]{2,1,0:T(8,128)(2,1)S(1)}, bf16[8,176,256]{2,1,0:T(8,128)(2,1)S(1)}, u32[]{:S(2)}, u32[]{:S(2)}) collective-permute-start(bf16[8,176,256]{2,1,0:T(8,128)(2,1)S(1)} %add_convert_fusion.1), channel_id=1, source_target_pairs={{0,2},{1,3},{2,0},{3,1},{4,6},{5,7},{6,4},{7,5},{8,10},{9,11},{10,... | collective-permute-start | bytes 2162696 | tf_op jit(solution)/shard_map/ppermute | solution.py:69
  109.6 14.6 %collective-permute-start.12 = (bf16[1280,256]{1,0:T(8,128)(2,1)S(1)}, bf16[1280,256]{1,0:T(8,128)(2,1)S(1)}, u32[]{:S(2)}, u32[]{:S(2)}) collective-permute-start(bf16[1280,256]{1,0:T(8,128)(2,1)S(1)} %get-tuple-element.94), channel_id=1, source_target_pairs={{0,1},{1,0},{2,3},{3,2},{4,5},{5,4},{6,7},{7,6},{8,9},{9,8},{10,11... | collective-permute-start | bytes 1966088 | tf_op jit(solution)/shard_map/ppermute | solution.py:69
  109.6 14.6 %collective-permute-start.13 = (bf16[1280,256]{1,0:T(8,128)(2,1)}, bf16[1280,256]{1,0:T(8,128)(2,1)}, u32[]{:S(2)}, u32[]{:S(2)}) collective-permute-start(bf16[1280,256]{1,0:T(8,128)(2,1)} %get-tuple-element.95), channel_id=1, source_target_pairs={{0,1},{1,0},{2,3},{3,2},{4,5},{5,4},{6,7},{7,6},{8,9},{9,8},{10,11... | collective-permute-start | bytes 1966088 | tf_op jit(solution)/shard_map/ppermute | solution.py:69
  120.5 23.9 %all-to-all-start.3 = ((bf16[8,176,256]{2,1,0:T(8,128)(2,1)}), bf16[8,176,256]{2,1,0:T(8,128)(2,1)S(1)}, u32[]{:S(2)}, u32[]{:S(2)}) async-start(bf16[8,176,256]{2,1,0:T(8,128)(2,1)} %add_convert_fusion.refs_4_), calls=%async_computation.3 | async-start | bytes 1441792 | tf_op jit(solution)/shard_map/all_to_all | solution.py:799
  128.7 18.6 %collective-permute-start.15 = (bf16[1280,256]{1,0:T(8,128)(2,1)S(1)}, bf16[1280,256]{1,0:T(8,128)(2,1)}, u32[]{:S(2)}, u32[]{:S(2)}) collective-permute-start(bf16[1280,256]{1,0:T(8,128)(2,1)S(1)} %get-tuple-element.99.refs_3_.refs_5_), channel_id=1, source_target_pairs={{0,2},{1,3},{2,0},{3,1},{4,6},{5,7},{6,4},{7,5},{8,10},{9,11},{10,... | collective-permute-start | bytes 1966088 | tf_op jit(solution)/shard_map/ppermute | solution.py:69
  146.2 9.3 %collective-permute-start.20 = (bf16[394,256]{1,0:T(8,128)(2,1)S(1)}, bf16[394,256]{1,0:T(8,128)(2,1)S(1)}, u32[]{:S(2)}, u32[]{:S(2)}) collective-permute-start(bf16[394,256]{1,0:T(8,128)(2,1)S(1)} %shard_map.282.refs_1_), channel_id=1, source_target_pairs={{0,2},{1,3},{2,0},{3,1},{4,6},{5,7},{6,4},{7,5},{8,10},{9,11},{10,... | collective-permute-start | bytes 605192 | tf_op jit(solution)/shard_map/ppermute | solution.py:69
  149.5 26.5 %all-to-all-start.2 = ((bf16[8,160,256]{2,1,0:T(8,128)(2,1)}), bf16[8,160,256]{2,1,0:T(8,128)(2,1)S(1)}, u32[]{:S(2)}, u32[]{:S(2)}) async-start(bf16[8,160,256]{2,1,0:T(8,128)(2,1)} %bitcast.16), calls=%async_computation.2 | async-start | bytes 1310720 | tf_op jit(solution)/shard_map/all_to_all | solution.py:853
  172.4 12.0 %collective-permute-start.31 = (bf16[768,256]{1,0:T(8,128)(2,1)}, bf16[768,256]{1,0:T(8,128)(2,1)S(1)}, u32[]{:S(2)}, u32[]{:S(2)}) collective-permute-start(bf16[768,256]{1,0:T(8,128)(2,1)} %get-tuple-element.118), channel_id=1, source_target_pairs={{0,8},{4,12},{8,0},{12,4},{16,24},{20,28},{24,16},{28,20},{1,9},{5... | collective-permute-start | bytes 1179656 | tf_op jit(solution)/shard_map/ppermute | solution.py:69
  174.5 9.2 %collective-permute-start.37 = (bf16[512,256]{1,0:T(8,128)(2,1)S(1)}, bf16[512,256]{1,0:T(8,128)(2,1)S(1)}, u32[]{:S(2)}, u32[]{:S(2)}) collective-permute-start(bf16[512,256]{1,0:T(8,128)(2,1)S(1)} %copy-done.38), channel_id=1, source_target_pairs={{0,4},{4,0},{8,12},{12,8},{16,20},{20,16},{24,28},{28,24},{1,5},{5... | collective-permute-start | bytes 786440 | tf_op jit(solution)/shard_map/ppermute | solution.py:69
  178.6 13.4 %collective-permute-start.25 = (bf16[768,256]{1,0:T(8,128)(2,1)S(1)}, bf16[768,256]{1,0:T(8,128)(2,1)S(1)}, u32[]{:S(2)}, u32[]{:S(2)}) collective-permute-start(bf16[768,256]{1,0:T(8,128)(2,1)S(1)} %copy-done.37), channel_id=1, source_target_pairs={{0,4},{4,0},{8,12},{12,8},{16,20},{20,16},{24,28},{28,24},{1,5},{5... | collective-permute-start | bytes 1179656 | tf_op jit(solution)/shard_map/ppermute | solution.py:69
  183.6 9.7 %collective-permute-start.16 = (bf16[394,256]{1,0:T(8,128)(2,1)S(1)}, bf16[394,256]{1,0:T(8,128)(2,1)S(1)}, u32[]{:S(2)}, u32[]{:S(2)}) collective-permute-start(bf16[394,256]{1,0:T(8,128)(2,1)S(1)} %shard_map.278.refs_2_), channel_id=1, source_target_pairs={{0,1},{1,0},{2,3},{3,2},{4,5},{5,4},{6,7},{7,6},{8,9},{9,8},{10,11... | collective-permute-start | bytes 605192 | tf_op jit(solution)/shard_map/ppermute | solution.py:69
  184.4 11.8 %collective-permute-start.18 = (bf16[394,256]{1,0:T(8,128)(2,1)S(1)}, bf16[394,256]{1,0:T(8,128)(2,1)S(1)}, u32[]{:S(2)}, u32[]{:S(2)}) collective-permute-start(bf16[394,256]{1,0:T(8,128)(2,1)S(1)} %collective-permute-done.17.refs_4_), channel_id=1, source_target_pairs={{0,1},{1,0},{2,3},{3,2},{4,5},{5,4},{6,7},{7,6},{8,9},{9,8},{10,11... | collective-permute-start | bytes 605192 | tf_op jit(solution)/shard_map/ppermute | solution.py:69
  184.5 8.5 %collective-permute-start.38 = (bf16[256,256]{1,0:T(8,128)(2,1)S(1)}, bf16[256,256]{1,0:T(8,128)(2,1)S(1)}, u32[]{:S(2)}, u32[]{:S(2)}) collective-permute-start(bf16[256,256]{1,0:T(8,128)(2,1)S(1)} %constant_dynamic-slice_fusion.1), channel_id=1, source_target_pairs={{0,8},{4,12},{8,0},{12,4},{16,24},{20,28},{24,16},{28,20},{1,9},{5... | collective-permute-start | bytes 393224 | tf_op jit(solution)/shard_map/ppermute | solution.py:69
  186.4 15.2 %collective-permute-start.32 = (bf16[384,256]{1,0:T(8,128)(2,1)S(1)}, bf16[384,256]{1,0:T(8,128)(2,1)S(1)}, u32[]{:S(2)}, u32[]{:S(2)}) collective-permute-start(bf16[384,256]{1,0:T(8,128)(2,1)S(1)} %constant_dynamic-slice_fusion.3), channel_id=1, source_target_pairs={{0,4},{4,0},{8,12},{12,8},{16,20},{20,16},{24,28},{28,24},{1,5},{5... | collective-permute-start | bytes 589832 | tf_op jit(solution)/shard_map/ppermute | solution.py:69
  192.1 12.7 %collective-permute-start.23 = (bf16[400,512]{1,0:T(8,128)(2,1)S(1)}, bf16[400,512]{1,0:T(8,128)(2,1)S(1)}, u32[]{:S(2)}, u32[]{:S(2)}) collective-permute-start(bf16[400,512]{1,0:T(8,128)(2,1)S(1)} %add_convert_fusion.5.refs_2_), channel_id=1, source_target_pairs={{0,2},{1,3},{2,0},{3,1},{4,6},{5,7},{6,4},{7,5},{8,10},{9,11},{10,... | collective-permute-start | bytes 1228808 | tf_op jit(solution)/shard_map/ppermute | solution.py:69
  193.1 9.4 %collective-permute-start.26 = (bf16[384,256]{1,0:T(8,128)(2,1)S(1)}, bf16[384,256]{1,0:T(8,128)(2,1)S(1)}, u32[]{:S(2)}, u32[]{:S(2)}) collective-permute-start(bf16[384,256]{1,0:T(8,128)(2,1)S(1)} %constant_dynamic-slice_fusion.5), channel_id=1, source_target_pairs={{0,8},{4,12},{8,0},{12,4},{16,24},{20,28},{24,16},{28,20},{1,9},{5... | collective-permute-start | bytes 589832 | tf_op jit(solution)/shard_map/ppermute | solution.py:69
  199.4 17.3 %collective-permute-start.40 = (bf16[128,256]{1,0:T(8,128)(2,1)S(1)}, bf16[128,256]{1,0:T(8,128)(2,1)S(1)}, u32[]{:S(2)}, u32[]{:S(2)}) collective-permute-start(bf16[128,256]{1,0:T(8,128)(2,1)S(1)} %add_convert_fusion.12), channel_id=1, source_target_pairs={{0,16},{4,20},{8,24},{12,28},{16,0},{20,4},{24,8},{28,12},{1,17},{... | collective-permute-start | bytes 196616 | tf_op jit(solution)/shard_map/ppermute | solution.py:69
  201.7 11.3 %collective-permute-start.33 = (bf16[192,256]{1,0:T(8,128)(2,1)S(1)}, bf16[192,256]{1,0:T(8,128)(2,1)S(1)}, u32[]{:S(2)}, u32[]{:S(2)}) collective-permute-start(bf16[192,256]{1,0:T(8,128)(2,1)S(1)} %constant_dynamic-slice_fusion.2), channel_id=1, source_target_pairs={{0,16},{4,20},{8,24},{12,28},{16,0},{20,4},{24,8},{28,12},{1,17},{... | collective-permute-start | bytes 294920 | tf_op jit(solution)/shard_map/ppermute | solution.py:69
  202.6 12.0 %collective-permute-start.27 = (bf16[192,256]{1,0:T(8,128)(2,1)S(1)}, bf16[192,256]{1,0:T(8,128)(2,1)S(1)}, u32[]{:S(2)}, u32[]{:S(2)}) collective-permute-start(bf16[192,256]{1,0:T(8,128)(2,1)S(1)} %constant_dynamic-slice_fusion.4), channel_id=1, source_target_pairs={{0,16},{4,20},{8,24},{12,28},{16,0},{20,4},{24,8},{28,12},{1,17},{... | collective-permute-start | bytes 294920 | tf_op jit(solution)/shard_map/ppermute | solution.py:69
  204.9 9.8 %collective-permute-start.24 = (bf16[400,512]{1,0:T(8,128)(2,1)S(1)}, bf16[400,512]{1,0:T(8,128)(2,1)S(1)}, u32[]{:S(2)}, u32[]{:S(2)}) collective-permute-start(bf16[400,512]{1,0:T(8,128)(2,1)S(1)} %add_convert_fusion.4.refs_3_), channel_id=1, source_target_pairs={{0,1},{1,0},{2,3},{3,2},{4,5},{5,4},{6,7},{7,6},{8,9},{9,8},{10,11... | collective-permute-start | bytes 1228808 | tf_op jit(solution)/shard_map/ppermute | solution.py:69
  213.0 8.8 %collective-permute-start.34 = (bf16[192,256]{1,0:T(8,128)(2,1)S(1)}, bf16[192,256]{1,0:T(8,128)(2,1)S(1)}, u32[]{:S(2)}, u32[]{:S(2)}) collective-permute-start(bf16[192,256]{1,0:T(8,128)(2,1)S(1)} %add_convert_fusion.10), channel_id=1, source_target_pairs={{0,16},{4,20},{8,24},{12,28},{16,0},{20,4},{24,8},{28,12},{1,17},{... | collective-permute-start | bytes 294920 | tf_op jit(solution)/shard_map/ppermute | solution.py:69
  215.3 8.6 %collective-permute-start.28 = (bf16[256,256]{1,0:T(8,128)(2,1)S(1)}, bf16[256,256]{1,0:T(8,128)(2,1)S(1)}, u32[]{:S(2)}, u32[]{:S(2)}) collective-permute-start(bf16[256,256]{1,0:T(8,128)(2,1)S(1)} %pad_maximum_fusion.2), channel_id=1, source_target_pairs={{0,16},{4,20},{8,24},{12,28},{16,0},{20,4},{24,8},{28,12},{1,17},{... | collective-permute-start | bytes 393224 | tf_op jit(solution)/shard_map/ppermute | solution.py:69
  224.1 8.5 %collective-permute-start.29 = (bf16[448,256]{1,0:T(8,128)(2,1)S(1)}, bf16[448,256]{1,0:T(8,128)(2,1)S(1)}, u32[]{:S(2)}, u32[]{:S(2)}) collective-permute-start(bf16[448,256]{1,0:T(8,128)(2,1)S(1)} %pad_maximum_fusion.1), channel_id=1, source_target_pairs={{0,8},{4,12},{8,0},{12,4},{16,24},{20,28},{24,16},{28,20},{1,9},{5... | collective-permute-start | bytes 688136 | tf_op jit(solution)/shard_map/ppermute | solution.py:69
  224.3 11.3 %collective-permute-start.42 = (bf16[512,256]{1,0:T(8,128)(2,1)S(1)}, bf16[512,256]{1,0:T(8,128)(2,1)S(1)}, u32[]{:S(2)}, u32[]{:S(2)}) collective-permute-start(bf16[512,256]{1,0:T(8,128)(2,1)S(1)} %maximum_select_fusion.2.refs_1_), channel_id=1, source_target_pairs={{0,4},{4,0},{8,12},{12,8},{16,20},{20,16},{24,28},{28,24},{1,5},{5... | collective-permute-start | bytes 786440 | tf_op jit(solution)/shard_map/ppermute | solution.py:69
  228.5 14.4 %collective-permute-start.36 = (bf16[768,256]{1,0:T(8,128)(2,1)S(1)}, bf16[768,256]{1,0:T(8,128)(2,1)S(1)}, u32[]{:S(2)}, u32[]{:S(2)}) collective-permute-start(bf16[768,256]{1,0:T(8,128)(2,1)S(1)} %maximum_select_fusion.1.refs_3_), channel_id=1, source_target_pairs={{0,8},{4,12},{8,0},{12,4},{16,24},{20,28},{24,16},{28,20},{1,9},{5... | collective-permute-start | bytes 1179656 | tf_op jit(solution)/shard_map/ppermute | solution.py:69
  (54 other events, 368.2 us)
